TPU v7x, 32 devices: a whole 2x2x4 slice. The times are simulated.
32 devices in a mesh: blk: 16 (over z, y, x), rep: 2 (over core).
Axes of the slice: x: 2, y: 2, z: 4, core: 2. Of those that a mesh axis runs over, the one named last changes fastest.
Arguments:
- entity: bfloat16 [8192, 512], P('blk'), may hold values from -1.1953125 to 1.1953125
- relation: bfloat16 [8, 512, 512], P('rep'), may hold values from -0.25 to 0.25
- head_owner: int32 [8192, 1], P(('blk', 'rep')), may hold values from 0 to 15; in each aligned block of 256 rows (0 to 255, 256 to 511, ...) at most 32 rows name the same one
- head_row: int32 [8192], P(('blk', 'rep')), may hold values from 0 to 511
- query_rel: int32 [8192, 4], P(('blk', 'rep')), may hold values from 0 to 3
- tail_row: int32 [8192, 4], P(('blk', 'rep')), may hold values from 0 to 511
- neg_row: int32 [16, 512], P('blk', 'rep'), may hold values from 0 to 511
Outputs:
- grad_entity: float32 [8192, 512], P('blk', 'rep')
- grad_rel: float32 [8, 512, 512], P('rep', 'blk')
Inputs may be any that keep to these rules, and one draw needn't show every extreme that they name: `head_owner`: in each aligned block of 256 rows (the heads of one group) no shard number appears more than 32 times.
All inputs are finite; a program needn't handle non-finite values.
Results may differ from a plain program's by a relative error of at most 0.0035.
Values may be sent and summed in bfloat16 or wider, within the bound.
No kernel may reach another device: no remote copies, remote signals or barrier semaphores. Data moves between devices by JAX's collectives and lax.ppermute only.
A program may use at most 64 MiB of HBM per device.

v0:
```python
import jax
import jax.numpy as jnp
from jax import lax
from jax.sharding import PartitionSpec as P

D = 512
STOPS = 6


def shifted(block, axis, distance):
    devices = range(lax.axis_size(axis))
    route = [((i - distance) % len(devices), i) for i in devices]
    return lax.ppermute(block, axis, route)


def visit(queries, neg_block, grad_query):
    scores = jnp.dot(queries, neg_block.T, preferred_element_type=jnp.float32)
    weights = (jax.nn.sigmoid(scores) / STOPS).astype(jnp.bfloat16)
    grad_query = grad_query + jnp.dot(weights, neg_block, preferred_element_type=jnp.float32)
    block_term = jnp.einsum("qn,qd->nd", weights, queries, preferred_element_type=jnp.float32)
    return (grad_query, block_term)


def per_device(entity, relation, head_owner, head_row, query_rel, tail_row, neg_row):
    shard_count = lax.axis_size("blk")
    head_count = head_row.shape[0]
    capacity = max(2, 2 * head_count // shard_count)
    head_shard = head_owner[:, 0]
    one_hot = (head_shard[:, None] == jnp.arange(shard_count, dtype=jnp.int32)[None, :]).astype(
        jnp.int32
    )
    head_slot = jnp.sum((jnp.cumsum(one_hot, axis=0) - one_hot) * one_hot, axis=1)
    asked = jnp.full((shard_count, capacity), -1, jnp.int32).at[head_shard, head_slot].set(head_row)
    wanted = lax.all_to_all(asked, "blk", split_axis=0, concat_axis=0, tiled=True)
    served = jnp.take(entity, jnp.maximum(wanted, 0), axis=0)
    fetched, wanted = (
        lax.all_to_all(served, "blk", split_axis=0, concat_axis=0, tiled=True),
        wanted,
    )
    head_vec = fetched[head_shard, head_slot]
    products = jnp.einsum("hd,kde->khe", head_vec, relation, preferred_element_type=jnp.float32)
    rel_count = relation.shape[0]
    queries = jnp.zeros(query_rel.shape + (D,), jnp.float32)
    for rel_index in range(rel_count):
        queries = queries + jnp.where(
            (query_rel == rel_index)[:, :, None], products[rel_index][:, None, :], 0.0
        )
    queries = queries.astype(jnp.bfloat16).reshape(-1, D)
    tail_vec = jnp.take(entity, tail_row.reshape(-1), axis=0)
    pos_score = jnp.sum(queries.astype(jnp.float32) * tail_vec.astype(jnp.float32), axis=1)
    pos_weight = jax.nn.sigmoid(pos_score) - 1.0
    grad_query = pos_weight[:, None] * tail_vec.astype(jnp.float32)
    own_block = jnp.take(entity, neg_row[0], axis=0)
    fore_reach = STOPS // 2
    back_reach = STOPS - 1 - fore_reach
    grad_query, fore_total = visit(queries, own_block, grad_query)
    fore_part = own_block
    for visit_index in range(fore_reach):
        fore_part = shifted(fore_part, "blk", 1)
        grad_query, block_term = visit(queries, fore_part, grad_query)
        fore_total = shifted(fore_total, "blk", 1) + block_term
    back_part = own_block
    back_total = jnp.zeros(own_block.shape, jnp.float32)
    for visit_index in range(back_reach):
        back_part = shifted(back_part, "blk", -1)
        grad_query, block_term = visit(queries, back_part, grad_query)
        if visit_index == 0:
            back_total = block_term
        else:
            back_total = shifted(back_total, "blk", -1) + block_term
    own_grad = shifted(fore_total, "blk", -fore_reach) + shifted(back_total, "blk", back_reach)
    grad_query = grad_query.reshape(query_rel.shape + (D,))
    pair_list = []
    for rel_index in range(rel_count):
        pair_list.append(
            jnp.sum(
                jnp.where((query_rel == rel_index)[:, :, None], grad_query, 0.0), axis=1
            ).astype(jnp.bfloat16)
        )
    grad_pair = jnp.stack(pair_list)
    grad_head = jnp.einsum("khe,kde->hd", grad_pair, relation, preferred_element_type=jnp.float32)
    rel_terms = jnp.einsum("hd,khe->kde", head_vec, grad_pair, preferred_element_type=jnp.float32)
    grad_rel = lax.psum_scatter(rel_terms, "blk", scatter_dimension=1, tiled=True)
    buckets = (
        jnp.zeros((shard_count, capacity, D), jnp.float32).at[head_shard, head_slot].set(grad_head)
    )
    returned = lax.all_to_all(buckets, "blk", split_axis=0, concat_axis=0, tiled=True)
    local_grad = jnp.zeros(entity.shape, jnp.float32)
    local_grad = local_grad.at[jnp.maximum(wanted, 0).reshape(-1)].add(returned.reshape(-1, D))
    local_grad = local_grad.at[tail_row.reshape(-1)].add(
        pos_weight[:, None] * queries.astype(jnp.float32)
    )
    local_grad = local_grad.at[neg_row[0]].add(own_grad)
    grad_entity = lax.psum_scatter(local_grad, "rep", scatter_dimension=1, tiled=True)
    return (grad_entity, grad_rel)


def solution(mesh):
    placed = (
        P("blk", None),
        P("rep", None, None),
        P(("blk", "rep"), None),
        P(("blk", "rep")),
        P(("blk", "rep"), None),
        P(("blk", "rep"), None),
        P("blk", "rep"),
    )
    return jax.shard_map(
        per_device,
        mesh=mesh,
        in_specs=placed,
        out_specs=(P("blk", "rep"), P("rep", "blk", None)),
        check_vma=False,
    )
```

profile of v0, /device:TPU:0, one launch (start us, length us, event | category | flops | bytes accessed | tf_op | source)
XLA Modules:
  0.0 393.5 jit_solution(3145565825554497488)
XLA Ops:
  8.0 0.8 fusion.42
  9.7 0.8 fusion.41
  11.7 35.8 %scatter_fusion = s32[16,32]{1,0:T(8,128)} fusion(s32[16,32]{1,0:T(8,128)} %broadcast_in_dim.171, s32[256]{0:T(256)S(1)} %bitcast.111, s32[256]{0:T(256)} %param.10), kind=kCustom, calls=%fused_computation.4 | custom fusion | bytes 5120 | tf_op jit(solution)/shard_map/scatter | solution.py:33
  47.6 8.3 %all-to-all-start = ((s32[16,1,32]{2,1,0:T(1,128)}), s32[16,1,32]{2,1,0:T(1,128)S(1)}, u32[]{:S(2)}, u32[]{:S(2)}) async-start(s32[16,1,32]{2,1,0:T(1,128)} %bitcast.6), calls=%async_computation | async-start | bytes 16384 | tf_op jit(solution)/shard_map/all_to_all | solution.py:34
  56.5 1.2 gather_fusion.3
  57.8 5.6 %collective-permute-start.3 = (bf16[256,512]{1,0:T(8,128)(2,1)S(1)}, bf16[256,512]{1,0:T(8,128)(2,1)}, u32[]{:S(2)}, u32[]{:S(2)}) collective-permute-start(bf16[256,512]{1,0:T(8,128)(2,1)S(1)} %broadcast_select_fusion.1), channel_id=1, source_target_pairs={{2,0},{4,2},{6,4},{8,6},{10,8},{12,10},{14,12},{16,14},{18,16},{20... | collective-permute-start | bytes 786440 | tf_op jit(solution)/shard_map/ppermute | solution.py:13
  63.5 2.0 gather_fusion
  65.5 0.9 broadcast_select_fusion
  66.4 7.0 %all-to-all-start.1 = ((bf16[16,32,512]{2,1,0:T(8,128)(2,1)}), bf16[16,32,512]{2,1,0:T(8,128)(2,1)S(1)}, u32[]{:S(2)}, u32[]{:S(2)}) async-start(bf16[16,32,512]{2,1,0:T(8,128)(2,1)} %broadcast_select_fusion), calls=%async_computation.1 | async-start | bytes 1048576 | tf_op jit(solution)/shard_map/all_to_all | solution.py:37
  74.4 2.0 collective-permute-start.1
  77.1 0.8 copy.48
  77.9 0.7 broadcast_in_dim.174
  78.6 0.8 copy.53
  79.4 0.7 broadcast_in_dim.197
  80.2 0.8 copy.50
  81.7 0.8 copy.52
  83.3 0.8 copy.51
  84.9 5.1 %gather_fusion.2 = bf16[1024,512]{1,0:T(8,128)(2,1)} fusion(bf16[512,512]{1,0:T(8,128)(2,1)S(1)} %copy-done.1, s32[1024]{0:T(1024)S(1)} %broadcast_clamp_fusion), kind=kCustom, calls=%fused_computation.2 | custom fusion | bytes 2101248 | tf_op jit(solution)/shard_map/jit(_take)/gather | solution.py:49
  90.0 4.2 %collective-permute-start.4 = (bf16[256,512]{1,0:T(8,128)(2,1)}, bf16[256,512]{1,0:T(8,128)(2,1)}, u32[]{:S(2)}, u32[]{:S(2)}) collective-permute-start(bf16[256,512]{1,0:T(8,128)(2,1)} %collective-permute-done.3), channel_id=1, source_target_pairs={{2,0},{4,2},{6,4},{8,6},{10,8},{12,10},{14,12},{16,14},{18,16},{20... | collective-permute-start | bytes 786440 | tf_op jit(solution)/shard_map/ppermute | solution.py:13
  94.1 2.1 gather_fusion.1
  97.0 1.0 slice_bitcast_fusion.3
  97.9 1.8 broadcast_in_dim.179
  99.7 2.9 broadcast_in_dim.180
  102.7 2.7 broadcast_in_dim.195
  105.4 3.0 broadcast_in_dim.196
  108.4 1.8 broadcast_in_dim.190
  110.1 2.9 broadcast_in_dim.191
  113.0 1.7 broadcast_in_dim.185
  114.7 3.0 broadcast_in_dim.186
  117.8 4.5 %fusion = (f32[1024]{0:T(1024)S(1)}, bf16[1024,512]{1,0:T(8,128)(2,1)S(1)}) fusion(bf16[1024,512]{1,0:T(8,128)(2,1)} %gather_fusion.2, pred[1024]{0:T(1024)(128)(4,1)S(1)} %copy-done.35, f32[1024,512]{1,0:T(8,128)} %broadcast_in_dim.196, pred[1024]{0:T(1024)(128)(4,1)S(1)} %copy-done.37, f32[1024,512]{1,0:T(8,128)} %broadcast_in_dim.191, ...), kind=kLoop, calls=%fused_computation.12 | loop fusion | flops 6814720 | bytes 10494976 | tf_op jit(solution)/shard_map/reduce_sum | solution.py:50
  122.8 1.6 fusion.27
  124.4 1.6 fusion.29
  126.0 1.6 fusion.30
  127.7 1.6 fusion.26
  129.8 1.4 fusion.28
  131.3 1.6 fusion.48
  132.8 1.4 fusion.51
  134.2 1.4 fusion.50
  135.6 1.5 fusion.49
  137.1 3.3 add_add_fusion
  140.4 2.9 reshape.291
  143.4 7.3 %select_reduce_fusion.3 = (bf16[256,512]{1,0:T(8,128)(2,1)S(1)}, bf16[256,512]{1,0:T(8,128)(2,1)S(1)}, bf16[256,512]{1,0:T(8,128)(2,1)S(1)}, bf16[256,512]{1,0:T(8,128)(2,1)S(1)}) fusion(f32[256,4,512]{2,1,0:T(4,128)} %reshape.291, pred[256,4]{1,0:T(8,128)(4,1)S(1)} %copy-done.24, pred[256,4]{1,0:T(8,128)(4,1)S(1)} %copy-done.28, ...), kind=kLoop, calls=%fused_computation.17 | loop fusion | flops 3670016 | bytes 3149824 | tf_op jit(solution)/shard_map/reduce_sum | solution.py:76
  151.7 2.8 convolution_bitcast_fusion
  154.5 5.4 %copy.60 = f32[4,512,512]{2,0,1:T(4,128)} copy(f32[4,512,512]{1,2,0:T(8,128)} %convolution_bitcast_fusion) | data formatting | bytes 8388608 | tf_op jit(solution)/shard_map/hd,khe->kde/transpose | solution.py:82
  160.0 2.4 fusion.52
  162.7 1.5 convolution_bitcast_fusion.2
  164.2 1.1 broadcast_in_dim.172
  165.3 33.0 %scatter_fusion.1 = f32[16,32,512]{2,1,0:T(8,128)} fusion(f32[16,32,512]{2,1,0:T(8,128)} %broadcast_in_dim.172, s32[256]{0:T(256)S(1)} %bitcast.112, f32[256,512]{1,0:T(8,128)} %convolution_bitcast_fusion.2), kind=kCustom, calls=%fused_computation.5 | custom fusion | bytes 1574912 | tf_op jit(solution)/shard_map/scatter | solution.py:85
  198.3 7.3 %all-to-all-start.2 = ((f32[16,32,512]{2,1,0:T(8,128)}), f32[16,32,512]{2,1,0:T(8,128)}, u32[]{:S(2)}, u32[]{:S(2)}) async-start(f32[16,32,512]{2,1,0:T(8,128)} %scatter_fusion.1), calls=%async_computation.2 | async-start | bytes 2097152 | tf_op jit(solution)/shard_map/all_to_all | solution.py:87
  205.7 1.7 convolution_add_fusion.1
  207.5 1.9 collective-permute-start.6
  209.8 3.8 collective-permute-start.9
  214.1 30.6 %collective-permute-done.6 = f32[256,512]{1,0:T(8,128)S(1)} collective-permute-done((f32[256,512]{1,0:T(8,128)S(1)}, f32[256,512]{1,0:T(8,128)S(1)}, u32[]{:S(2)}, u32[]{:S(2)}) %collective-permute-start.6) | collective-permute-done | bytes 524320 | tf_op jit(solution)/shard_map/ppermute | solution.py:13
  244.8 2.4 collective-permute-start.7
  247.6 2.3 collective-permute-done.9
  249.9 1.2 convolution_add_fusion
  251.1 18.8 %collective-permute-done.7 = f32[256,512]{1,0:T(8,128)S(1)} collective-permute-done((f32[256,512]{1,0:T(8,128)S(1)}, f32[256,512]{1,0:T(8,128)S(1)}, u32[]{:S(2)}, u32[]{:S(2)}) %collective-permute-start.7) | collective-permute-done | bytes 524320 | tf_op jit(solution)/shard_map/ppermute | solution.py:13
  269.9 0.9 add.203
  270.8 5.3 %scatter_custom_fusion.2 = f32[512,512]{1,0:T(8,128)} fusion(s32[512]{0:T(512)} %copy-done.33, f32[512,512]{1,0:T(8,128)} %bitcast.26, f32[]{:T(128)} %constant.38.clone.1), kind=kCustom, calls=%fused_computation.68 | custom fusion | flops 262144 | bytes 1049088 | tf_op jit(solution)/shard_map/scatter-add | solution.py:89
  276.1 9.4 %scatter_custom_fusion.3 = f32[512,512]{1,0:T(8,128)} fusion(f32[512,512]{1,0:T(8,128)} %scatter_custom_fusion.2, s32[1024]{0:T(1024)} %bitcast.126, bf16[1024,512]{1,0:T(8,128)(2,1)S(1)} %get-tuple-element.15, f32[1024]{0:T(1024)S(1)} %divide_add_fusion), kind=kCustom, calls=%fused_computation.13 | custom fusion | flops 1572864 | bytes 2101248 | tf_op jit(solution)/shard_map/scatter-add | solution.py:90
  285.5 5.0 %scatter_custom_fusion.4 = f32[512,512]{1,0:T(8,128)} fusion(f32[512,512]{1,0:T(8,128)} %scatter_custom_fusion.3, s32[256]{0:T(256)} %bitcast.130, f32[256,512]{1,0:T(8,128)} %collective-permute-done.8, f32[256,512]{1,0:T(8,128)} %collective-permute-done.10), kind=kCustom, calls=%fused_computation.66 | custom fusion | flops 262144 | bytes 2097152 | tf_op jit(solution)/shard_map/scatter-add | solution.py:93
  291.8 92.5 %all-reduce.3.cloned.1.call-done = f32[4,512,512]{2,0,1:T(4,128)} async-done(((f32[4,512,512]{2,0,1:T(4,128)}), f32[4,512,512]{2,0,1:T(4,128)}) %all-reduce.3.cloned.1.call-update) | async-done | bytes 4194320
  384.3 1.0 constant_dynamic-slice_fusion
  385.3 0.8 copy.61
  (141 shorter events, 11.7 us)
Async XLA Ops:
  8.0 88.3 %copy-start = (bf16[4,512,512]{2,1,0:T(8,128)(2,1)S(1)}, bf16[4,512,512]{2,1,0:T(8,128)(2,1)}, u32[]{:S(2)}) copy-start(bf16[4,512,512]{2,1,0:T(8,128)(2,1)} %param.8) | copy-start | bytes 6291460
  8.0 47.9 %copy-start.41 = (s32[1,256]{1,0:T(1,128)S(1)}, s32[1,256]{1,0:T(1,128)}, u32[]{:S(2)}) copy-start(s32[1,256]{1,0:T(1,128)} %param.13) | copy-start | bytes 3076
  8.0 48.5 %copy-start.1 = (bf16[512,512]{1,0:T(8,128)(2,1)S(1)}, bf16[512,512]{1,0:T(8,128)(2,1)}, u32[]{:S(2)}) copy-start(bf16[512,512]{1,0:T(8,128)(2,1)} %param.7) | copy-start | bytes 1572868
  47.6 15.8 %all-to-all-start = ((s32[16,1,32]{2,1,0:T(1,128)}), s32[16,1,32]{2,1,0:T(1,128)S(1)}, u32[]{:S(2)}, u32[]{:S(2)}) async-start(s32[16,1,32]{2,1,0:T(1,128)} %bitcast.6), calls=%async_computation | async-start | bytes 16384 | tf_op jit(solution)/shard_map/all_to_all | solution.py:34
  55.9 0.6 copy-start.39
  57.8 7.7 %copy-start.13 = (bf16[256,512]{1,0:T(8,128)(2,1)}, bf16[256,512]{1,0:T(8,128)(2,1)S(1)}, u32[]{:S(2)}) copy-start(bf16[256,512]{1,0:T(8,128)(2,1)S(1)} %broadcast_select_fusion.1) | copy-start | bytes 786436
  57.8 32.2 %collective-permute-start.3 = (bf16[256,512]{1,0:T(8,128)(2,1)S(1)}, bf16[256,512]{1,0:T(8,128)(2,1)}, u32[]{:S(2)}, u32[]{:S(2)}) collective-permute-start(bf16[256,512]{1,0:T(8,128)(2,1)S(1)} %broadcast_select_fusion.1), channel_id=1, source_target_pairs={{2,0},{4,2},{6,4},{8,6},{10,8},{12,10},{14,12},{16,14},{18,16},{20... | collective-permute-start | bytes 786440 | tf_op jit(solution)/shard_map/ppermute | solution.py:13
  63.4 11.0 %collective-permute-start = (bf16[256,512]{1,0:T(8,128)(2,1)S(1)}, bf16[256,512]{1,0:T(8,128)(2,1)}, u32[]{:S(2)}, u32[]{:S(2)}) collective-permute-start(bf16[256,512]{1,0:T(8,128)(2,1)S(1)} %broadcast_select_fusion.1), channel_id=1, source_target_pairs={{30,0},{0,2},{2,4},{4,6},{6,8},{8,10},{10,12},{12,14},{14,16},{16,... | collective-permute-start | bytes 786440 | tf_op jit(solution)/shard_map/ppermute | solution.py:13
  63.5 2.0 copy-start.33
  65.5 8.0 %copy-start.40 = (s32[256,4]{0,1:T(4,128)S(1)}, s32[256,4]{0,1:T(4,128)}, u32[]{:S(2)}) copy-start(s32[256,4]{0,1:T(4,128)} %param.11) | copy-start | bytes 12292
  65.5 8.6 %copy-start.31 = (s32[256,4]{0,1:T(4,128)S(1)}, s32[256,4]{0,1:T(4,128)}, u32[]{:S(2)}) copy-start(s32[256,4]{0,1:T(4,128)} %param.12) | copy-start | bytes 12292
  66.4 27.7 %all-to-all-start.1 = ((bf16[16,32,512]{2,1,0:T(8,128)(2,1)}), bf16[16,32,512]{2,1,0:T(8,128)(2,1)S(1)}, u32[]{:S(2)}, u32[]{:S(2)}) async-start(bf16[16,32,512]{2,1,0:T(8,128)(2,1)} %broadcast_select_fusion), calls=%async_computation.1 | async-start | bytes 1048576 | tf_op jit(solution)/shard_map/all_to_all | solution.py:37
  73.4 310.9 %all-reduce.3.cloned.1.call-start = ((), (), s32[]{:S(2)}) async-start(), calls=%async_computation.5 | async-start | bytes 8388608
  74.4 2.0 copy-start.32
  74.4 19.7 %collective-permute-start.1 = (bf16[256,512]{1,0:T(8,128)(2,1)}, bf16[256,512]{1,0:T(8,128)(2,1)}, u32[]{:S(2)}, u32[]{:S(2)}) collective-permute-start(bf16[256,512]{1,0:T(8,128)(2,1)} %collective-permute-done), channel_id=1, source_target_pairs={{30,0},{0,2},{2,4},{4,6},{6,8},{8,10},{10,12},{12,14},{14,16},{16,... | collective-permute-start | bytes 786440 | tf_op jit(solution)/shard_map/ppermute | solution.py:13
  77.9 12.0 %copy-start.23 = (pred[256,4]{1,0:T(8,128)(4,1)}, pred[256,4]{1,0:T(8,128)(4,1)S(1)}, u32[]{:S(2)}) copy-start(pred[256,4]{1,0:T(8,128)(4,1)S(1)} %copy.48) | copy-start | bytes 3076
  81.0 8.9 %copy-start.25 = (pred[256,4]{1,0:T(8,128)(4,1)}, pred[256,4]{1,0:T(8,128)(4,1)S(1)}, u32[]{:S(2)}) copy-start(pred[256,4]{1,0:T(8,128)(4,1)S(1)} %copy.50) | copy-start | bytes 3076
  82.6 7.4 %copy-start.27 = (pred[256,4]{1,0:T(8,128)(4,1)}, pred[256,4]{1,0:T(8,128)(4,1)S(1)}, u32[]{:S(2)}) copy-start(pred[256,4]{1,0:T(8,128)(4,1)S(1)} %copy.52) | copy-start | bytes 3076
  84.1 5.8 %copy-start.29 = (pred[256,4]{1,0:T(8,128)(4,1)}, pred[256,4]{1,0:T(8,128)(4,1)S(1)}, u32[]{:S(2)}) copy-start(pred[256,4]{1,0:T(8,128)(4,1)S(1)} %copy.51) | copy-start | bytes 3076
  90.0 37.7 %collective-permute-start.4 = (bf16[256,512]{1,0:T(8,128)(2,1)}, bf16[256,512]{1,0:T(8,128)(2,1)}, u32[]{:S(2)}, u32[]{:S(2)}) collective-permute-start(bf16[256,512]{1,0:T(8,128)(2,1)} %collective-permute-done.3), channel_id=1, source_target_pairs={{2,0},{4,2},{6,4},{8,6},{10,8},{12,10},{14,12},{16,14},{18,16},{20... | collective-permute-start | bytes 786440 | tf_op jit(solution)/shard_map/ppermute | solution.py:13
  94.1 35.6 %collective-permute-start.2 = (bf16[256,512]{1,0:T(8,128)(2,1)}, bf16[256,512]{1,0:T(8,128)(2,1)}, u32[]{:S(2)}, u32[]{:S(2)}) collective-permute-start(bf16[256,512]{1,0:T(8,128)(2,1)} %collective-permute-done.1), channel_id=1, source_target_pairs={{30,0},{0,2},{2,4},{4,6},{6,8},{8,10},{10,12},{12,14},{14,16},{16,... | collective-permute-start | bytes 786440 | tf_op jit(solution)/shard_map/ppermute | solution.py:13
  114.7 3.0 copy-start.34
  114.7 3.0 copy-start.35
  114.7 3.0 copy-start.36
  114.7 3.0 copy-start.37
  114.7 3.0 copy-start.38
  117.8 4.5 %copy-start.14 = (bf16[256,512]{1,0:T(8,128)(2,1)S(1)}, bf16[256,512]{1,0:T(8,128)(2,1)}, u32[]{:S(2)}) copy-start(bf16[256,512]{1,0:T(8,128)(2,1)} %copy-done.13) | copy-start | bytes 786436
  122.8 6.6 %copy-start.12 = (bf16[1024,256]{1,0:T(8,128)(2,1)}, bf16[1024,256]{1,0:T(8,128)(2,1)S(1)}, u32[]{:S(2)}) copy-start(bf16[1024,256]{1,0:T(8,128)(2,1)S(1)} %fusion.31) | copy-start | bytes 1572868
  124.4 9.8 %copy-start.10 = (bf16[1024,256]{1,0:T(8,128)(2,1)}, bf16[1024,256]{1,0:T(8,128)(2,1)S(1)}, u32[]{:S(2)}) copy-start(bf16[1024,256]{1,0:T(8,128)(2,1)S(1)} %fusion.27) | copy-start | bytes 1572868
  126.0 9.6 %copy-start.8 = (bf16[1024,256]{1,0:T(8,128)(2,1)}, bf16[1024,256]{1,0:T(8,128)(2,1)S(1)}, u32[]{:S(2)}) copy-start(bf16[1024,256]{1,0:T(8,128)(2,1)S(1)} %fusion.29) | copy-start | bytes 1572868
  127.7 3.6 copy-start.7
  129.3 3.5 copy-start.3
  131.2 5.9 %copy-start.5 = (bf16[1024,256]{1,0:T(8,128)(2,1)}, bf16[1024,256]{1,0:T(8,128)(2,1)S(1)}, u32[]{:S(2)}) copy-start(bf16[1024,256]{1,0:T(8,128)(2,1)S(1)} %fusion.28) | copy-start | bytes 1572868
  135.6 1.5 copy-start.2
  140.4 2.9 copy-start.24
  140.4 2.9 copy-start.26
  140.4 2.9 copy-start.28
  140.4 2.9 copy-start.30
  150.7 0.7 copy-start.15
  150.7 0.8 copy-start.17
  150.7 0.9 copy-start.19
  150.7 0.9 copy-start.21
  160.0 2.7 copy-start.16
  160.0 2.7 copy-start.18
  160.0 2.7 copy-start.20
  160.0 2.7 copy-start.22
  162.4 43.3 %collective-permute-start.5 = (f32[256,512]{1,0:T(8,128)}, f32[256,512]{1,0:T(8,128)}, u32[]{:S(2)}, u32[]{:S(2)}) collective-permute-start(f32[256,512]{1,0:T(8,128)} %fusion.52), channel_id=1, source_target_pairs={{30,0},{0,2},{2,4},{4,6},{6,8},{8,10},{10,12},{12,14},{14,16},{16,... | collective-permute-start | bytes 1572872 | tf_op jit(solution)/shard_map/ppermute | solution.py:13
  198.3 72.5 %all-to-all-start.2 = ((f32[16,32,512]{2,1,0:T(8,128)}), f32[16,32,512]{2,1,0:T(8,128)}, u32[]{:S(2)}, u32[]{:S(2)}) async-start(f32[16,32,512]{2,1,0:T(8,128)} %scatter_fusion.1), calls=%async_computation.2 | async-start | bytes 2097152 | tf_op jit(solution)/shard_map/all_to_all | solution.py:87
  205.6 180.4 %reduce-scatter.2.cloned.1.call-start = ((), (), s32[]{:S(2)}) async-start(), calls=%async_computation.4 | async-start | bytes 1572864 | tf_op jit(solution)/shard_map/reduce_scatter | solution.py:94
  205.7 3.7 copy-start.11
  205.7 8.0 %copy-start.9 = (bf16[1024,256]{1,0:T(8,128)(2,1)S(1)}, bf16[1024,256]{1,0:T(8,128)(2,1)}, u32[]{:S(2)}) copy-start(bf16[1024,256]{1,0:T(8,128)(2,1)} %copy-done.8) | copy-start | bytes 1572868
  207.5 37.2 %collective-permute-start.6 = (f32[256,512]{1,0:T(8,128)S(1)}, f32[256,512]{1,0:T(8,128)S(1)}, u32[]{:S(2)}, u32[]{:S(2)}) collective-permute-start(f32[256,512]{1,0:T(8,128)S(1)} %convolution_add_fusion.1), channel_id=1, source_target_pairs={{30,0},{0,2},{2,4},{4,6},{6,8},{8,10},{10,12},{12,14},{14,16},{16,... | collective-permute-start | bytes 1572872 | tf_op jit(solution)/shard_map/ppermute | solution.py:13
  209.8 37.3 %copy-start.6 = (bf16[1024,256]{1,0:T(8,128)(2,1)S(1)}, bf16[1024,256]{1,0:T(8,128)(2,1)}, u32[]{:S(2)}) copy-start(bf16[1024,256]{1,0:T(8,128)(2,1)} %copy-done.5) | copy-start | bytes 1572868
  209.8 40.0 %collective-permute-start.9 = (f32[256,512]{1,0:T(8,128)S(1)}, f32[256,512]{1,0:T(8,128)S(1)}, u32[]{:S(2)}, u32[]{:S(2)}) collective-permute-start(f32[256,512]{1,0:T(8,128)S(1)} %fusion.55), channel_id=1, source_target_pairs={{2,0},{4,2},{6,4},{8,6},{10,8},{12,10},{14,12},{16,14},{18,16},{20... | collective-permute-start | bytes 1572872 | tf_op jit(solution)/shard_map/ppermute | solution.py:13
  214.1 35.7 %copy-start.4 = (bf16[1024,256]{1,0:T(8,128)(2,1)S(1)}, bf16[1024,256]{1,0:T(8,128)(2,1)}, u32[]{:S(2)}) copy-start(bf16[1024,256]{1,0:T(8,128)(2,1)} %copy-done.3) | copy-start | bytes 1572868
  244.8 25.2 %collective-permute-start.7 = (f32[256,512]{1,0:T(8,128)S(1)}, f32[256,512]{1,0:T(8,128)S(1)}, u32[]{:S(2)}, u32[]{:S(2)}) collective-permute-start(f32[256,512]{1,0:T(8,128)S(1)} %add.202), channel_id=1, source_target_pairs={{30,0},{0,2},{2,4},{4,6},{6,8},{8,10},{10,12},{12,14},{14,16},{16,... | collective-permute-start | bytes 1572872 | tf_op jit(solution)/shard_map/ppermute | solution.py:13
  251.1 34.4 %collective-permute-start.10 = (f32[256,512]{1,0:T(8,128)}, f32[256,512]{1,0:T(8,128)}, u32[]{:S(2)}, u32[]{:S(2)}) collective-permute-start(f32[256,512]{1,0:T(8,128)} %convolution_add_fusion), channel_id=1, source_target_pairs={{28,0},{30,2},{0,4},{2,6},{4,8},{6,10},{8,12},{10,14},{12,16},{14,... | collective-permute-start | bytes 1572872 | tf_op jit(solution)/shard_map/ppermute | solution.py:13
  270.8 14.7 %collective-permute-start.8 = (f32[256,512]{1,0:T(8,128)}, f32[256,512]{1,0:T(8,128)}, u32[]{:S(2)}, u32[]{:S(2)}) collective-permute-start(f32[256,512]{1,0:T(8,128)} %add.203), channel_id=1, source_target_pairs={{6,0},{8,2},{10,4},{12,6},{14,8},{16,10},{18,12},{20,14},{22,16},{... | collective-permute-start | bytes 1572872 | tf_op jit(solution)/shard_map/ppermute | solution.py:13
  285.5 5.0 %copy-start.42 = (u32[32]{0:T(128)S(1)}, u32[32]{0:T(128)}, u32[]{:S(2)}) copy-start(u32[32]{0:T(128)} %constant.133) | copy-start | bytes 388
Sparse Core Ops, SparseCore 0:
  160.1 224.1 all-reduce.2
Sparse Core Ops, SparseCore 1:
  290.6 15.3 reduce-scatter.1
where the time goes:
time: 397 us; the launch traced here: 394 us
  waiting for transfers between devices  144 us (36%)
  local copies, waits for them, and re-layouts  122 us (31%)
  starting transfers between devices  42.8 us (11%)
  other arithmetic  37.6 us (9%)
  matrix products  29.7 us (7%)
  between operations  16.9 us (4%)
    unnamed x3, waiting for transfers between devices  92.6 us
    ppermute x11, waiting for transfers between devices, shifted(): return lax.ppermute(block, axis, route)  51.7 us
    scatter x1, local copies, waits for them, and re-layouts, per_device(): jnp.full((shard_count, capacity), -1, jnp.int32).at[head_shard, head_slot]  35.8 us
    scatter x1, local copies, waits for them, and re-layouts, per_device(): jnp.zeros((shard_count, capacity, D), jnp.float32).at[head_shard, head_slot]  33 us
    broadcast_in_dim x12, local copies, waits for them, and re-layouts, per_device(): jnp.where((query_rel == rel_index)[:, :, None], products[rel_index][:, No...  22.9 us
    ppermute x11, starting transfers between devices, shifted(): return lax.ppermute(block, axis, route)  20.1 us
    dot_general x6, matrix products, visit(): jnp.dot(weights, neg_block, preferred_element_type=jnp.float32)  9.54 us
    scatter-add x1, other arithmetic, per_device(): local_grad.at[tail_row.reshape(-1)]  9.43 us
  transfers between devices with their start and end apart: 16, of which 4 were waited for; matrix products, arithmetic and copies ran while one was open for 30% of the time, Pallas kernels for 0%

commit v1 on v0

v1 whole, which is shorter than its diff:
```python
import functools

import jax
import jax.numpy as jnp
from jax import lax
from jax.experimental import pallas as pl
from jax.experimental.pallas import tpu as pltpu
from jax.sharding import PartitionSpec as P

STOPS = 6
FORE = STOPS // 2
BACK = STOPS - 1 - FORE
OFFSETS = tuple(range(1, FORE + 1)) + tuple(range(-1, -BACK - 1, -1))
BF = jnp.bfloat16
F32 = jnp.float32


def iota(shape, dim):
    return lax.broadcasted_iota(jnp.int32, shape, dim)


def column(row):
    n = row.shape[1]
    return jnp.sum(
        jnp.where(iota((n, n), 0) == iota((n, n), 1), row.astype(F32), 0.0), axis=1, keepdims=True
    ).astype(jnp.int32)


def hot(index, shape, dim):
    return jnp.where(iota(shape, dim) == index, 1.0, 0.0).astype(BF)


def dot(a, b):
    return jnp.dot(a, b, preferred_element_type=F32)


def dot_t(a, b):
    return lax.dot_general(a, b, (((1,), (1,)), ((), ())), preferred_element_type=F32)


def t_dot(a, b):
    return lax.dot_general(a, b, (((0,), (0,)), ((), ())), preferred_element_type=F32)


def halves(x):
    top = x.astype(BF)
    return top, (x - top.astype(F32)).astype(BF)


def ask_kernel(owner_ref, row_ref, asked_ref, pos_ref):
    shards, cap = asked_ref.shape
    heads = owner_ref.shape[1]
    owner = owner_ref[...]
    owner_col = column(owner)
    square = (heads, heads)
    same = owner_col == owner
    slot_row = jnp.sum(
        jnp.where(same & (iota(square, 0) < iota(square, 1)), 1.0, 0.0), axis=0, keepdims=True
    ).astype(jnp.int32)
    slot_col = jnp.sum(
        jnp.where(same & (iota(square, 1) < iota(square, 0)), 1.0, 0.0), axis=1, keepdims=True
    ).astype(jnp.int32)
    pos_ref[...] = owner * cap + slot_row
    value = row_ref[...] + 1
    mine = iota((shards, heads), 0) == owner
    high = jnp.where(mine, (value // 256).astype(F32), 0.0).astype(BF)
    low = jnp.where(mine, (value % 256).astype(F32), 0.0).astype(BF)
    place = hot(slot_col, (heads, cap), 1)
    asked_ref[...] = (256.0 * dot(high, place) + dot(low, place)).astype(jnp.int32) - 1


def take_kernel(row_ref, entity_ref, out_ref):
    count = row_ref.shape[1]
    pick = hot(column(row_ref[...]), (count, entity_ref.shape[0]), 1)
    out_ref[...] = dot(pick, entity_ref[...]).astype(BF)


def serve_kernel(wanted_ref, entity_ref, out_ref):
    shards, cap = wanted_ref.shape
    cols = jnp.concatenate([column(wanted_ref[s : s + 1, :]) for s in range(shards)], axis=0)
    pick = hot(cols, (shards * cap, entity_ref.shape[0]), 1)
    out_ref[...] = dot(pick, entity_ref[...]).astype(BF)


def visit_kernel(pos_ref, qrel_ref, tail_ref, fetched_ref, rel_ref, ent_ref, *refs):
    blocks = refs[:STOPS]
    terms = refs[STOPS : 2 * STOPS]
    vec_ref, q_ref, pw_ref, pair_ref, prod, near, weight, gq = refs[2 * STOPS :]
    heads, width = vec_ref.shape
    rels = rel_ref.shape[0]
    per = qrel_ref.shape[0]
    slots = fetched_ref.shape[0]
    rows = blocks[0].shape[0]
    ents = ent_ref.shape[0]
    for index, block in enumerate(blocks):
        near[index * rows : (index + 1) * rows, :] = block[...]
    vec = dot(hot(column(pos_ref[...]), (heads, slots), 1), fetched_ref[...]).astype(BF)
    vec_ref[...] = vec

    @pl.loop(0, rels)
    def _(k):
        prod[k] = dot(vec_ref[...], rel_ref[k])

    @pl.loop(0, per)
    def _(j):
        kind = column(qrel_ref[pl.ds(j, 1), :])
        query = prod[0]
        for k in range(1, rels):
            query = jnp.where(kind == k, prod[k], query)
        query = query.astype(BF)
        q_ref[j] = query
        tail = dot(hot(column(tail_ref[pl.ds(j, 1), :]), (heads, ents), 1), ent_ref[...])
        score = jnp.sum(query.astype(F32) * tail, axis=1, keepdims=True)
        pw = jax.nn.sigmoid(score) - 1.0
        pw_ref[j] = pw
        seen = dot_t(query, near[...])
        w = (jax.nn.sigmoid(seen) / STOPS).astype(BF)
        weight[pl.ds(pl.multiple_of(j * heads, heads), heads), :] = w
        gq[j] = pw * tail + dot(w, near[...])

    for index, term in enumerate(terms):
        part = t_dot(
            weight[:, index * rows : (index + 1) * rows], q_ref[...].reshape(per * heads, width)
        )
        term[...] = part.astype(term.dtype)
    kinds = [column(qrel_ref[j : j + 1, :]) for j in range(per)]

    @pl.loop(0, rels)
    def _(k):
        total = jnp.where(kinds[0] == k, gq[0], 0.0)
        for j in range(1, per):
            total = total + jnp.where(kinds[j] == k, gq[j], 0.0)
        pair_ref[k] = total.astype(BF)


def push_kernel(
    step, me_ref, pos_ref, vec_ref, pair_ref, rel_ref, keep_a, send_a, keep_b, send_b, bucket_ref, turned, a_side, b_side
):
    heads, width = vec_ref.shape
    rels = rel_ref.shape[0]
    half = width // 2
    slots = bucket_ref.shape[0]
    me = me_ref[0]
    x, y = me % 2, (me // 2) % 2
    turned[...] = vec_ref[...].astype(F32).T
    deep = a_side.shape[0] // 4
    lines = deep // step
    for fx in range(2):
        for fy in range(2):
            for z in range(lines):
                block = z * 4 + ((y + fy) % 2) * 2 + (x + fx) % 2
                rows = turned[pl.ds(pl.multiple_of(block * step, step), step), :]
                at = (fx * 2 + fy) * deep + z * step
                bt = (fy * 2 + fx) * deep + z * step
                a_side[at : at + step, :] = rows
                b_side[bt : bt + step, :] = rows
    head = jnp.zeros((heads, width), F32)
    for k in range(rels):
        head = head + dot_t(pair_ref[k], rel_ref[k])
    bucket_ref[...] = dot(hot(pos_ref[...], (slots, heads), 0), head.astype(BF)).astype(BF)
    for side, keep, send, first in ((a_side, keep_a, send_a, 0), (b_side, keep_b, send_b, rels // 2)):
        for k in range(rels // 2):
            full = dot(side[...].astype(BF), pair_ref[first + k])
            keep[k] = full[:half]
            send[k] = full[half:].astype(BF)


def tail_kernel(tail_ref, q_ref, pw_ref, out_ref):
    ents, heads = out_ref.shape[0], q_ref.shape[1]
    total = jnp.zeros(out_ref.shape, F32)
    for j in range(q_ref.shape[0]):
        spot = hot(tail_ref[j : j + 1, :], (ents, heads), 0)
        top, rest = halves(pw_ref[j] * q_ref[j].astype(F32))
        total = total + dot(spot, top) + dot(spot, rest)
    out_ref[...] = total


def sum_kernel(reps, me_ref, wanted_ref, neg_ref, returned_ref, base_ref, *refs):
    terms = refs[:STOPS]
    own_ref, outs = refs[STOPS], refs[STOPS + 1 :]
    ents = base_ref.shape[0]
    total = terms[0][...]
    for term in terms[1:]:
        total = total + term[...].astype(F32)
    top, rest = halves(total)
    spot = hot(neg_ref[...], (ents, neg_ref.shape[1]), 0)
    back = hot(wanted_ref[...], (ents, wanted_ref.shape[1]), 0)
    full = base_ref[...] + dot(back, returned_ref[...]) + dot(spot, top) + dot(spot, rest)
    chunk = own_ref.shape[1]
    rep = me_ref[1]
    parts = [full[:, c * chunk : (c + 1) * chunk] for c in range(reps)]

    def pick(number):
        value = parts[0]
        for c in range(1, reps):
            value = jnp.where(number == c, parts[c], value)
        return value

    own_ref[...] = pick(rep)
    for shift, out in enumerate(outs):
        out[...] = pick((rep + shift + 1) % reps).astype(BF)


def kernel(body, outs, scratch=(), smem=0):
    def call(*args):
        specs = [
            pl.BlockSpec(memory_space=pltpu.SMEM if i < smem else pltpu.VMEM) for i in range(len(args))
        ]
        return pl.pallas_call(
            body,
            out_shape=[jax.ShapeDtypeStruct(s, d) for s, d in outs],
            in_specs=specs,
            out_specs=[pl.BlockSpec(memory_space=pltpu.VMEM)] * len(outs),
            scratch_shapes=[pltpu.VMEM(s, d) for s, d in scratch],
        )(*args)

    return call


def per_device(entity, relation, head_owner, head_row, query_rel, tail_row, neg_row):
    shards, reps = lax.axis_size("blk"), lax.axis_size("rep")
    ents, width = entity.shape
    rels = relation.shape[0]
    heads = head_row.shape[0]
    per = query_rel.shape[1]
    rows = neg_row.shape[1]
    cap = max(2, 2 * heads // shards)
    slots = shards * cap
    step = width // shards
    lines = shards // 4
    me = jnp.stack([lax.axis_index("blk"), lax.axis_index("rep")]).astype(jnp.int32)

    owner_row = head_owner.reshape(1, heads)
    qrel, tail = query_rel.T, tail_row.T
    asked, pos = kernel(ask_kernel, [((shards, cap), jnp.int32), ((1, heads), jnp.int32)])(
        owner_row, head_row.reshape(1, heads)
    )
    wanted = lax.all_to_all(asked, "blk", split_axis=0, concat_axis=0, tiled=True)
    (own_block,) = kernel(take_kernel, [((rows, width), BF)])(neg_row, entity)

    def moved(value, distance):
        return lax.ppermute(value, "blk", [((i - distance) % shards, i) for i in range(shards)])

    def flipped(value, bit):
        return lax.ppermute(value, "blk", [(i, i ^ bit) for i in range(shards)])

    blocks = [own_block] + [moved(own_block, o) for o in OFFSETS]
    (served,) = kernel(serve_kernel, [((slots, width), BF)])(wanted, entity)
    fetched = lax.all_to_all(
        served.reshape(shards, cap, width), "blk", split_axis=0, concat_axis=0, tiled=True
    ).reshape(slots, width)

    outs = [((rows, width), F32)] + [((rows, width), BF)] * (STOPS - 1)
    outs += [((heads, width), BF), ((per, heads, width), BF), ((per, heads, 1), F32), ((rels, heads, width), BF)]
    scratch = [
        ((rels, heads, width), F32),
        ((STOPS * rows, width), BF),
        ((per * heads, STOPS * rows), BF),
        ((per, heads, width), F32),
    ]
    *terms, vec, queries, pos_weight, pair = kernel(visit_kernel, outs, scratch)(
        pos, qrel, tail, fetched, relation, entity, *blocks
    )
    back = [terms[0]] + [moved(t, -o) for t, o in zip(terms[1:], OFFSETS)]

    part = (rels // 2, width // 2, width)
    keep_a, send_a, keep_b, send_b, buckets = kernel(
        functools.partial(push_kernel, step),
        [(part, F32), (part, BF), (part, F32), (part, BF), ((slots, width), BF)],
        [((width, heads), F32)] * 3,
        smem=1,
    )(me, pos, vec, pair, relation)
    got_a, got_b = flipped(send_a, 1), flipped(send_b, 2)
    returned = lax.all_to_all(
        buckets.reshape(shards, cap, width), "blk", split_axis=0, concat_axis=0, tiled=True
    ).reshape(slots, width)
    (base,) = kernel(tail_kernel, [((ents, width), F32)])(tail, queries, pos_weight)

    quarter = width // 4
    sum_a = keep_a + got_a.astype(F32)
    sum_b = keep_b + got_b.astype(F32)
    more_a = flipped(sum_a[:, quarter:].astype(BF), 2)
    more_b = flipped(sum_b[:, quarter:].astype(BF), 1)
    sum_a = sum_a[:, :quarter] + more_a.astype(F32)
    sum_b = sum_b[:, :quarter] + more_b.astype(F32)
    both = jnp.concatenate([sum_a, sum_b]).astype(BF).reshape(rels, lines, step, width)
    both = both.transpose(1, 0, 2, 3)
    groups = [[c + 4 * z for z in range(lines)] for c in range(4)]
    lined = lax.all_to_all(
        both, "blk", split_axis=0, concat_axis=0, tiled=True, axis_index_groups=groups
    )
    grad_rel = jnp.sum(lined.astype(F32), axis=0)

    chunk = width // reps
    own, *others = kernel(
        functools.partial(sum_kernel, reps),
        [((ents, chunk), F32)] + [((ents, chunk), BF)] * (reps - 1),
        smem=1,
    )(me, wanted.reshape(1, slots), neg_row, returned, base, *back)
    grad_entity = own
    for shift, other in enumerate(others):
        route = [(i, (i + shift + 1) % reps) for i in range(reps)]
        grad_entity = grad_entity + lax.ppermute(other, "rep", route).astype(F32)
    return (grad_entity, grad_rel)


def solution(mesh):
    placed = (
        P("blk", None),
        P("rep", None, None),
        P(("blk", "rep"), None),
        P(("blk", "rep")),
        P(("blk", "rep"), None),
        P(("blk", "rep"), None),
        P("blk", "rep"),
    )
    return jax.shard_map(
        per_device,
        mesh=mesh,
        in_specs=placed,
        out_specs=(P("blk", "rep"), P("rep", "blk", None)),
        check_vma=False,
    )
```

time: 397 us -> 144 us (0.36)
  local copies, waits for them, and re-layouts: 122 us -> 2.72 us
  waiting for transfers between devices: 144 us -> 45.7 us
  Pallas kernels: 0 us -> 32.1 us
  other arithmetic: 37.6 us -> 6.54 us
  matrix products: 29.7 us -> 0 us
  between operations: 16.9 us -> 0.81 us
  blocking collectives: 0 us -> 15.7 us
  starting transfers between devices: 42.8 us -> 38.8 us
    unnamed x3 -> x0, waiting for transfers between devices: 92.6 us -> none
    scatter x2 -> x0, local copies, waits for them, and re-layouts: 68.8 us -> none  [the longest x1 35.8 us: per_device(): jnp.full((shard_count, capacity), -1, jnp.int32).at[head_shard, head_slot]]
    pallas_call x0 -> x7, Pallas kernels: none -> 32.1 us  [call(): pl.pallas_call(body, out_shape=[jax.ShapeDtypeStruct(s, d) for s, d in ou...]
    dot_general x21 -> x0, matrix products: 29.7 us -> none  [the longest x6 9.54 us: visit(): jnp.dot(weights, neg_block, preferred_element_type=jnp.float32)]
    broadcast_in_dim x16 -> x0, local copies, waits for them, and re-layouts: 26 us -> none  [the longest x12 22.9 us: per_device(): jnp.where((query_rel == rel_index)[:, :, None], products[rel_index][:, No...]
    scatter-add x3 -> x0, other arithmetic: 19.7 us -> none  [the longest x1 9.43 us: per_device(): local_grad.at[tail_row.reshape(-1)]]
    all_to_all x0 -> x1, blocking collectives: none -> 15.7 us  [per_device(): lax.all_to_all(asked, 'blk', split_axis=0, concat_axis=0, tiled=True)]
    reduce_sum x3 -> x1, other arithmetic: 12.6 us -> 0.77 us  [per_device(): grad_rel = jnp.sum(lined.astype(F32), axis=0)]
  transfers between devices with their start and end apart: 16 -> 18, of which waited for: 4 -> 11; matrix products, arithmetic and copies ran while one was open for 30% -> 5% of each run, Pallas kernels for 0% -> 7%
where the time goes in v1:
time: 144 us; the launch traced here: 142 us
  waiting for transfers between devices  45.7 us (32%)
  starting transfers between devices  38.8 us (27%)
  Pallas kernels  32.1 us (22%)
  blocking collectives  15.7 us (11%)
  other arithmetic  6.54 us (5%)
  local copies, waits for them, and re-layouts  2.72 us (2%)
    pallas_call x7, Pallas kernels, call(): pl.pallas_call(body, out_shape=[jax.ShapeDtypeStruct(s, d) for s, d in ou...  32.1 us
    ppermute x10, waiting for transfers between devices, moved(): lax.ppermute(value, 'blk', [((i - distance) % shards, i) for i in range(s...  32 us
    ppermute x10, starting transfers between devices, moved(): lax.ppermute(value, 'blk', [((i - distance) % shards, i) for i in range(s...  17.9 us
    all_to_all x1, blocking collectives, per_device(): lax.all_to_all(asked, 'blk', split_axis=0, concat_axis=0, tiled=True)  15.7 us
    ppermute x4, waiting for transfers between devices, flipped(): return lax.ppermute(value, 'blk', [(i, i ^ bit) for i in range(shards)])  11.6 us
    ppermute x4, starting transfers between devices, flipped(): return lax.ppermute(value, 'blk', [(i, i ^ bit) for i in range(shards)])  8.36 us
    all_to_all x1, starting transfers between devices, per_device(): lax.all_to_all(buckets.reshape(shards, cap, width), 'blk', split_axis=0,...  5.49 us
    all_to_all x1, starting transfers between devices, per_device(): lax.all_to_all(served.reshape(shards, cap, width), 'blk', split_axis=0, c...  3.57 us
  transfers between devices with their start and end apart: 18, of which 11 were waited for; matrix products, arithmetic and copies ran while one was open for 5% of the time, Pallas kernels for 7%

profile of v1, /device:TPU:0, one launch (start us, length us, event | category | flops | bytes accessed | tf_op | source)
XLA Modules:
  0.0 142.3 jit_solution(8815691997129775744)
XLA Ops:
  0.6 1.6 %shard_map.86 = (s32[16,32]{1,0:T(8,128)}, s32[1,256]{1,0:T(1,128)}) custom-call(s32[1,256]{1,0:T(1,128)} %bitcast.29, s32[1,256]{1,0:T(1,128)} %bitcast.30), custom_call_target="tpu_custom_call" | custom-call | tf_op jit(solution)/shard_map/pallas_call | solution.py:209
  2.3 15.7 %all_to_all.26 = s32[16,1,32]{2,1,0:T(1,128)} all-to-all(s32[16,1,32]{2,1,0:T(1,128)} %bitcast.27), channel_id=1, replica_groups=mesh['blk'=16,'rep'=2] {'blk'}, dimensions={0} | all-to-all | bytes 4096 | tf_op jit(solution)/shard_map/all_to_all | solution.py:238
  17.9 2.5 %shard_map.87 = bf16[512,512]{1,0:T(8,128)(2,1)} custom-call(s32[16,32]{1,0:T(8,128)} %bitcast.24, bf16[512,512]{1,0:T(8,128)(2,1)} %ent_ref.1), custom_call_target="tpu_custom_call" | custom-call | tf_op jit(solution)/shard_map/pallas_call | solution.py:209
  20.4 3.6 %all-to-all-start.1 = ((bf16[16,32,512]{2,1,0:T(8,128)(2,1)}), bf16[16,32,512]{2,1,0:T(8,128)(2,1)S(1)}, u32[]{:S(2)}, u32[]{:S(2)}) async-start(bf16[16,32,512]{2,1,0:T(8,128)(2,1)} %bitcast.18), calls=%async_computation.1 | async-start | bytes 1048576 | tf_op jit(solution)/shard_map/all_to_all | solution.py:249
  24.0 2.1 %shard_map.88.refs_0_ = bf16[256,512]{1,0:T(8,128)(2,1)} custom-call(s32[1,256]{1,0:T(1,128)} %neg_ref.1, bf16[512,512]{1,0:T(8,128)(2,1)} %ent_ref.1), custom_call_target="tpu_custom_call" | custom-call | tf_op jit(solution)/shard_map/pallas_call | solution.py:209
  26.1 4.6 %collective-permute-start.4 = (bf16[256,512]{1,0:T(8,128)(2,1)}, bf16[256,512]{1,0:T(8,128)(2,1)S(1)}, u32[]{:S(2)}, u32[]{:S(2)}) collective-permute-start(bf16[256,512]{1,0:T(8,128)(2,1)} %shard_map.88.refs_0_), channel_id=1, source_target_pairs={{4,0},{6,2},{8,4},{10,6},{12,8},{14,10},{16,12},{18,14},{20,16},{2... | collective-permute-start | bytes 786440 | tf_op jit(solution)/shard_map/ppermute | solution.py:242
  30.7 1.5 %collective-permute-start.3 = (bf16[256,512]{1,0:T(8,128)(2,1)}, bf16[256,512]{1,0:T(8,128)(2,1)S(1)}, u32[]{:S(2)}, u32[]{:S(2)}) collective-permute-start(bf16[256,512]{1,0:T(8,128)(2,1)} %shard_map.88.refs_0_), channel_id=1, source_target_pairs={{2,0},{4,2},{6,4},{8,6},{10,8},{12,10},{14,12},{16,14},{18,16},{20... | collective-permute-start | bytes 786440 | tf_op jit(solution)/shard_map/ppermute | solution.py:242
  32.2 0.0 collective-permute-start.2
  32.2 1.5 %collective-permute-start.1 = (bf16[256,512]{1,0:T(8,128)(2,1)}, bf16[256,512]{1,0:T(8,128)(2,1)S(1)}, u32[]{:S(2)}, u32[]{:S(2)}) collective-permute-start(bf16[256,512]{1,0:T(8,128)(2,1)} %shard_map.88.refs_0_), channel_id=1, source_target_pairs={{28,0},{30,2},{0,4},{2,6},{4,8},{6,10},{8,12},{10,14},{12,16},{14,... | collective-permute-start | bytes 786440 | tf_op jit(solution)/shard_map/ppermute | solution.py:242
  33.7 0.1 collective-permute-start
  33.8 0.6 pad_add_fusion.me_ref
  34.5 4.8 %collective-permute-done.4.refs_5_ = bf16[256,512]{1,0:T(8,128)(2,1)S(1)} collective-permute-done((bf16[256,512]{1,0:T(8,128)(2,1)}, bf16[256,512]{1,0:T(8,128)(2,1)S(1)}, u32[]{:S(2)}, u32[]{:S(2)}) %collective-permute-start.4) | collective-permute-done | bytes 262176 | tf_op jit(solution)/shard_map/ppermute | solution.py:242
  39.3 4.2 %collective-permute-done.3.refs_4_ = bf16[256,512]{1,0:T(8,128)(2,1)S(1)} collective-permute-done((bf16[256,512]{1,0:T(8,128)(2,1)}, bf16[256,512]{1,0:T(8,128)(2,1)S(1)}, u32[]{:S(2)}, u32[]{:S(2)}) %collective-permute-start.3) | collective-permute-done | bytes 262176 | tf_op jit(solution)/shard_map/ppermute | solution.py:242
  43.5 6.5 %collective-permute-done.2.refs_3_ = bf16[256,512]{1,0:T(8,128)(2,1)S(1)} collective-permute-done((bf16[256,512]{1,0:T(8,128)(2,1)}, bf16[256,512]{1,0:T(8,128)(2,1)S(1)}, u32[]{:S(2)}, u32[]{:S(2)}) %collective-permute-start.2) | collective-permute-done | bytes 262176 | tf_op jit(solution)/shard_map/ppermute | solution.py:242
  49.9 0.0 collective-permute-done.1.refs_2_
  50.0 4.7 %collective-permute-done.refs_1_ = bf16[256,512]{1,0:T(8,128)(2,1)S(1)} collective-permute-done((bf16[256,512]{1,0:T(8,128)(2,1)}, bf16[256,512]{1,0:T(8,128)(2,1)S(1)}, u32[]{:S(2)}, u32[]{:S(2)}) %collective-permute-start) | collective-permute-done | bytes 262176 | tf_op jit(solution)/shard_map/ppermute | solution.py:242
  54.6 0.3 all-to-all-done.1
  55.0 0.0 copy-done.8
  55.0 0.0 copy-done.9
  55.0 0.0 copy-done.10
  55.0 0.3 copy-done.12
  55.3 0.4 copy-done.1
  55.8 13.4 %shard_map.89 = (f32[256,512]{1,0:T(8,128)}, bf16[256,512]{1,0:T(8,128)(2,1)}, bf16[256,512]{1,0:T(8,128)(2,1)}, bf16[256,512]{1,0:T(8,128)(2,1)}, bf16[256,512]...) custom-call(s32[1,256]{1,0:T(1,128)} %get-tuple-element.22.pos_ref, ...), custom_call_target="tpu_custom_call" | custom-call | tf_op jit(solution)/shard_map/pallas_call | solution.py:209
  69.2 5.0 %shard_map.90 = (f32[2,256,512]{2,1,0:T(8,128)}, bf16[2,256,512]{2,1,0:T(8,128)(2,1)}, f32[2,256,512]{2,1,0:T(8,128)}, bf16[2,256,512]{2,1,0:T(8,128)(2,1)}, bf16[512,512]{1,0:T(8,128)(2,1)}) custom-call(s32[2]{0:T(128)} %pad_add_fusion.me_ref, s32[1,256]{1,0:T(1,128)} %get-tuple-element.22.pos_ref, bf16[256,512]{1,0:T(8,128)(2,1)} %get-tuple-element.23.vec_ref, ...), custom_call_target="tpu_custom_call" | custom-call | tf_op jit(solution)/shard_map/pallas_call | solution.py:209
  74.2 1.3 collective-permute-start.11
  75.5 1.5 %collective-permute-start.13 = (bf16[2,256,512]{2,1,0:T(8,128)(2,1)}, bf16[2,256,512]{2,1,0:T(8,128)(2,1)S(1)}, u32[]{:S(2)}, u32[]{:S(2)}) collective-permute-start(bf16[2,256,512]{2,1,0:T(8,128)(2,1)} %get-tuple-element.39), channel_id=1, source_target_pairs={{0,4},{2,6},{4,0},{6,2},{8,12},{10,14},{12,8},{14,10},{16,20},{18,... | collective-permute-start | bytes 1572872 | tf_op jit(solution)/shard_map/ppermute | solution.py:245
  77.0 5.5 %all-to-all-start.2 = ((bf16[16,32,512]{2,1,0:T(8,128)(2,1)}), bf16[16,32,512]{2,1,0:T(8,128)(2,1)S(1)}, u32[]{:S(2)}, u32[]{:S(2)}) async-start(bf16[16,32,512]{2,1,0:T(8,128)(2,1)} %bitcast.23), calls=%async_computation.2 | async-start | bytes 1048576 | tf_op jit(solution)/shard_map/all_to_all | solution.py:274
  82.5 7.3 %collective-permute-done.11 = bf16[2,256,512]{2,1,0:T(8,128)(2,1)S(1)} collective-permute-done((bf16[2,256,512]{2,1,0:T(8,128)(2,1)}, bf16[2,256,512]{2,1,0:T(8,128)(2,1)S(1)}, u32[]{:S(2)}, u32[]{:S(2)}) %collective-permute-start.11) | collective-permute-done | bytes 524320 | tf_op jit(solution)/shard_map/ppermute | solution.py:245
  89.8 1.4 convert_add_fusion.1
  91.3 3.2 %collective-permute-start.12 = (bf16[2,128,512]{2,1,0:T(8,128)(2,1)S(1)}, bf16[2,128,512]{2,1,0:T(8,128)(2,1)S(1)}, u32[]{:S(2)}, u32[]{:S(2)}) collective-permute-start(bf16[2,128,512]{2,1,0:T(8,128)(2,1)S(1)} %slice.31), channel_id=1, source_target_pairs={{0,4},{2,6},{4,0},{6,2},{8,12},{10,14},{12,8},{14,10},{16,20},{18,... | collective-permute-start | bytes 786440 | tf_op jit(solution)/shard_map/ppermute | solution.py:245
  94.4 0.0 collective-permute-done.13
  94.4 0.2 convert_add_fusion
  94.7 2.4 %collective-permute-start.14 = (bf16[2,128,512]{2,1,0:T(8,128)(2,1)S(1)}, bf16[2,128,512]{2,1,0:T(8,128)(2,1)S(1)}, u32[]{:S(2)}, u32[]{:S(2)}) collective-permute-start(bf16[2,128,512]{2,1,0:T(8,128)(2,1)S(1)} %slice.30), channel_id=1, source_target_pairs={{0,2},{2,0},{4,6},{6,4},{8,10},{10,8},{12,14},{14,12},{16,18},{18,... | collective-permute-start | bytes 786440 | tf_op jit(solution)/shard_map/ppermute | solution.py:245
  97.1 3.2 %collective-permute-done.12 = bf16[2,128,512]{2,1,0:T(8,128)(2,1)S(1)} collective-permute-done((bf16[2,128,512]{2,1,0:T(8,128)(2,1)S(1)}, bf16[2,128,512]{2,1,0:T(8,128)(2,1)S(1)}, u32[]{:S(2)}, u32[]{:S(2)}) %collective-permute-start.12) | collective-permute-done | bytes 262176 | tf_op jit(solution)/shard_map/ppermute | solution.py:245
  100.3 0.1 fusion.1
  100.3 1.1 collective-permute-done.14
  101.5 0.1 fusion
  101.5 0.8 copy_bitcast_fusion
  102.4 0.0 all-to-all-done.2
  102.4 3.5 %all-to-all-start.3 = ((bf16[4,4,32,512]{3,2,1,0:T(8,128)(2,1)}), bf16[4,4,32,512]{3,2,1,0:T(8,128)(2,1)S(1)}, u32[]{:S(2)}, u32[]{:S(2)}) async-start(bf16[4,4,32,512]{3,2,1,0:T(8,128)(2,1)} %copy_bitcast_fusion), calls=%async_computation.3 | async-start | bytes 1048576 | tf_op jit(solution)/shard_map/all_to_all | solution.py:289
  105.9 4.7 %collective-permute-start.5 = (bf16[256,512]{1,0:T(8,128)(2,1)}, bf16[256,512]{1,0:T(8,128)(2,1)S(1)}, u32[]{:S(2)}, u32[]{:S(2)}) collective-permute-start(bf16[256,512]{1,0:T(8,128)(2,1)} %get-tuple-element.29), channel_id=1, source_target_pairs={{2,0},{4,2},{6,4},{8,6},{10,8},{12,10},{14,12},{16,14},{18,16},{20... | collective-permute-start | bytes 786440 | tf_op jit(solution)/shard_map/ppermute | solution.py:242
  110.7 0.0 copy-done.17
  110.7 2.0 %collective-permute-start.6 = (bf16[256,512]{1,0:T(8,128)(2,1)S(1)}, bf16[256,512]{1,0:T(8,128)(2,1)S(1)}, u32[]{:S(2)}, u32[]{:S(2)}) collective-permute-start(bf16[256,512]{1,0:T(8,128)(2,1)S(1)} %copy-done.17), channel_id=1, source_target_pairs={{4,0},{6,2},{8,4},{10,6},{12,8},{14,10},{16,12},{18,14},{20,16},{2... | collective-permute-start | bytes 786440 | tf_op jit(solution)/shard_map/ppermute | solution.py:242
  112.7 0.3 collective-permute-start.7
  113.0 0.0 copy-done.15
  113.0 1.3 collective-permute-start.8
  114.2 2.0 %collective-permute-start.9 = (bf16[256,512]{1,0:T(8,128)(2,1)S(1)}, bf16[256,512]{1,0:T(8,128)(2,1)S(1)}, u32[]{:S(2)}, u32[]{:S(2)}) collective-permute-start(bf16[256,512]{1,0:T(8,128)(2,1)S(1)} %copy-done.14), channel_id=1, source_target_pairs={{28,0},{30,2},{0,4},{2,6},{4,8},{6,10},{8,12},{10,14},{12,16},{14,... | collective-permute-start | bytes 786440 | tf_op jit(solution)/shard_map/ppermute | solution.py:242
  116.2 0.5 broadcast.3
  116.7 0.7 reduce.3
  117.4 0.7 reshape.35.wanted_ref
  118.0 3.8 %shard_map.91.base_ref = f32[512,512]{1,0:T(8,128)} custom-call(s32[4,256]{1,0:T(4,128)} %bitcast.26, bf16[4,256,512]{2,1,0:T(8,128)(2,1)} %get-tuple-element.26.q_ref, f32[4,256,1]{2,1,0:T(8,128)} %get-tuple-element.27.pw_ref), custom_call_target="tpu_custom_call" | custom-call | tf_op jit(solution)/shard_map/pallas_call | solution.py:209
  121.8 0.0 collective-permute-done.5.refs_1_
  121.8 10.8 %collective-permute-done.6.refs_2_ = bf16[256,512]{1,0:T(8,128)(2,1)S(1)} collective-permute-done((bf16[256,512]{1,0:T(8,128)(2,1)S(1)}, bf16[256,512]{1,0:T(8,128)(2,1)S(1)}, u32[]{:S(2)}, u32[]{:S(2)}) %collective-permute-start.6) | collective-permute-done | bytes 262176 | tf_op jit(solution)/shard_map/ppermute | solution.py:242
  132.7 0.0 collective-permute-done.7.refs_3_
  132.7 0.0 collective-permute-done.8.refs_4_
  132.7 1.0 collective-permute-done.9.refs_5_
  133.6 0.0 copy-done
  133.7 0.7 copy-done.7
  134.3 3.6 %shard_map.92 = (f32[512,256]{1,0:T(8,128)}, bf16[512,256]{1,0:T(8,128)(2,1)}) custom-call(s32[2]{0:T(128)} %pad_add_fusion.me_ref, s32[1,512]{1,0:T(1,128)} %reshape.35.wanted_ref, s32[1,256]{1,0:T(1,128)} %neg_ref.1, bf16[512,512]{1,0:T(8,128)(2,1)} %bitcast.19, f32[512,512]{1,0:T(8,128)} %shard_map.91.base_ref, f32[256,512]{1,0:T(8,128)} %get-tuple-element.28.refs_0_, ...), custom_call_target="tpu_custom_call" | custom-call | tf_op jit(solution)/shard_map/pallas_call | solution.py:209
  137.9 0.0 collective-permute-start.10
  137.9 1.7 %collective-permute-done.10 = bf16[512,256]{1,0:T(8,128)(2,1)S(1)} collective-permute-done((bf16[512,256]{1,0:T(8,128)(2,1)}, bf16[512,256]{1,0:T(8,128)(2,1)S(1)}, u32[]{:S(2)}, u32[]{:S(2)}) %collective-permute-start.10) | collective-permute-done | bytes 262176 | tf_op jit(solution)/shard_map/ppermute | solution.py:303
  139.6 1.9 %convert_add_fusion.2 = f32[512,256]{1,0:T(8,128)} fusion(f32[512,256]{1,0:T(8,128)} %get-tuple-element.34, bf16[512,256]{1,0:T(8,128)(2,1)S(1)} %collective-permute-done.10), kind=kLoop, calls=%fused_computation.11 | loop fusion | flops 262144 | bytes 1310720 | tf_op jit(solution)/shard_map/add | solution.py:303
  141.5 0.0 all-to-all-done.3
  141.5 0.8 convert_reduce_fusion
  (29 shorter events, 0.1 us)
Async XLA Ops:
  20.4 34.5 %all-to-all-start.1 = ((bf16[16,32,512]{2,1,0:T(8,128)(2,1)}), bf16[16,32,512]{2,1,0:T(8,128)(2,1)S(1)}, u32[]{:S(2)}, u32[]{:S(2)}) async-start(bf16[16,32,512]{2,1,0:T(8,128)(2,1)} %bitcast.18), calls=%async_computation.1 | async-start | bytes 1048576 | tf_op jit(solution)/shard_map/all_to_all | solution.py:249
  26.1 13.1 %collective-permute-start.4 = (bf16[256,512]{1,0:T(8,128)(2,1)}, bf16[256,512]{1,0:T(8,128)(2,1)S(1)}, u32[]{:S(2)}, u32[]{:S(2)}) collective-permute-start(bf16[256,512]{1,0:T(8,128)(2,1)} %shard_map.88.refs_0_), channel_id=1, source_target_pairs={{4,0},{6,2},{8,4},{10,6},{12,8},{14,10},{16,12},{18,14},{20,16},{2... | collective-permute-start | bytes 786440 | tf_op jit(solution)/shard_map/ppermute | solution.py:242
  30.7 12.7 %collective-permute-start.3 = (bf16[256,512]{1,0:T(8,128)(2,1)}, bf16[256,512]{1,0:T(8,128)(2,1)S(1)}, u32[]{:S(2)}, u32[]{:S(2)}) collective-permute-start(bf16[256,512]{1,0:T(8,128)(2,1)} %shard_map.88.refs_0_), channel_id=1, source_target_pairs={{2,0},{4,2},{6,4},{8,6},{10,8},{12,10},{14,12},{16,14},{18,16},{20... | collective-permute-start | bytes 786440 | tf_op jit(solution)/shard_map/ppermute | solution.py:242
  32.2 17.8 %collective-permute-start.2 = (bf16[256,512]{1,0:T(8,128)(2,1)}, bf16[256,512]{1,0:T(8,128)(2,1)S(1)}, u32[]{:S(2)}, u32[]{:S(2)}) collective-permute-start(bf16[256,512]{1,0:T(8,128)(2,1)} %shard_map.88.refs_0_), channel_id=1, source_target_pairs={{26,0},{28,2},{30,4},{0,6},{2,8},{4,10},{6,12},{8,14},{10,16},{12,... | collective-permute-start | bytes 786440 | tf_op jit(solution)/shard_map/ppermute | solution.py:242
  32.2 17.8 %collective-permute-start.1 = (bf16[256,512]{1,0:T(8,128)(2,1)}, bf16[256,512]{1,0:T(8,128)(2,1)S(1)}, u32[]{:S(2)}, u32[]{:S(2)}) collective-permute-start(bf16[256,512]{1,0:T(8,128)(2,1)} %shard_map.88.refs_0_), channel_id=1, source_target_pairs={{28,0},{30,2},{0,4},{2,6},{4,8},{6,10},{8,12},{10,14},{12,16},{14,... | collective-permute-start | bytes 786440 | tf_op jit(solution)/shard_map/ppermute | solution.py:242
  33.7 21.0 %collective-permute-start = (bf16[256,512]{1,0:T(8,128)(2,1)}, bf16[256,512]{1,0:T(8,128)(2,1)S(1)}, u32[]{:S(2)}, u32[]{:S(2)}) collective-permute-start(bf16[256,512]{1,0:T(8,128)(2,1)} %shard_map.88.refs_0_), channel_id=1, source_target_pairs={{30,0},{0,2},{2,4},{4,6},{6,8},{8,10},{10,12},{12,14},{14,16},{16,... | collective-permute-start | bytes 786440 | tf_op jit(solution)/shard_map/ppermute | solution.py:242
  39.3 15.7 %copy-start.8 = (bf16[256,512]{1,0:T(8,128)(2,1)}, bf16[256,512]{1,0:T(8,128)(2,1)S(1)}, u32[]{:S(2)}) copy-start(bf16[256,512]{1,0:T(8,128)(2,1)S(1)} %collective-permute-done.4.refs_5_) | copy-start | bytes 786436
  43.5 11.5 %copy-start.9 = (bf16[256,512]{1,0:T(8,128)(2,1)}, bf16[256,512]{1,0:T(8,128)(2,1)S(1)}, u32[]{:S(2)}) copy-start(bf16[256,512]{1,0:T(8,128)(2,1)S(1)} %collective-permute-done.3.refs_4_) | copy-start | bytes 786436
  49.9 5.1 %copy-start.10 = (bf16[256,512]{1,0:T(8,128)(2,1)}, bf16[256,512]{1,0:T(8,128)(2,1)S(1)}, u32[]{:S(2)}) copy-start(bf16[256,512]{1,0:T(8,128)(2,1)S(1)} %collective-permute-done.2.refs_3_) | copy-start | bytes 786436
  49.9 5.1 %copy-start.11 = (bf16[256,512]{1,0:T(8,128)(2,1)}, bf16[256,512]{1,0:T(8,128)(2,1)S(1)}, u32[]{:S(2)}) copy-start(bf16[256,512]{1,0:T(8,128)(2,1)S(1)} %collective-permute-done.1.refs_2_) | copy-start | bytes 786436
  54.6 0.7 copy-start.12
  55.0 0.8 copy-start.1
  74.2 15.6 %collective-permute-start.11 = (bf16[2,256,512]{2,1,0:T(8,128)(2,1)}, bf16[2,256,512]{2,1,0:T(8,128)(2,1)S(1)}, u32[]{:S(2)}, u32[]{:S(2)}) collective-permute-start(bf16[2,256,512]{2,1,0:T(8,128)(2,1)} %get-tuple-element.37), channel_id=1, source_target_pairs={{0,2},{2,0},{4,6},{6,4},{8,10},{10,8},{12,14},{14,12},{16,18},{18,... | collective-permute-start | bytes 1572872 | tf_op jit(solution)/shard_map/ppermute | solution.py:245
  75.5 18.9 %collective-permute-start.13 = (bf16[2,256,512]{2,1,0:T(8,128)(2,1)}, bf16[2,256,512]{2,1,0:T(8,128)(2,1)S(1)}, u32[]{:S(2)}, u32[]{:S(2)}) collective-permute-start(bf16[2,256,512]{2,1,0:T(8,128)(2,1)} %get-tuple-element.39), channel_id=1, source_target_pairs={{0,4},{2,6},{4,0},{6,2},{8,12},{10,14},{12,8},{14,10},{16,20},{18,... | collective-permute-start | bytes 1572872 | tf_op jit(solution)/shard_map/ppermute | solution.py:245
  77.0 17.4 %copy-start.2 = (f32[2,256,512]{2,1,0:T(8,128)S(1)}, f32[2,256,512]{2,1,0:T(8,128)}, u32[]{:S(2)}) copy-start(f32[2,256,512]{2,1,0:T(8,128)} %get-tuple-element.38) | copy-start | bytes 3145732
  77.0 25.4 %all-to-all-start.2 = ((bf16[16,32,512]{2,1,0:T(8,128)(2,1)}), bf16[16,32,512]{2,1,0:T(8,128)(2,1)S(1)}, u32[]{:S(2)}, u32[]{:S(2)}) async-start(bf16[16,32,512]{2,1,0:T(8,128)(2,1)} %bitcast.23), calls=%async_computation.2 | async-start | bytes 1048576 | tf_op jit(solution)/shard_map/all_to_all | solution.py:274
  91.3 9.0 %collective-permute-start.12 = (bf16[2,128,512]{2,1,0:T(8,128)(2,1)S(1)}, bf16[2,128,512]{2,1,0:T(8,128)(2,1)S(1)}, u32[]{:S(2)}, u32[]{:S(2)}) collective-permute-start(bf16[2,128,512]{2,1,0:T(8,128)(2,1)S(1)} %slice.31), channel_id=1, source_target_pairs={{0,4},{2,6},{4,0},{6,2},{8,12},{10,14},{12,8},{14,10},{16,20},{18,... | collective-permute-start | bytes 786440 | tf_op jit(solution)/shard_map/ppermute | solution.py:245
  94.7 16.0 %copy-start.17 = (bf16[256,512]{1,0:T(8,128)(2,1)S(1)}, bf16[256,512]{1,0:T(8,128)(2,1)}, u32[]{:S(2)}) copy-start(bf16[256,512]{1,0:T(8,128)(2,1)} %get-tuple-element.30) | copy-start | bytes 786436
  94.7 18.0 %copy-start.16 = (bf16[256,512]{1,0:T(8,128)(2,1)S(1)}, bf16[256,512]{1,0:T(8,128)(2,1)}, u32[]{:S(2)}) copy-start(bf16[256,512]{1,0:T(8,128)(2,1)} %get-tuple-element.31) | copy-start | bytes 786436
  94.7 18.3 %copy-start.15 = (bf16[256,512]{1,0:T(8,128)(2,1)S(1)}, bf16[256,512]{1,0:T(8,128)(2,1)}, u32[]{:S(2)}) copy-start(bf16[256,512]{1,0:T(8,128)(2,1)} %get-tuple-element.32) | copy-start | bytes 786436
  94.7 19.5 %copy-start.14 = (bf16[256,512]{1,0:T(8,128)(2,1)S(1)}, bf16[256,512]{1,0:T(8,128)(2,1)}, u32[]{:S(2)}) copy-start(bf16[256,512]{1,0:T(8,128)(2,1)} %get-tuple-element.33) | copy-start | bytes 786436
  94.7 22.0 %copy-start.13 = (s32[16,1,32]{2,1,0:T(1,128)S(1)}, s32[16,1,32]{2,1,0:T(1,128)}, u32[]{:S(2)}) copy-start(s32[16,1,32]{2,1,0:T(1,128)} %all_to_all.26) | copy-start | bytes 6148
  94.7 6.8 %collective-permute-start.14 = (bf16[2,128,512]{2,1,0:T(8,128)(2,1)S(1)}, bf16[2,128,512]{2,1,0:T(8,128)(2,1)S(1)}, u32[]{:S(2)}, u32[]{:S(2)}) collective-permute-start(bf16[2,128,512]{2,1,0:T(8,128)(2,1)S(1)} %slice.30), channel_id=1, source_target_pairs={{0,2},{2,0},{4,6},{6,4},{8,10},{10,8},{12,14},{14,12},{16,18},{18,... | collective-permute-start | bytes 786440 | tf_op jit(solution)/shard_map/ppermute | solution.py:245
  102.4 31.2 %copy-start = (bf16[16,32,512]{2,1,0:T(8,128)(2,1)}, bf16[16,32,512]{2,1,0:T(8,128)(2,1)S(1)}, u32[]{:S(2)}) copy-start(bf16[16,32,512]{2,1,0:T(8,128)(2,1)S(1)} %all-to-all-done.2) | copy-start | bytes 1572868
  102.4 39.1 %all-to-all-start.3 = ((bf16[4,4,32,512]{3,2,1,0:T(8,128)(2,1)}), bf16[4,4,32,512]{3,2,1,0:T(8,128)(2,1)S(1)}, u32[]{:S(2)}, u32[]{:S(2)}) async-start(bf16[4,4,32,512]{3,2,1,0:T(8,128)(2,1)} %copy_bitcast_fusion), calls=%async_computation.3 | async-start | bytes 1048576 | tf_op jit(solution)/shard_map/all_to_all | solution.py:289
  105.9 15.9 %collective-permute-start.5 = (bf16[256,512]{1,0:T(8,128)(2,1)}, bf16[256,512]{1,0:T(8,128)(2,1)S(1)}, u32[]{:S(2)}, u32[]{:S(2)}) collective-permute-start(bf16[256,512]{1,0:T(8,128)(2,1)} %get-tuple-element.29), channel_id=1, source_target_pairs={{2,0},{4,2},{6,4},{8,6},{10,8},{12,10},{14,12},{16,14},{18,16},{20... | collective-permute-start | bytes 786440 | tf_op jit(solution)/shard_map/ppermute | solution.py:242
  110.7 22.0 %collective-permute-start.6 = (bf16[256,512]{1,0:T(8,128)(2,1)S(1)}, bf16[256,512]{1,0:T(8,128)(2,1)S(1)}, u32[]{:S(2)}, u32[]{:S(2)}) collective-permute-start(bf16[256,512]{1,0:T(8,128)(2,1)S(1)} %copy-done.17), channel_id=1, source_target_pairs={{4,0},{6,2},{8,4},{10,6},{12,8},{14,10},{16,12},{18,14},{20,16},{2... | collective-permute-start | bytes 786440 | tf_op jit(solution)/shard_map/ppermute | solution.py:242
  112.7 20.0 %collective-permute-start.7 = (bf16[256,512]{1,0:T(8,128)(2,1)S(1)}, bf16[256,512]{1,0:T(8,128)(2,1)S(1)}, u32[]{:S(2)}, u32[]{:S(2)}) collective-permute-start(bf16[256,512]{1,0:T(8,128)(2,1)S(1)} %copy-done.16), channel_id=1, source_target_pairs={{6,0},{8,2},{10,4},{12,6},{14,8},{16,10},{18,12},{20,14},{22,16},{... | collective-permute-start | bytes 786440 | tf_op jit(solution)/shard_map/ppermute | solution.py:242
  113.0 19.7 %collective-permute-start.8 = (bf16[256,512]{1,0:T(8,128)(2,1)S(1)}, bf16[256,512]{1,0:T(8,128)(2,1)S(1)}, u32[]{:S(2)}, u32[]{:S(2)}) collective-permute-start(bf16[256,512]{1,0:T(8,128)(2,1)S(1)} %copy-done.15), channel_id=1, source_target_pairs={{30,0},{0,2},{2,4},{4,6},{6,8},{8,10},{10,12},{12,14},{14,16},{16,... | collective-permute-start | bytes 786440 | tf_op jit(solution)/shard_map/ppermute | solution.py:242
  114.2 19.4 %collective-permute-start.9 = (bf16[256,512]{1,0:T(8,128)(2,1)S(1)}, bf16[256,512]{1,0:T(8,128)(2,1)S(1)}, u32[]{:S(2)}, u32[]{:S(2)}) collective-permute-start(bf16[256,512]{1,0:T(8,128)(2,1)S(1)} %copy-done.14), channel_id=1, source_target_pairs={{28,0},{30,2},{0,4},{2,6},{4,8},{6,10},{8,12},{10,14},{12,16},{14,... | collective-permute-start | bytes 786440 | tf_op jit(solution)/shard_map/ppermute | solution.py:242
  121.8 11.8 %copy-start.3 = (bf16[256,512]{1,0:T(8,128)(2,1)}, bf16[256,512]{1,0:T(8,128)(2,1)S(1)}, u32[]{:S(2)}) copy-start(bf16[256,512]{1,0:T(8,128)(2,1)S(1)} %collective-permute-done.5.refs_1_) | copy-start | bytes 786436
  132.6 1.0 copy-start.4
  132.7 1.0 copy-start.5
  132.7 1.0 copy-start.6
  133.6 0.7 copy-start.7
  137.9 1.7 %collective-permute-start.10 = (bf16[512,256]{1,0:T(8,128)(2,1)}, bf16[512,256]{1,0:T(8,128)(2,1)S(1)}, u32[]{:S(2)}, u32[]{:S(2)}) collective-permute-start(bf16[512,256]{1,0:T(8,128)(2,1)} %get-tuple-element.35), channel_id=1, source_target_pairs={{0,1},{1,0},{2,3},{3,2},{4,5},{5,4},{6,7},{7,6},{8,9},{9,8},{10,11... | collective-permute-start | bytes 786440 | tf_op jit(solution)/shard_map/ppermute | solution.py:303

commit v2 on v1

--- a/solution.py
+++ b/solution.py
@@ -6,6 +6,7 @@
 from jax.experimental import pallas as pl
 from jax.experimental.pallas import tpu as pltpu
 from jax.sharding import PartitionSpec as P
+
 
 STOPS = 6
 FORE = STOPS // 2
@@ -230,25 +231,27 @@
     lines = shards // 4
     me = jnp.stack([lax.axis_index("blk"), lax.axis_index("rep")]).astype(jnp.int32)
 
+    def moved(value, distance):
+        return lax.ppermute(value, "blk", [((i - distance) % shards, i) for i in range(shards)])
+
+    def flipped(value, bit):
+        return lax.ppermute(value, "blk", [(i, i ^ bit) for i in range(shards)])
+
+    def dealt(value, groups=None):
+        return lax.all_to_all(
+            value, "blk", split_axis=0, concat_axis=0, tiled=True, axis_index_groups=groups
+        )
+
     owner_row = head_owner.reshape(1, heads)
     qrel, tail = query_rel.T, tail_row.T
+    (own_block,) = kernel(take_kernel, [((rows, width), BF)])(neg_row, entity)
+    blocks = [own_block] + [moved(own_block, o) for o in OFFSETS]
     asked, pos = kernel(ask_kernel, [((shards, cap), jnp.int32), ((1, heads), jnp.int32)])(
         owner_row, head_row.reshape(1, heads)
     )
-    wanted = lax.all_to_all(asked, "blk", split_axis=0, concat_axis=0, tiled=True)
-    (own_block,) = kernel(take_kernel, [((rows, width), BF)])(neg_row, entity)
-
-    def moved(value, distance):
-        return lax.ppermute(value, "blk", [((i - distance) % shards, i) for i in range(shards)])
-
-    def flipped(value, bit):
-        return lax.ppermute(value, "blk", [(i, i ^ bit) for i in range(shards)])
-
-    blocks = [own_block] + [moved(own_block, o) for o in OFFSETS]
+    wanted = dealt(asked)
     (served,) = kernel(serve_kernel, [((slots, width), BF)])(wanted, entity)
-    fetched = lax.all_to_all(
-        served.reshape(shards, cap, width), "blk", split_axis=0, concat_axis=0, tiled=True
-    ).reshape(slots, width)
+    fetched = dealt(served.reshape(shards, cap, width)).reshape(slots, width)
 
     outs = [((rows, width), F32)] + [((rows, width), BF)] * (STOPS - 1)
     outs += [((heads, width), BF), ((per, heads, width), BF), ((per, heads, 1), F32), ((rels, heads, width), BF)]
@@ -261,7 +264,7 @@
     *terms, vec, queries, pos_weight, pair = kernel(visit_kernel, outs, scratch)(
         pos, qrel, tail, fetched, relation, entity, *blocks
     )
-    back = [terms[0]] + [moved(t, -o) for t, o in zip(terms[1:], OFFSETS)]
+    back = [terms[0]] + [moved(terms[n + 1], -o) for n, o in enumerate(OFFSETS)]
 
     part = (rels // 2, width // 2, width)
     keep_a, send_a, keep_b, send_b, buckets = kernel(
@@ -270,25 +273,22 @@
         [((width, heads), F32)] * 3,
         smem=1,
     )(me, pos, vec, pair, relation)
-    got_a, got_b = flipped(send_a, 1), flipped(send_b, 2)
-    returned = lax.all_to_all(
-        buckets.reshape(shards, cap, width), "blk", split_axis=0, concat_axis=0, tiled=True
-    ).reshape(slots, width)
+    got_a = flipped(send_a, 1)
+    got_b = flipped(send_b, 2)
+    returned = dealt(buckets.reshape(shards, cap, width)).reshape(slots, width)
     (base,) = kernel(tail_kernel, [((ents, width), F32)])(tail, queries, pos_weight)
 
     quarter = width // 4
     sum_a = keep_a + got_a.astype(F32)
     sum_b = keep_b + got_b.astype(F32)
-    more_a = flipped(sum_a[:, quarter:].astype(BF), 2)
-    more_b = flipped(sum_b[:, quarter:].astype(BF), 1)
+    next_a, next_b = sum_a[:, quarter:].astype(BF), sum_b[:, quarter:].astype(BF)
+    more_a = flipped(next_a, 2)
+    more_b = flipped(next_b, 1)
     sum_a = sum_a[:, :quarter] + more_a.astype(F32)
     sum_b = sum_b[:, :quarter] + more_b.astype(F32)
     both = jnp.concatenate([sum_a, sum_b]).astype(BF).reshape(rels, lines, step, width)
     both = both.transpose(1, 0, 2, 3)
-    groups = [[c + 4 * z for z in range(lines)] for c in range(4)]
-    lined = lax.all_to_all(
-        both, "blk", split_axis=0, concat_axis=0, tiled=True, axis_index_groups=groups
-    )
+    lined = dealt(both, [[c + 4 * z for z in range(lines)] for c in range(4)])
     grad_rel = jnp.sum(lined.astype(F32), axis=0)
 
     chunk = width // reps
@@ -314,6 +314,7 @@
         P(("blk", "rep"), None),
         P("blk", "rep"),
     )
+
     return jax.shard_map(
         per_device,
         mesh=mesh,

time: 144 us -> 144 us (level)
  no operation moved by 1% of the time
where the time goes in v2:
time: 144 us; the launch traced here: 142 us
  waiting for transfers between devices  45.7 us (32%)
  starting transfers between devices  38.8 us (27%)
  Pallas kernels  32.1 us (22%)
  blocking collectives  15.7 us (11%)
  other arithmetic  6.54 us (5%)
  local copies, waits for them, and re-layouts  2.72 us (2%)
    pallas_call x7, Pallas kernels, call(): pl.pallas_call(body, out_shape=[jax.ShapeDtypeStruct(s, d) for s, d in ou...  32.1 us
    ppermute x10, waiting for transfers between devices, moved(): lax.ppermute(value, 'blk', [((i - distance) % shards, i) for i in range(s...  32 us
    ppermute x10, starting transfers between devices, moved(): lax.ppermute(value, 'blk', [((i - distance) % shards, i) for i in range(s...  17.9 us
    all_to_all x1, blocking collectives, dealt(): lax.all_to_all(value, 'blk', split_axis=0, concat_axis=0, tiled=True, axi...  15.7 us
    all_to_all x3, starting transfers between devices, dealt(): lax.all_to_all(value, 'blk', split_axis=0, concat_axis=0, tiled=True, axi...  12.6 us
    ppermute x4, waiting for transfers between devices, flipped(): return lax.ppermute(value, 'blk', [(i, i ^ bit) for i in range(shards)])  11.6 us
    ppermute x4, starting transfers between devices, flipped(): return lax.ppermute(value, 'blk', [(i, i ^ bit) for i in range(shards)])  8.36 us
  transfers between devices with their start and end apart: 18, of which 11 were waited for; matrix products, arithmetic and copies ran while one was open for 5% of the time, Pallas kernels for 7%

profile of v2, /device:TPU:0, one launch (start us, length us, event | category | flops | bytes accessed | tf_op | source)
XLA Modules:
  0.0 142.3 jit_solution(8815691997129775744)
XLA Ops:
  0.6 1.6 %shard_map.86 = (s32[16,32]{1,0:T(8,128)}, s32[1,256]{1,0:T(1,128)}) custom-call(s32[1,256]{1,0:T(1,128)} %bitcast.29, s32[1,256]{1,0:T(1,128)} %bitcast.30), custom_call_target="tpu_custom_call" | custom-call | tf_op jit(solution)/shard_map/pallas_call | solution.py:210
  2.3 15.7 %all_to_all.26 = s32[16,1,32]{2,1,0:T(1,128)} all-to-all(s32[16,1,32]{2,1,0:T(1,128)} %bitcast.27), channel_id=1, replica_groups=mesh['blk'=16,'rep'=2] {'blk'}, dimensions={0} | all-to-all | bytes 4096 | tf_op jit(solution)/shard_map/all_to_all | solution.py:241
  17.9 2.5 %shard_map.87 = bf16[512,512]{1,0:T(8,128)(2,1)} custom-call(s32[16,32]{1,0:T(8,128)} %bitcast.24, bf16[512,512]{1,0:T(8,128)(2,1)} %ent_ref.1), custom_call_target="tpu_custom_call" | custom-call | tf_op jit(solution)/shard_map/pallas_call | solution.py:210
  20.4 3.6 %all-to-all-start.1 = ((bf16[16,32,512]{2,1,0:T(8,128)(2,1)}), bf16[16,32,512]{2,1,0:T(8,128)(2,1)S(1)}, u32[]{:S(2)}, u32[]{:S(2)}) async-start(bf16[16,32,512]{2,1,0:T(8,128)(2,1)} %bitcast.18), calls=%async_computation.1 | async-start | bytes 1048576 | tf_op jit(solution)/shard_map/all_to_all | solution.py:241
  24.0 2.1 %shard_map.88.refs_0_ = bf16[256,512]{1,0:T(8,128)(2,1)} custom-call(s32[1,256]{1,0:T(1,128)} %neg_ref.1, bf16[512,512]{1,0:T(8,128)(2,1)} %ent_ref.1), custom_call_target="tpu_custom_call" | custom-call | tf_op jit(solution)/shard_map/pallas_call | solution.py:210
  26.1 4.6 %collective-permute-start.4 = (bf16[256,512]{1,0:T(8,128)(2,1)}, bf16[256,512]{1,0:T(8,128)(2,1)S(1)}, u32[]{:S(2)}, u32[]{:S(2)}) collective-permute-start(bf16[256,512]{1,0:T(8,128)(2,1)} %shard_map.88.refs_0_), channel_id=1, source_target_pairs={{4,0},{6,2},{8,4},{10,6},{12,8},{14,10},{16,12},{18,14},{20,16},{2... | collective-permute-start | bytes 786440 | tf_op jit(solution)/shard_map/ppermute | solution.py:235
  30.7 1.5 %collective-permute-start.3 = (bf16[256,512]{1,0:T(8,128)(2,1)}, bf16[256,512]{1,0:T(8,128)(2,1)S(1)}, u32[]{:S(2)}, u32[]{:S(2)}) collective-permute-start(bf16[256,512]{1,0:T(8,128)(2,1)} %shard_map.88.refs_0_), channel_id=1, source_target_pairs={{2,0},{4,2},{6,4},{8,6},{10,8},{12,10},{14,12},{16,14},{18,16},{20... | collective-permute-start | bytes 786440 | tf_op jit(solution)/shard_map/ppermute | solution.py:235
  32.2 0.0 collective-permute-start.2
  32.2 1.5 %collective-permute-start.1 = (bf16[256,512]{1,0:T(8,128)(2,1)}, bf16[256,512]{1,0:T(8,128)(2,1)S(1)}, u32[]{:S(2)}, u32[]{:S(2)}) collective-permute-start(bf16[256,512]{1,0:T(8,128)(2,1)} %shard_map.88.refs_0_), channel_id=1, source_target_pairs={{28,0},{30,2},{0,4},{2,6},{4,8},{6,10},{8,12},{10,14},{12,16},{14,... | collective-permute-start | bytes 786440 | tf_op jit(solution)/shard_map/ppermute | solution.py:235
  33.7 0.1 collective-permute-start
  33.8 0.6 pad_add_fusion.me_ref
  34.5 4.8 %collective-permute-done.4.refs_5_ = bf16[256,512]{1,0:T(8,128)(2,1)S(1)} collective-permute-done((bf16[256,512]{1,0:T(8,128)(2,1)}, bf16[256,512]{1,0:T(8,128)(2,1)S(1)}, u32[]{:S(2)}, u32[]{:S(2)}) %collective-permute-start.4) | collective-permute-done | bytes 262176 | tf_op jit(solution)/shard_map/ppermute | solution.py:235
  39.3 4.2 %collective-permute-done.3.refs_4_ = bf16[256,512]{1,0:T(8,128)(2,1)S(1)} collective-permute-done((bf16[256,512]{1,0:T(8,128)(2,1)}, bf16[256,512]{1,0:T(8,128)(2,1)S(1)}, u32[]{:S(2)}, u32[]{:S(2)}) %collective-permute-start.3) | collective-permute-done | bytes 262176 | tf_op jit(solution)/shard_map/ppermute | solution.py:235
  43.5 6.5 %collective-permute-done.2.refs_3_ = bf16[256,512]{1,0:T(8,128)(2,1)S(1)} collective-permute-done((bf16[256,512]{1,0:T(8,128)(2,1)}, bf16[256,512]{1,0:T(8,128)(2,1)S(1)}, u32[]{:S(2)}, u32[]{:S(2)}) %collective-permute-start.2) | collective-permute-done | bytes 262176 | tf_op jit(solution)/shard_map/ppermute | solution.py:235
  49.9 0.0 collective-permute-done.1.refs_2_
  50.0 4.7 %collective-permute-done.refs_1_ = bf16[256,512]{1,0:T(8,128)(2,1)S(1)} collective-permute-done((bf16[256,512]{1,0:T(8,128)(2,1)}, bf16[256,512]{1,0:T(8,128)(2,1)S(1)}, u32[]{:S(2)}, u32[]{:S(2)}) %collective-permute-start) | collective-permute-done | bytes 262176 | tf_op jit(solution)/shard_map/ppermute | solution.py:235
  54.6 0.3 all-to-all-done.1
  55.0 0.0 copy-done.8
  55.0 0.0 copy-done.9
  55.0 0.3 copy-done.12
  55.3 0.4 copy-done.1
  55.8 13.4 %shard_map.89 = (f32[256,512]{1,0:T(8,128)}, bf16[256,512]{1,0:T(8,128)(2,1)}, bf16[256,512]{1,0:T(8,128)(2,1)}, bf16[256,512]{1,0:T(8,128)(2,1)}, bf16[256,512]...) custom-call(s32[1,256]{1,0:T(1,128)} %get-tuple-element.22.pos_ref, ...), custom_call_target="tpu_custom_call" | custom-call | tf_op jit(solution)/shard_map/pallas_call | solution.py:210
  69.2 5.0 %shard_map.90 = (f32[2,256,512]{2,1,0:T(8,128)}, bf16[2,256,512]{2,1,0:T(8,128)(2,1)}, f32[2,256,512]{2,1,0:T(8,128)}, bf16[2,256,512]{2,1,0:T(8,128)(2,1)}, bf16[512,512]{1,0:T(8,128)(2,1)}) custom-call(s32[2]{0:T(128)} %pad_add_fusion.me_ref, s32[1,256]{1,0:T(1,128)} %get-tuple-element.22.pos_ref, bf16[256,512]{1,0:T(8,128)(2,1)} %get-tuple-element.23.vec_ref, ...), custom_call_target="tpu_custom_call" | custom-call | tf_op jit(solution)/shard_map/pallas_call | solution.py:210
  74.2 1.3 collective-permute-start.11
  75.5 1.5 %collective-permute-start.13 = (bf16[2,256,512]{2,1,0:T(8,128)(2,1)}, bf16[2,256,512]{2,1,0:T(8,128)(2,1)S(1)}, u32[]{:S(2)}, u32[]{:S(2)}) collective-permute-start(bf16[2,256,512]{2,1,0:T(8,128)(2,1)} %get-tuple-element.39), channel_id=1, source_target_pairs={{0,4},{2,6},{4,0},{6,2},{8,12},{10,14},{12,8},{14,10},{16,20},{18,... | collective-permute-start | bytes 1572872 | tf_op jit(solution)/shard_map/ppermute | solution.py:238
  77.0 5.5 %all-to-all-start.2 = ((bf16[16,32,512]{2,1,0:T(8,128)(2,1)}), bf16[16,32,512]{2,1,0:T(8,128)(2,1)S(1)}, u32[]{:S(2)}, u32[]{:S(2)}) async-start(bf16[16,32,512]{2,1,0:T(8,128)(2,1)} %bitcast.23), calls=%async_computation.2 | async-start | bytes 1048576 | tf_op jit(solution)/shard_map/all_to_all | solution.py:241
  82.5 7.3 %collective-permute-done.11 = bf16[2,256,512]{2,1,0:T(8,128)(2,1)S(1)} collective-permute-done((bf16[2,256,512]{2,1,0:T(8,128)(2,1)}, bf16[2,256,512]{2,1,0:T(8,128)(2,1)S(1)}, u32[]{:S(2)}, u32[]{:S(2)}) %collective-permute-start.11) | collective-permute-done | bytes 524320 | tf_op jit(solution)/shard_map/ppermute | solution.py:238
  89.8 1.4 convert_add_fusion.1
  91.3 3.2 %collective-permute-start.12 = (bf16[2,128,512]{2,1,0:T(8,128)(2,1)S(1)}, bf16[2,128,512]{2,1,0:T(8,128)(2,1)S(1)}, u32[]{:S(2)}, u32[]{:S(2)}) collective-permute-start(bf16[2,128,512]{2,1,0:T(8,128)(2,1)S(1)} %slice.31), channel_id=1, source_target_pairs={{0,4},{2,6},{4,0},{6,2},{8,12},{10,14},{12,8},{14,10},{16,20},{18,... | collective-permute-start | bytes 786440 | tf_op jit(solution)/shard_map/ppermute | solution.py:238
  94.4 0.0 collective-permute-done.13
  94.4 0.2 convert_add_fusion
  94.7 2.4 %collective-permute-start.14 = (bf16[2,128,512]{2,1,0:T(8,128)(2,1)S(1)}, bf16[2,128,512]{2,1,0:T(8,128)(2,1)S(1)}, u32[]{:S(2)}, u32[]{:S(2)}) collective-permute-start(bf16[2,128,512]{2,1,0:T(8,128)(2,1)S(1)} %slice.30), channel_id=1, source_target_pairs={{0,2},{2,0},{4,6},{6,4},{8,10},{10,8},{12,14},{14,12},{16,18},{18,... | collective-permute-start | bytes 786440 | tf_op jit(solution)/shard_map/ppermute | solution.py:238
  97.1 3.2 %collective-permute-done.12 = bf16[2,128,512]{2,1,0:T(8,128)(2,1)S(1)} collective-permute-done((bf16[2,128,512]{2,1,0:T(8,128)(2,1)S(1)}, bf16[2,128,512]{2,1,0:T(8,128)(2,1)S(1)}, u32[]{:S(2)}, u32[]{:S(2)}) %collective-permute-start.12) | collective-permute-done | bytes 262176 | tf_op jit(solution)/shard_map/ppermute | solution.py:238
  100.3 0.1 fusion.1
  100.3 1.1 collective-permute-done.14
  101.5 0.1 fusion
  101.5 0.8 copy_bitcast_fusion
  102.4 0.0 all-to-all-done.2
  102.4 3.5 %all-to-all-start.3 = ((bf16[4,4,32,512]{3,2,1,0:T(8,128)(2,1)}), bf16[4,4,32,512]{3,2,1,0:T(8,128)(2,1)S(1)}, u32[]{:S(2)}, u32[]{:S(2)}) async-start(bf16[4,4,32,512]{3,2,1,0:T(8,128)(2,1)} %copy_bitcast_fusion), calls=%async_computation.3 | async-start | bytes 1048576 | tf_op jit(solution)/shard_map/all_to_all | solution.py:241
  105.9 4.7 %collective-permute-start.5 = (bf16[256,512]{1,0:T(8,128)(2,1)}, bf16[256,512]{1,0:T(8,128)(2,1)S(1)}, u32[]{:S(2)}, u32[]{:S(2)}) collective-permute-start(bf16[256,512]{1,0:T(8,128)(2,1)} %get-tuple-element.29), channel_id=1, source_target_pairs={{2,0},{4,2},{6,4},{8,6},{10,8},{12,10},{14,12},{16,14},{18,16},{20... | collective-permute-start | bytes 786440 | tf_op jit(solution)/shard_map/ppermute | solution.py:235
  110.7 2.0 %collective-permute-start.6 = (bf16[256,512]{1,0:T(8,128)(2,1)S(1)}, bf16[256,512]{1,0:T(8,128)(2,1)S(1)}, u32[]{:S(2)}, u32[]{:S(2)}) collective-permute-start(bf16[256,512]{1,0:T(8,128)(2,1)S(1)} %copy-done.17), channel_id=1, source_target_pairs={{4,0},{6,2},{8,4},{10,6},{12,8},{14,10},{16,12},{18,14},{20,16},{2... | collective-permute-start | bytes 786440 | tf_op jit(solution)/shard_map/ppermute | solution.py:235
  112.7 0.0 copy-done.16
  112.7 0.3 collective-permute-start.7
  113.0 1.3 collective-permute-start.8
  114.2 2.0 %collective-permute-start.9 = (bf16[256,512]{1,0:T(8,128)(2,1)S(1)}, bf16[256,512]{1,0:T(8,128)(2,1)S(1)}, u32[]{:S(2)}, u32[]{:S(2)}) collective-permute-start(bf16[256,512]{1,0:T(8,128)(2,1)S(1)} %copy-done.14), channel_id=1, source_target_pairs={{28,0},{30,2},{0,4},{2,6},{4,8},{6,10},{8,12},{10,14},{12,16},{14,... | collective-permute-start | bytes 786440 | tf_op jit(solution)/shard_map/ppermute | solution.py:235
  116.2 0.5 broadcast.3
  116.7 0.7 reduce.3
  117.4 0.7 reshape.35.wanted_ref
  118.0 3.8 %shard_map.91.base_ref = f32[512,512]{1,0:T(8,128)} custom-call(s32[4,256]{1,0:T(4,128)} %bitcast.26, bf16[4,256,512]{2,1,0:T(8,128)(2,1)} %get-tuple-element.26.q_ref, f32[4,256,1]{2,1,0:T(8,128)} %get-tuple-element.27.pw_ref), custom_call_target="tpu_custom_call" | custom-call | tf_op jit(solution)/shard_map/pallas_call | solution.py:210
  121.8 0.0 collective-permute-done.5.refs_1_
  121.8 10.8 %collective-permute-done.6.refs_2_ = bf16[256,512]{1,0:T(8,128)(2,1)S(1)} collective-permute-done((bf16[256,512]{1,0:T(8,128)(2,1)S(1)}, bf16[256,512]{1,0:T(8,128)(2,1)S(1)}, u32[]{:S(2)}, u32[]{:S(2)}) %collective-permute-start.6) | collective-permute-done | bytes 262176 | tf_op jit(solution)/shard_map/ppermute | solution.py:235
  132.7 0.0 collective-permute-done.7.refs_3_
  132.7 0.0 collective-permute-done.8.refs_4_
  132.7 0.0 copy-start.6
  132.7 1.0 collective-permute-done.9.refs_5_
  133.6 0.0 copy-done
  133.6 0.0 copy-done.4
  133.7 0.7 copy-done.7
  134.3 3.6 %shard_map.92 = (f32[512,256]{1,0:T(8,128)}, bf16[512,256]{1,0:T(8,128)(2,1)}) custom-call(s32[2]{0:T(128)} %pad_add_fusion.me_ref, s32[1,512]{1,0:T(1,128)} %reshape.35.wanted_ref, s32[1,256]{1,0:T(1,128)} %neg_ref.1, bf16[512,512]{1,0:T(8,128)(2,1)} %bitcast.19, f32[512,512]{1,0:T(8,128)} %shard_map.91.base_ref, f32[256,512]{1,0:T(8,128)} %get-tuple-element.28.refs_0_, ...), custom_call_target="tpu_custom_call" | custom-call | tf_op jit(solution)/shard_map/pallas_call | solution.py:210
  137.9 0.0 collective-permute-start.10
  137.9 1.7 %collective-permute-done.10 = bf16[512,256]{1,0:T(8,128)(2,1)S(1)} collective-permute-done((bf16[512,256]{1,0:T(8,128)(2,1)}, bf16[512,256]{1,0:T(8,128)(2,1)S(1)}, u32[]{:S(2)}, u32[]{:S(2)}) %collective-permute-start.10) | collective-permute-done | bytes 262176 | tf_op jit(solution)/shard_map/ppermute | solution.py:303
  139.6 1.9 %convert_add_fusion.2 = f32[512,256]{1,0:T(8,128)} fusion(f32[512,256]{1,0:T(8,128)} %get-tuple-element.34, bf16[512,256]{1,0:T(8,128)(2,1)S(1)} %collective-permute-done.10), kind=kLoop, calls=%fused_computation.11 | loop fusion | flops 262144 | bytes 1310720 | tf_op jit(solution)/shard_map/add | solution.py:303
  141.5 0.0 all-to-all-done.3
  141.5 0.8 convert_reduce_fusion
  (29 shorter events, 0.1 us)
Async XLA Ops:
  20.4 34.5 %all-to-all-start.1 = ((bf16[16,32,512]{2,1,0:T(8,128)(2,1)}), bf16[16,32,512]{2,1,0:T(8,128)(2,1)S(1)}, u32[]{:S(2)}, u32[]{:S(2)}) async-start(bf16[16,32,512]{2,1,0:T(8,128)(2,1)} %bitcast.18), calls=%async_computation.1 | async-start | bytes 1048576 | tf_op jit(solution)/shard_map/all_to_all | solution.py:241
  26.1 13.1 %collective-permute-start.4 = (bf16[256,512]{1,0:T(8,128)(2,1)}, bf16[256,512]{1,0:T(8,128)(2,1)S(1)}, u32[]{:S(2)}, u32[]{:S(2)}) collective-permute-start(bf16[256,512]{1,0:T(8,128)(2,1)} %shard_map.88.refs_0_), channel_id=1, source_target_pairs={{4,0},{6,2},{8,4},{10,6},{12,8},{14,10},{16,12},{18,14},{20,16},{2... | collective-permute-start | bytes 786440 | tf_op jit(solution)/shard_map/ppermute | solution.py:235
  30.7 12.7 %collective-permute-start.3 = (bf16[256,512]{1,0:T(8,128)(2,1)}, bf16[256,512]{1,0:T(8,128)(2,1)S(1)}, u32[]{:S(2)}, u32[]{:S(2)}) collective-permute-start(bf16[256,512]{1,0:T(8,128)(2,1)} %shard_map.88.refs_0_), channel_id=1, source_target_pairs={{2,0},{4,2},{6,4},{8,6},{10,8},{12,10},{14,12},{16,14},{18,16},{20... | collective-permute-start | bytes 786440 | tf_op jit(solution)/shard_map/ppermute | solution.py:235
  32.2 17.8 %collective-permute-start.2 = (bf16[256,512]{1,0:T(8,128)(2,1)}, bf16[256,512]{1,0:T(8,128)(2,1)S(1)}, u32[]{:S(2)}, u32[]{:S(2)}) collective-permute-start(bf16[256,512]{1,0:T(8,128)(2,1)} %shard_map.88.refs_0_), channel_id=1, source_target_pairs={{26,0},{28,2},{30,4},{0,6},{2,8},{4,10},{6,12},{8,14},{10,16},{12,... | collective-permute-start | bytes 786440 | tf_op jit(solution)/shard_map/ppermute | solution.py:235
  32.2 17.8 %collective-permute-start.1 = (bf16[256,512]{1,0:T(8,128)(2,1)}, bf16[256,512]{1,0:T(8,128)(2,1)S(1)}, u32[]{:S(2)}, u32[]{:S(2)}) collective-permute-start(bf16[256,512]{1,0:T(8,128)(2,1)} %shard_map.88.refs_0_), channel_id=1, source_target_pairs={{28,0},{30,2},{0,4},{2,6},{4,8},{6,10},{8,12},{10,14},{12,16},{14,... | collective-permute-start | bytes 786440 | tf_op jit(solution)/shard_map/ppermute | solution.py:235
  33.7 21.0 %collective-permute-start = (bf16[256,512]{1,0:T(8,128)(2,1)}, bf16[256,512]{1,0:T(8,128)(2,1)S(1)}, u32[]{:S(2)}, u32[]{:S(2)}) collective-permute-start(bf16[256,512]{1,0:T(8,128)(2,1)} %shard_map.88.refs_0_), channel_id=1, source_target_pairs={{30,0},{0,2},{2,4},{4,6},{6,8},{8,10},{10,12},{12,14},{14,16},{16,... | collective-permute-start | bytes 786440 | tf_op jit(solution)/shard_map/ppermute | solution.py:235
  39.3 15.7 %copy-start.8 = (bf16[256,512]{1,0:T(8,128)(2,1)}, bf16[256,512]{1,0:T(8,128)(2,1)S(1)}, u32[]{:S(2)}) copy-start(bf16[256,512]{1,0:T(8,128)(2,1)S(1)} %collective-permute-done.4.refs_5_) | copy-start | bytes 786436
  43.5 11.5 %copy-start.9 = (bf16[256,512]{1,0:T(8,128)(2,1)}, bf16[256,512]{1,0:T(8,128)(2,1)S(1)}, u32[]{:S(2)}) copy-start(bf16[256,512]{1,0:T(8,128)(2,1)S(1)} %collective-permute-done.3.refs_4_) | copy-start | bytes 786436
  49.9 5.1 %copy-start.10 = (bf16[256,512]{1,0:T(8,128)(2,1)}, bf16[256,512]{1,0:T(8,128)(2,1)S(1)}, u32[]{:S(2)}) copy-start(bf16[256,512]{1,0:T(8,128)(2,1)S(1)} %collective-permute-done.2.refs_3_) | copy-start | bytes 786436
  49.9 5.1 %copy-start.11 = (bf16[256,512]{1,0:T(8,128)(2,1)}, bf16[256,512]{1,0:T(8,128)(2,1)S(1)}, u32[]{:S(2)}) copy-start(bf16[256,512]{1,0:T(8,128)(2,1)S(1)} %collective-permute-done.1.refs_2_) | copy-start | bytes 786436
  54.6 0.7 copy-start.12
  55.0 0.8 copy-start.1
  74.2 15.6 %collective-permute-start.11 = (bf16[2,256,512]{2,1,0:T(8,128)(2,1)}, bf16[2,256,512]{2,1,0:T(8,128)(2,1)S(1)}, u32[]{:S(2)}, u32[]{:S(2)}) collective-permute-start(bf16[2,256,512]{2,1,0:T(8,128)(2,1)} %get-tuple-element.37), channel_id=1, source_target_pairs={{0,2},{2,0},{4,6},{6,4},{8,10},{10,8},{12,14},{14,12},{16,18},{18,... | collective-permute-start | bytes 1572872 | tf_op jit(solution)/shard_map/ppermute | solution.py:238
  75.5 18.9 %collective-permute-start.13 = (bf16[2,256,512]{2,1,0:T(8,128)(2,1)}, bf16[2,256,512]{2,1,0:T(8,128)(2,1)S(1)}, u32[]{:S(2)}, u32[]{:S(2)}) collective-permute-start(bf16[2,256,512]{2,1,0:T(8,128)(2,1)} %get-tuple-element.39), channel_id=1, source_target_pairs={{0,4},{2,6},{4,0},{6,2},{8,12},{10,14},{12,8},{14,10},{16,20},{18,... | collective-permute-start | bytes 1572872 | tf_op jit(solution)/shard_map/ppermute | solution.py:238
  77.0 17.4 %copy-start.2 = (f32[2,256,512]{2,1,0:T(8,128)S(1)}, f32[2,256,512]{2,1,0:T(8,128)}, u32[]{:S(2)}) copy-start(f32[2,256,512]{2,1,0:T(8,128)} %get-tuple-element.38) | copy-start | bytes 3145732
  77.0 25.4 %all-to-all-start.2 = ((bf16[16,32,512]{2,1,0:T(8,128)(2,1)}), bf16[16,32,512]{2,1,0:T(8,128)(2,1)S(1)}, u32[]{:S(2)}, u32[]{:S(2)}) async-start(bf16[16,32,512]{2,1,0:T(8,128)(2,1)} %bitcast.23), calls=%async_computation.2 | async-start | bytes 1048576 | tf_op jit(solution)/shard_map/all_to_all | solution.py:241
  91.3 9.0 %collective-permute-start.12 = (bf16[2,128,512]{2,1,0:T(8,128)(2,1)S(1)}, bf16[2,128,512]{2,1,0:T(8,128)(2,1)S(1)}, u32[]{:S(2)}, u32[]{:S(2)}) collective-permute-start(bf16[2,128,512]{2,1,0:T(8,128)(2,1)S(1)} %slice.31), channel_id=1, source_target_pairs={{0,4},{2,6},{4,0},{6,2},{8,12},{10,14},{12,8},{14,10},{16,20},{18,... | collective-permute-start | bytes 786440 | tf_op jit(solution)/shard_map/ppermute | solution.py:238
  94.7 16.0 %copy-start.17 = (bf16[256,512]{1,0:T(8,128)(2,1)S(1)}, bf16[256,512]{1,0:T(8,128)(2,1)}, u32[]{:S(2)}) copy-start(bf16[256,512]{1,0:T(8,128)(2,1)} %get-tuple-element.30) | copy-start | bytes 786436
  94.7 18.0 %copy-start.16 = (bf16[256,512]{1,0:T(8,128)(2,1)S(1)}, bf16[256,512]{1,0:T(8,128)(2,1)}, u32[]{:S(2)}) copy-start(bf16[256,512]{1,0:T(8,128)(2,1)} %get-tuple-element.31) | copy-start | bytes 786436
  94.7 18.3 %copy-start.15 = (bf16[256,512]{1,0:T(8,128)(2,1)S(1)}, bf16[256,512]{1,0:T(8,128)(2,1)}, u32[]{:S(2)}) copy-start(bf16[256,512]{1,0:T(8,128)(2,1)} %get-tuple-element.32) | copy-start | bytes 786436
  94.7 19.5 %copy-start.14 = (bf16[256,512]{1,0:T(8,128)(2,1)S(1)}, bf16[256,512]{1,0:T(8,128)(2,1)}, u32[]{:S(2)}) copy-start(bf16[256,512]{1,0:T(8,128)(2,1)} %get-tuple-element.33) | copy-start | bytes 786436
  94.7 22.0 %copy-start.13 = (s32[16,1,32]{2,1,0:T(1,128)S(1)}, s32[16,1,32]{2,1,0:T(1,128)}, u32[]{:S(2)}) copy-start(s32[16,1,32]{2,1,0:T(1,128)} %all_to_all.26) | copy-start | bytes 6148
  94.7 6.8 %collective-permute-start.14 = (bf16[2,128,512]{2,1,0:T(8,128)(2,1)S(1)}, bf16[2,128,512]{2,1,0:T(8,128)(2,1)S(1)}, u32[]{:S(2)}, u32[]{:S(2)}) collective-permute-start(bf16[2,128,512]{2,1,0:T(8,128)(2,1)S(1)} %slice.30), channel_id=1, source_target_pairs={{0,2},{2,0},{4,6},{6,4},{8,10},{10,8},{12,14},{14,12},{16,18},{18,... | collective-permute-start | bytes 786440 | tf_op jit(solution)/shard_map/ppermute | solution.py:238
  102.4 31.2 %copy-start = (bf16[16,32,512]{2,1,0:T(8,128)(2,1)}, bf16[16,32,512]{2,1,0:T(8,128)(2,1)S(1)}, u32[]{:S(2)}) copy-start(bf16[16,32,512]{2,1,0:T(8,128)(2,1)S(1)} %all-to-all-done.2) | copy-start | bytes 1572868
  102.4 39.1 %all-to-all-start.3 = ((bf16[4,4,32,512]{3,2,1,0:T(8,128)(2,1)}), bf16[4,4,32,512]{3,2,1,0:T(8,128)(2,1)S(1)}, u32[]{:S(2)}, u32[]{:S(2)}) async-start(bf16[4,4,32,512]{3,2,1,0:T(8,128)(2,1)} %copy_bitcast_fusion), calls=%async_computation.3 | async-start | bytes 1048576 | tf_op jit(solution)/shard_map/all_to_all | solution.py:241
  105.9 15.9 %collective-permute-start.5 = (bf16[256,512]{1,0:T(8,128)(2,1)}, bf16[256,512]{1,0:T(8,128)(2,1)S(1)}, u32[]{:S(2)}, u32[]{:S(2)}) collective-permute-start(bf16[256,512]{1,0:T(8,128)(2,1)} %get-tuple-element.29), channel_id=1, source_target_pairs={{2,0},{4,2},{6,4},{8,6},{10,8},{12,10},{14,12},{16,14},{18,16},{20... | collective-permute-start | bytes 786440 | tf_op jit(solution)/shard_map/ppermute | solution.py:235
  110.7 22.0 %collective-permute-start.6 = (bf16[256,512]{1,0:T(8,128)(2,1)S(1)}, bf16[256,512]{1,0:T(8,128)(2,1)S(1)}, u32[]{:S(2)}, u32[]{:S(2)}) collective-permute-start(bf16[256,512]{1,0:T(8,128)(2,1)S(1)} %copy-done.17), channel_id=1, source_target_pairs={{4,0},{6,2},{8,4},{10,6},{12,8},{14,10},{16,12},{18,14},{20,16},{2... | collective-permute-start | bytes 786440 | tf_op jit(solution)/shard_map/ppermute | solution.py:235
  112.7 20.0 %collective-permute-start.7 = (bf16[256,512]{1,0:T(8,128)(2,1)S(1)}, bf16[256,512]{1,0:T(8,128)(2,1)S(1)}, u32[]{:S(2)}, u32[]{:S(2)}) collective-permute-start(bf16[256,512]{1,0:T(8,128)(2,1)S(1)} %copy-done.16), channel_id=1, source_target_pairs={{6,0},{8,2},{10,4},{12,6},{14,8},{16,10},{18,12},{20,14},{22,16},{... | collective-permute-start | bytes 786440 | tf_op jit(solution)/shard_map/ppermute | solution.py:235
  113.0 19.7 %collective-permute-start.8 = (bf16[256,512]{1,0:T(8,128)(2,1)S(1)}, bf16[256,512]{1,0:T(8,128)(2,1)S(1)}, u32[]{:S(2)}, u32[]{:S(2)}) collective-permute-start(bf16[256,512]{1,0:T(8,128)(2,1)S(1)} %copy-done.15), channel_id=1, source_target_pairs={{30,0},{0,2},{2,4},{4,6},{6,8},{8,10},{10,12},{12,14},{14,16},{16,... | collective-permute-start | bytes 786440 | tf_op jit(solution)/shard_map/ppermute | solution.py:235
  114.2 19.4 %collective-permute-start.9 = (bf16[256,512]{1,0:T(8,128)(2,1)S(1)}, bf16[256,512]{1,0:T(8,128)(2,1)S(1)}, u32[]{:S(2)}, u32[]{:S(2)}) collective-permute-start(bf16[256,512]{1,0:T(8,128)(2,1)S(1)} %copy-done.14), channel_id=1, source_target_pairs={{28,0},{30,2},{0,4},{2,6},{4,8},{6,10},{8,12},{10,14},{12,16},{14,... | collective-permute-start | bytes 786440 | tf_op jit(solution)/shard_map/ppermute | solution.py:235
  121.8 11.8 %copy-start.3 = (bf16[256,512]{1,0:T(8,128)(2,1)}, bf16[256,512]{1,0:T(8,128)(2,1)S(1)}, u32[]{:S(2)}) copy-start(bf16[256,512]{1,0:T(8,128)(2,1)S(1)} %collective-permute-done.5.refs_1_) | copy-start | bytes 786436
  132.6 1.0 copy-start.4
  132.7 1.0 copy-start.5
  132.7 1.0 copy-start.6
  133.6 0.7 copy-start.7
  137.9 1.7 %collective-permute-start.10 = (bf16[512,256]{1,0:T(8,128)(2,1)}, bf16[512,256]{1,0:T(8,128)(2,1)S(1)}, u32[]{:S(2)}, u32[]{:S(2)}) collective-permute-start(bf16[512,256]{1,0:T(8,128)(2,1)} %get-tuple-element.35), channel_id=1, source_target_pairs={{0,1},{1,0},{2,3},{3,2},{4,5},{5,4},{6,7},{7,6},{8,9},{9,8},{10,11... | collective-permute-start | bytes 786440 | tf_op jit(solution)/shard_map/ppermute | solution.py:303

commit v3 on v2

--- a/solution.py
+++ b/solution.py
@@ -12,6 +12,7 @@
 FORE = STOPS // 2
 BACK = STOPS - 1 - FORE
 OFFSETS = tuple(range(1, FORE + 1)) + tuple(range(-1, -BACK - 1, -1))
+VMEM = 24 << 20
 BF = jnp.bfloat16
 F32 = jnp.float32
 
@@ -83,95 +84,96 @@
     out_ref[...] = dot(pick, entity_ref[...]).astype(BF)
 
 
-def visit_kernel(pos_ref, qrel_ref, tail_ref, fetched_ref, rel_ref, ent_ref, *refs):
-    blocks = refs[:STOPS]
-    terms = refs[STOPS : 2 * STOPS]
-    vec_ref, q_ref, pw_ref, pair_ref, prod, near, weight, gq = refs[2 * STOPS :]
-    heads, width = vec_ref.shape
+def query_kernel(pos_ref, qrel_ref, fetched_ref, rel_ref, vec_ref, q_ref, prod):
+    heads = vec_ref.shape[0]
     rels = rel_ref.shape[0]
-    per = qrel_ref.shape[0]
     slots = fetched_ref.shape[0]
-    rows = blocks[0].shape[0]
-    ents = ent_ref.shape[0]
-    for index, block in enumerate(blocks):
-        near[index * rows : (index + 1) * rows, :] = block[...]
     vec = dot(hot(column(pos_ref[...]), (heads, slots), 1), fetched_ref[...]).astype(BF)
     vec_ref[...] = vec
-
-    @pl.loop(0, rels)
-    def _(k):
-        prod[k] = dot(vec_ref[...], rel_ref[k])
-
-    @pl.loop(0, per)
-    def _(j):
-        kind = column(qrel_ref[pl.ds(j, 1), :])
+    for k in range(rels):
+        prod[k] = dot(vec, rel_ref[k])
+    for j in range(qrel_ref.shape[0]):
+        kind = column(qrel_ref[j : j + 1, :])
         query = prod[0]
         for k in range(1, rels):
             query = jnp.where(kind == k, prod[k], query)
-        query = query.astype(BF)
-        q_ref[j] = query
-        tail = dot(hot(column(tail_ref[pl.ds(j, 1), :]), (heads, ents), 1), ent_ref[...])
-        score = jnp.sum(query.astype(F32) * tail, axis=1, keepdims=True)
+        q_ref[j * heads : (j + 1) * heads, :] = query.astype(BF)
+
+
+def weigh(q_ref, block_ref, weight, chunk):
+    for at in range(0, q_ref.shape[0], chunk):
+        seen = dot_t(q_ref[at : at + chunk, :], block_ref[...])
+        weight[at : at + chunk, :] = (jax.nn.sigmoid(seen) / STOPS).astype(BF)
+
+
+def visit_kernel(chunk, q_ref, block_ref, weight, term):
+    weigh(q_ref, block_ref, weight, chunk)
+    term[...] = t_dot(weight[...], q_ref[...]).astype(term.dtype)
+
+
+def pair_kernel(q_ref, qrel_ref, tail_ref, ent_ref, own_ref, *refs):
+    others = STOPS - 1
+    weights, blocks = refs[:others], refs[others : 2 * others]
+    pw_ref, pair_ref, term, weight, gq = refs[2 * others :]
+    per, heads = qrel_ref.shape
+    ents = ent_ref.shape[0]
+    weigh(q_ref, own_ref, weight, heads)
+    term[...] = t_dot(weight[...], q_ref[...])
+    for j in range(per):
+        here = slice(j * heads, (j + 1) * heads)
+        tail = dot(hot(column(tail_ref[j : j + 1, :]), (heads, ents), 1), ent_ref[...])
+        score = jnp.sum(q_ref[here, :].astype(F32) * tail, axis=1, keepdims=True)
         pw = jax.nn.sigmoid(score) - 1.0
         pw_ref[j] = pw
-        seen = dot_t(query, near[...])
-        w = (jax.nn.sigmoid(seen) / STOPS).astype(BF)
-        weight[pl.ds(pl.multiple_of(j * heads, heads), heads), :] = w
-        gq[j] = pw * tail + dot(w, near[...])
-
-    for index, term in enumerate(terms):
-        part = t_dot(
-            weight[:, index * rows : (index + 1) * rows], q_ref[...].reshape(per * heads, width)
-        )
-        term[...] = part.astype(term.dtype)
+        total = pw * tail + dot(weight[here, :], own_ref[...])
+        for one, block in zip(weights, blocks):
+            total = total + dot(one[here, :], block[...])
+        gq[j] = total
     kinds = [column(qrel_ref[j : j + 1, :]) for j in range(per)]
-
-    @pl.loop(0, rels)
-    def _(k):
+    for k in range(pair_ref.shape[0]):
         total = jnp.where(kinds[0] == k, gq[0], 0.0)
         for j in range(1, per):
             total = total + jnp.where(kinds[j] == k, gq[j], 0.0)
         pair_ref[k] = total.astype(BF)
 
 
-def push_kernel(
-    step, me_ref, pos_ref, vec_ref, pair_ref, rel_ref, keep_a, send_a, keep_b, send_b, bucket_ref, turned, a_side, b_side
-):
-    heads, width = vec_ref.shape
-    rels = rel_ref.shape[0]
-    half = width // 2
+def rel_kernel(step, first, outer, me_ref, vec_ref, pair_ref, keep, send, turned, side):
+    count, half = keep.shape[:2]
+    inner = 1 - outer
+    me = me_ref[0]
+    bits = (me % 2, (me // 2) % 2)
+    turned[...] = vec_ref[...].astype(F32).T
+    lines = half // 2 // step
+    for flips in range(4):
+        flip = (flips // 2, flips % 2)
+        bit = [0, 0]
+        bit[outer] = (bits[outer] + flip[0]) % 2
+        bit[inner] = (bits[inner] + flip[1]) % 2
+        for z in range(lines):
+            block = z * 4 + bit[1] * 2 + bit[0]
+            at = (flips * lines + z) * step
+            side[at : at + step, :] = turned[pl.ds(pl.multiple_of(block * step, step), step), :]
+    for k in range(count):
+        send[k] = dot(side[half:, :].astype(BF), pair_ref[first + k]).astype(BF)
+    for k in range(count):
+        keep[k] = dot(side[:half, :].astype(BF), pair_ref[first + k])
+
+
+def head_kernel(pos_ref, pair_ref, rel_ref, bucket_ref):
+    rels, heads, _ = pair_ref.shape
+    head = dot_t(pair_ref[0], rel_ref[0])
+    for k in range(1, rels):
+        head = head + dot_t(pair_ref[k], rel_ref[k])
     slots = bucket_ref.shape[0]
-    me = me_ref[0]
-    x, y = me % 2, (me // 2) % 2
-    turned[...] = vec_ref[...].astype(F32).T
-    deep = a_side.shape[0] // 4
-    lines = deep // step
-    for fx in range(2):
-        for fy in range(2):
-            for z in range(lines):
-                block = z * 4 + ((y + fy) % 2) * 2 + (x + fx) % 2
-                rows = turned[pl.ds(pl.multiple_of(block * step, step), step), :]
-                at = (fx * 2 + fy) * deep + z * step
-                bt = (fy * 2 + fx) * deep + z * step
-                a_side[at : at + step, :] = rows
-                b_side[bt : bt + step, :] = rows
-    head = jnp.zeros((heads, width), F32)
-    for k in range(rels):
-        head = head + dot_t(pair_ref[k], rel_ref[k])
     bucket_ref[...] = dot(hot(pos_ref[...], (slots, heads), 0), head.astype(BF)).astype(BF)
-    for side, keep, send, first in ((a_side, keep_a, send_a, 0), (b_side, keep_b, send_b, rels // 2)):
-        for k in range(rels // 2):
-            full = dot(side[...].astype(BF), pair_ref[first + k])
-            keep[k] = full[:half]
-            send[k] = full[half:].astype(BF)
 
 
 def tail_kernel(tail_ref, q_ref, pw_ref, out_ref):
-    ents, heads = out_ref.shape[0], q_ref.shape[1]
+    ents, heads = out_ref.shape[0], tail_ref.shape[1]
     total = jnp.zeros(out_ref.shape, F32)
-    for j in range(q_ref.shape[0]):
+    for j in range(tail_ref.shape[0]):
         spot = hot(tail_ref[j : j + 1, :], (ents, heads), 0)
-        top, rest = halves(pw_ref[j] * q_ref[j].astype(F32))
+        top, rest = halves(pw_ref[j] * q_ref[j * heads : (j + 1) * heads, :].astype(F32))
         total = total + dot(spot, top) + dot(spot, rest)
     out_ref[...] = total
 
@@ -213,6 +215,7 @@
             in_specs=specs,
             out_specs=[pl.BlockSpec(memory_space=pltpu.VMEM)] * len(outs),
             scratch_shapes=[pltpu.VMEM(s, d) for s, d in scratch],
+            compiler_params=pltpu.CompilerParams(vmem_limit_bytes=VMEM),
         )(*args)
 
     return call
@@ -253,28 +256,39 @@
     (served,) = kernel(serve_kernel, [((slots, width), BF)])(wanted, entity)
     fetched = dealt(served.reshape(shards, cap, width)).reshape(slots, width)
 
-    outs = [((rows, width), F32)] + [((rows, width), BF)] * (STOPS - 1)
-    outs += [((heads, width), BF), ((per, heads, width), BF), ((per, heads, 1), F32), ((rels, heads, width), BF)]
-    scratch = [
-        ((rels, heads, width), F32),
-        ((STOPS * rows, width), BF),
-        ((per * heads, STOPS * rows), BF),
-        ((per, heads, width), F32),
-    ]
-    *terms, vec, queries, pos_weight, pair = kernel(visit_kernel, outs, scratch)(
-        pos, qrel, tail, fetched, relation, entity, *blocks
-    )
-    back = [terms[0]] + [moved(terms[n + 1], -o) for n, o in enumerate(OFFSETS)]
+    many = per * heads
+    vec, queries = kernel(
+        query_kernel, [((heads, width), BF), ((many, width), BF)], [((rels, heads, width), F32)]
+    )(pos, qrel, fetched, relation)
+    weights, back = [], []
+    for n, offset in enumerate(OFFSETS):
+        weight, term = kernel(
+            functools.partial(visit_kernel, heads), [((many, rows), BF), ((rows, width), BF)]
+        )(queries, blocks[n + 1])
+        weights.append(weight)
+        back.append(moved(term, -offset))
+    pos_weight, pair, own_term = kernel(
+        pair_kernel,
+        [((per, heads, 1), F32), ((rels, heads, width), BF), ((rows, width), F32)],
+        [((many, rows), BF), ((per, heads, width), F32)],
+    )(queries, qrel, tail, entity, own_block, *weights, *blocks[1:])
+    back = [own_term] + back
 
     part = (rels // 2, width // 2, width)
-    keep_a, send_a, keep_b, send_b, buckets = kernel(
-        functools.partial(push_kernel, step),
-        [(part, F32), (part, BF), (part, F32), (part, BF), ((slots, width), BF)],
-        [((width, heads), F32)] * 3,
-        smem=1,
-    )(me, pos, vec, pair, relation)
+
+    def relations(first, outer):
+        return kernel(
+            functools.partial(rel_kernel, step, first, outer),
+            [(part, F32), (part, BF)],
+            [((width, heads), F32)] * 2,
+            smem=1,
+        )(me, vec, pair)
+
+    keep_a, send_a = relations(0, 0)
     got_a = flipped(send_a, 1)
+    keep_b, send_b = relations(rels // 2, 1)
     got_b = flipped(send_b, 2)
+    (buckets,) = kernel(head_kernel, [((slots, width), BF)])(pos, pair, relation)
     returned = dealt(buckets.reshape(shards, cap, width)).reshape(slots, width)
     (base,) = kernel(tail_kernel, [((ents, width), F32)])(tail, queries, pos_weight)
 

time: 144 us -> 142 us (0.986)
  local copies, waits for them, and re-layouts: 2.72 us -> 11 us
  Pallas kernels: 32.1 us -> 25.9 us
  starting transfers between devices: 38.8 us -> 35.6 us
  waiting for transfers between devices: 45.7 us -> 43.7 us
    ppermute x10, waiting for transfers between devices: 32 us -> 9.67 us  [moved(): lax.ppermute(value, 'blk', [((i - distance) % shards, i) for i in range(s...]
    all_to_all x3, waiting for transfers between devices: 0.35 us -> 21.6 us  [dealt(): lax.all_to_all(value, 'blk', split_axis=0, concat_axis=0, tiled=True, axi...]
    unnamed x36 -> x44, local copies, waits for them, and re-layouts: 1.49 us -> 10.4 us
    pallas_call x7 -> x15, Pallas kernels: 32.1 us -> 25.9 us  [call(): pl.pallas_call(body, out_shape=[jax.ShapeDtypeStruct(s, d) for s, d in ou...]
    ppermute x4, starting transfers between devices: 8.36 us -> 4.59 us  [flipped(): return lax.ppermute(value, 'blk', [(i, i ^ bit) for i in range(shards)])]
  transfers between devices with their start and end apart: 18 -> 18, of which waited for: 11 -> 8; matrix products, arithmetic and copies ran while one was open for 5% -> 4% of each run, Pallas kernels for 7% -> 11%
where the time goes in v3:
time: 142 us; the launch traced here: 140 us
  waiting for transfers between devices  43.7 us (31%)
  starting transfers between devices  35.6 us (25%)
  Pallas kernels  25.9 us (18%)
  blocking collectives  15.4 us (11%)
  local copies, waits for them, and re-layouts  11 us (8%)
  other arithmetic  7.18 us (5%)
    pallas_call x15, Pallas kernels, call(): pl.pallas_call(body, out_shape=[jax.ShapeDtypeStruct(s, d) for s, d in ou...  25.9 us
    all_to_all x3, waiting for transfers between devices, dealt(): lax.all_to_all(value, 'blk', split_axis=0, concat_axis=0, tiled=True, axi...  21.6 us
    ppermute x10, starting transfers between devices, moved(): lax.ppermute(value, 'blk', [((i - distance) % shards, i) for i in range(s...  18.3 us
    all_to_all x1, blocking collectives, dealt(): lax.all_to_all(value, 'blk', split_axis=0, concat_axis=0, tiled=True, axi...  15.4 us
    all_to_all x3, starting transfers between devices, dealt(): lax.all_to_all(value, 'blk', split_axis=0, concat_axis=0, tiled=True, axi...  12.6 us
    ppermute x4, waiting for transfers between devices, flipped(): return lax.ppermute(value, 'blk', [(i, i ^ bit) for i in range(shards)])  10.9 us
    unnamed x44, local copies, waits for them, and re-layouts  10.4 us
    ppermute x10, waiting for transfers between devices, moved(): lax.ppermute(value, 'blk', [((i - distance) % shards, i) for i in range(s...  9.67 us
  transfers between devices with their start and end apart: 18, of which 8 were waited for; matrix products, arithmetic and copies ran while one was open for 4% of the time, Pallas kernels for 11%

profile of v3, /device:TPU:0, one launch (start us, length us, event | category | flops | bytes accessed | tf_op | source)
XLA Modules:
  0.0 139.8 jit_solution(10109520572680529542)
XLA Ops:
  0.7 0.8 copy-done.17
  1.5 0.7 copy-done.18
  2.1 0.3 shard_map.86
  2.5 15.4 %all_to_all.26 = s32[16,1,32]{2,1,0:T(1,128)S(1)} all-to-all(s32[16,1,32]{2,1,0:T(1,128)S(1)} %bitcast.26), channel_id=1, replica_groups=mesh['blk'=16,'rep'=2] {'blk'}, dimensions={0} | all-to-all | bytes 4096 | tf_op jit(solution)/shard_map/all_to_all | solution.py:244
  17.9 1.0 copy-done.1
  19.0 1.5 %shard_map.87 = bf16[512,512]{1,0:T(8,128)(2,1)} custom-call(s32[16,32]{1,0:T(8,128)S(1)} %bitcast.21, bf16[512,512]{1,0:T(8,128)(2,1)S(1)} %copy-done.1), custom_call_target="tpu_custom_call" | custom-call | tf_op jit(solution)/shard_map/pallas_call | solution.py:212
  20.4 3.6 %all-to-all-start.1 = ((bf16[16,32,512]{2,1,0:T(8,128)(2,1)}), bf16[16,32,512]{2,1,0:T(8,128)(2,1)S(1)}, u32[]{:S(2)}, u32[]{:S(2)}) async-start(bf16[16,32,512]{2,1,0:T(8,128)(2,1)} %bitcast.8), calls=%async_computation.1 | async-start | bytes 1048576 | tf_op jit(solution)/shard_map/all_to_all | solution.py:244
  24.0 0.0 copy-start.2
  24.0 1.0 copy-done.2
  25.1 1.1 shard_map.89.own_ref
  26.1 4.6 %collective-permute-start.4 = (bf16[256,512]{1,0:T(8,128)(2,1)}, bf16[256,512]{1,0:T(8,128)(2,1)S(1)}, u32[]{:S(2)}, u32[]{:S(2)}) collective-permute-start(bf16[256,512]{1,0:T(8,128)(2,1)} %shard_map.89.own_ref), channel_id=1, source_target_pairs={{4,0},{6,2},{8,4},{10,6},{12,8},{14,10},{16,12},{18,14},{20,16},{2... | collective-permute-start | bytes 786440 | tf_op jit(solution)/shard_map/ppermute | solution.py:238
  30.7 1.5 %collective-permute-start.3 = (bf16[256,512]{1,0:T(8,128)(2,1)}, bf16[256,512]{1,0:T(8,128)(2,1)}, u32[]{:S(2)}, u32[]{:S(2)}) collective-permute-start(bf16[256,512]{1,0:T(8,128)(2,1)} %shard_map.89.own_ref), channel_id=1, source_target_pairs={{2,0},{4,2},{6,4},{8,6},{10,8},{12,10},{14,12},{16,14},{18,16},{20... | collective-permute-start | bytes 786440 | tf_op jit(solution)/shard_map/ppermute | solution.py:238
  32.2 1.5 %collective-permute-start.1 = (bf16[256,512]{1,0:T(8,128)(2,1)}, bf16[256,512]{1,0:T(8,128)(2,1)}, u32[]{:S(2)}, u32[]{:S(2)}) collective-permute-start(bf16[256,512]{1,0:T(8,128)(2,1)} %shard_map.89.own_ref), channel_id=1, source_target_pairs={{28,0},{30,2},{0,4},{2,6},{4,8},{6,10},{8,12},{10,14},{12,16},{14,... | collective-permute-start | bytes 786440 | tf_op jit(solution)/shard_map/ppermute | solution.py:238
  33.6 0.1 collective-permute-start
  33.8 0.1 pad_add_fusion.me_ref
  33.9 21.6 %all-to-all-done.1 = bf16[16,32,512]{2,1,0:T(8,128)(2,1)S(1)} async-done(((bf16[16,32,512]{2,1,0:T(8,128)(2,1)}), bf16[16,32,512]{2,1,0:T(8,128)(2,1)S(1)}, u32[]{:S(2)}, u32[]{:S(2)}) %all-to-all-start.1) | async-done | bytes 524320 | tf_op jit(solution)/shard_map/all_to_all | solution.py:244
  55.5 0.8 copy-done.4
  56.3 1.0 copy-done.5
  57.3 1.2 shard_map.88
  58.5 1.6 %shard_map.94 = (bf16[1024,256]{1,0:T(8,128)(2,1)S(1)}, bf16[256,512]{1,0:T(8,128)(2,1)}) custom-call(bf16[1024,512]{1,0:T(8,128)(2,1)S(1)} %get-tuple-element.27.q_ref, bf16[256,512]{1,0:T(8,128)(2,1)S(1)} %collective-permute-done.4.block_ref.refs_9_), custom_call_target="tpu_custom_call" | custom-call | tf_op jit(solution)/shard_map/pallas_call | solution.py:212
  60.1 2.5 %shard_map.93 = (bf16[1024,256]{1,0:T(8,128)(2,1)S(1)}, bf16[256,512]{1,0:T(8,128)(2,1)}) custom-call(bf16[1024,512]{1,0:T(8,128)(2,1)S(1)} %get-tuple-element.27.q_ref, bf16[256,512]{1,0:T(8,128)(2,1)} %collective-permute-done.3.block_ref.refs_8_), custom_call_target="tpu_custom_call" | custom-call | tf_op jit(solution)/shard_map/pallas_call | solution.py:212
  62.6 1.8 %shard_map.92 = (bf16[1024,256]{1,0:T(8,128)(2,1)S(1)}, bf16[256,512]{1,0:T(8,128)(2,1)S(1)}) custom-call(bf16[1024,512]{1,0:T(8,128)(2,1)S(1)} %get-tuple-element.27.q_ref, bf16[256,512]{1,0:T(8,128)(2,1)} %collective-permute-done.2.block_ref.refs_7_), custom_call_target="tpu_custom_call" | custom-call | tf_op jit(solution)/shard_map/pallas_call | solution.py:212
  64.4 0.7 copy-done.19
  65.1 1.8 %shard_map.91 = (bf16[1024,256]{1,0:T(8,128)(2,1)S(1)}, bf16[256,512]{1,0:T(8,128)(2,1)S(1)}) custom-call(bf16[1024,512]{1,0:T(8,128)(2,1)S(1)} %get-tuple-element.27.q_ref, bf16[256,512]{1,0:T(8,128)(2,1)} %collective-permute-done.1.block_ref.refs_6_), custom_call_target="tpu_custom_call" | custom-call | tf_op jit(solution)/shard_map/pallas_call | solution.py:212
  66.9 0.7 copy-done.20
  67.6 1.7 %shard_map.90 = (bf16[1024,256]{1,0:T(8,128)(2,1)S(1)}, bf16[256,512]{1,0:T(8,128)(2,1)S(1)}) custom-call(bf16[1024,512]{1,0:T(8,128)(2,1)S(1)} %get-tuple-element.27.q_ref, bf16[256,512]{1,0:T(8,128)(2,1)} %collective-permute-done.block_ref.refs_5_), custom_call_target="tpu_custom_call" | custom-call | tf_op jit(solution)/shard_map/pallas_call | solution.py:212
  69.4 0.7 copy-done.21
  70.1 4.8 %shard_map.95 = (f32[4,256,1]{2,1,0:T(8,128)S(1)}, bf16[4,256,512]{2,1,0:T(8,128)(2,1)S(1)}, f32[256,512]{1,0:T(8,128)S(1)}) custom-call(bf16[1024,512]{1,0:T(8,128)(2,1)S(1)} %get-tuple-element.27.q_ref, s32[4,256]{1,0:T(4,128)S(1)} %bitcast.23, s32[4,256]{1,0:T(4,128)S(1)} %bitcast.24, bf16[512,512]{1,0:T(8,128)(2,1)S(1)} %copy-done.3, ...), custom_call_target="tpu_custom_call" | custom-call | tf_op jit(solution)/shard_map/pallas_call | solution.py:212
  74.9 1.8 %shard_map.99 = (f32[2,256,512]{2,1,0:T(8,128)S(1)}, bf16[2,256,512]{2,1,0:T(8,128)(2,1)}) custom-call(s32[2]{0:T(128)S(1)} %pad_add_fusion.me_ref, bf16[256,512]{1,0:T(8,128)(2,1)S(1)} %get-tuple-element.43.vec_ref, bf16[4,256,512]{2,1,0:T(8,128)(2,1)S(1)} %get-tuple-element.33.pair_ref), custom_call_target="tpu_custom_call" | custom-call | tf_op jit(solution)/shard_map/pallas_call | solution.py:212
  76.6 1.0 copy-done.9
  77.6 1.8 %shard_map.100 = (f32[2,256,512]{2,1,0:T(8,128)S(1)}, bf16[2,256,512]{2,1,0:T(8,128)(2,1)}) custom-call(s32[2]{0:T(128)S(1)} %pad_add_fusion.me_ref, bf16[256,512]{1,0:T(8,128)(2,1)S(1)} %get-tuple-element.43.vec_ref, bf16[4,256,512]{2,1,0:T(8,128)(2,1)S(1)} %get-tuple-element.33.pair_ref), custom_call_target="tpu_custom_call" | custom-call | tf_op jit(solution)/shard_map/pallas_call | solution.py:212
  79.4 1.0 copy-done.7
  80.4 0.9 collective-permute-start.13
  81.3 1.0 shard_map.96
  82.4 0.8 copy-done.6
  83.2 4.7 %all-to-all-start.2 = ((bf16[16,32,512]{2,1,0:T(8,128)(2,1)}), bf16[16,32,512]{2,1,0:T(8,128)(2,1)S(1)}, u32[]{:S(2)}, u32[]{:S(2)}) async-start(bf16[16,32,512]{2,1,0:T(8,128)(2,1)} %bitcast.20), calls=%async_computation.2 | async-start | bytes 1048576 | tf_op jit(solution)/shard_map/all_to_all | solution.py:244
  87.9 1.5 %convert_add_fusion.1 = f32[2,256,512]{2,1,0:T(8,128)S(1)} fusion(f32[2,256,512]{2,1,0:T(8,128)} %copy-done.9, bf16[2,256,512]{2,1,0:T(8,128)(2,1)} %collective-permute-done.11), kind=kLoop, calls=%fused_computation.2 | loop fusion | flops 524288 | bytes 2621440 | tf_op jit(solution)/shard_map/add | solution.py:296
  89.5 2.0 %collective-permute-start.12 = (bf16[2,128,512]{2,1,0:T(8,128)(2,1)S(1)}, bf16[2,128,512]{2,1,0:T(8,128)(2,1)S(1)}, u32[]{:S(2)}, u32[]{:S(2)}) collective-permute-start(bf16[2,128,512]{2,1,0:T(8,128)(2,1)S(1)} %slice.31), channel_id=1, source_target_pairs={{0,4},{2,6},{4,0},{6,2},{8,12},{10,14},{12,8},{14,10},{16,20},{18,... | collective-permute-start | bytes 786440 | tf_op jit(solution)/shard_map/ppermute | solution.py:241
  91.5 6.2 %collective-permute-done.13 = bf16[2,256,512]{2,1,0:T(8,128)(2,1)} collective-permute-done((bf16[2,256,512]{2,1,0:T(8,128)(2,1)}, bf16[2,256,512]{2,1,0:T(8,128)(2,1)}, u32[]{:S(2)}, u32[]{:S(2)}) %collective-permute-start.13) | collective-permute-done | bytes 524320 | tf_op jit(solution)/shard_map/ppermute | solution.py:241
  97.7 1.2 convert_add_fusion
  99.0 1.7 %collective-permute-start.14 = (bf16[2,128,512]{2,1,0:T(8,128)(2,1)S(1)}, bf16[2,128,512]{2,1,0:T(8,128)(2,1)S(1)}, u32[]{:S(2)}, u32[]{:S(2)}) collective-permute-start(bf16[2,128,512]{2,1,0:T(8,128)(2,1)S(1)} %slice.30), channel_id=1, source_target_pairs={{0,2},{2,0},{4,6},{6,4},{8,10},{10,8},{12,14},{14,12},{16,18},{18,... | collective-permute-start | bytes 786440 | tf_op jit(solution)/shard_map/ppermute | solution.py:241
  100.6 0.8 collective-permute-done.12
  101.5 0.1 fusion.1
  101.5 3.9 %collective-permute-done.14 = bf16[2,128,512]{2,1,0:T(8,128)(2,1)S(1)} collective-permute-done((bf16[2,128,512]{2,1,0:T(8,128)(2,1)S(1)}, bf16[2,128,512]{2,1,0:T(8,128)(2,1)S(1)}, u32[]{:S(2)}, u32[]{:S(2)}) %collective-permute-start.14) | collective-permute-done | bytes 262176 | tf_op jit(solution)/shard_map/ppermute | solution.py:241
  105.4 0.1 fusion
  105.5 0.9 copy_bitcast_fusion
  106.4 4.3 %all-to-all-start.3 = ((bf16[4,4,32,512]{3,2,1,0:T(8,128)(2,1)}), bf16[4,4,32,512]{3,2,1,0:T(8,128)(2,1)}, u32[]{:S(2)}, u32[]{:S(2)}) async-start(bf16[4,4,32,512]{3,2,1,0:T(8,128)(2,1)} %copy_bitcast_fusion), calls=%async_computation.3 | async-start | bytes 1048576 | tf_op jit(solution)/shard_map/all_to_all | solution.py:244
  110.7 0.8 collective-permute-start.9
  111.5 2.0 %collective-permute-start.8 = (bf16[256,512]{1,0:T(8,128)(2,1)}, bf16[256,512]{1,0:T(8,128)(2,1)S(1)}, u32[]{:S(2)}, u32[]{:S(2)}) collective-permute-start(bf16[256,512]{1,0:T(8,128)(2,1)} %get-tuple-element.39), channel_id=1, source_target_pairs={{30,0},{0,2},{2,4},{4,6},{6,8},{8,10},{10,12},{12,14},{14,16},{16,... | collective-permute-start | bytes 786440 | tf_op jit(solution)/shard_map/ppermute | solution.py:238
  113.5 3.4 %collective-permute-start.7 = (bf16[256,512]{1,0:T(8,128)(2,1)}, bf16[256,512]{1,0:T(8,128)(2,1)S(1)}, u32[]{:S(2)}, u32[]{:S(2)}) collective-permute-start(bf16[256,512]{1,0:T(8,128)(2,1)} %copy-done.19), channel_id=1, source_target_pairs={{6,0},{8,2},{10,4},{12,6},{14,8},{16,10},{18,12},{20,14},{22,16},{... | collective-permute-start | bytes 786440 | tf_op jit(solution)/shard_map/ppermute | solution.py:238
  116.9 2.1 %collective-permute-start.6 = (bf16[256,512]{1,0:T(8,128)(2,1)}, bf16[256,512]{1,0:T(8,128)(2,1)}, u32[]{:S(2)}, u32[]{:S(2)}) collective-permute-start(bf16[256,512]{1,0:T(8,128)(2,1)} %copy-done.20), channel_id=1, source_target_pairs={{4,0},{6,2},{8,4},{10,6},{12,8},{14,10},{16,12},{18,14},{20,16},{2... | collective-permute-start | bytes 786440 | tf_op jit(solution)/shard_map/ppermute | solution.py:238
  119.0 2.3 %collective-permute-start.5 = (bf16[256,512]{1,0:T(8,128)(2,1)}, bf16[256,512]{1,0:T(8,128)(2,1)}, u32[]{:S(2)}, u32[]{:S(2)}) collective-permute-start(bf16[256,512]{1,0:T(8,128)(2,1)} %copy-done.21), channel_id=1, source_target_pairs={{2,0},{4,2},{6,4},{8,6},{10,8},{12,10},{14,12},{16,14},{18,16},{20... | collective-permute-start | bytes 786440 | tf_op jit(solution)/shard_map/ppermute | solution.py:238
  121.3 0.5 broadcast.3
  121.8 0.7 reduce.3
  122.5 0.1 reshape.35.wanted_ref
  122.6 1.4 %shard_map.97.base_ref = f32[512,512]{1,0:T(8,128)S(1)} custom-call(s32[4,256]{1,0:T(4,128)S(1)} %bitcast.25, bf16[1024,512]{1,0:T(8,128)(2,1)S(1)} %get-tuple-element.27.q_ref, f32[4,256,1]{2,1,0:T(8,128)S(1)} %copy-done.11), custom_call_target="tpu_custom_call" | custom-call | tf_op jit(solution)/shard_map/pallas_call | solution.py:212
  124.0 4.5 %collective-permute-done.9.refs_5_ = bf16[256,512]{1,0:T(8,128)(2,1)S(1)} collective-permute-done((bf16[256,512]{1,0:T(8,128)(2,1)}, bf16[256,512]{1,0:T(8,128)(2,1)S(1)}, u32[]{:S(2)}, u32[]{:S(2)}) %collective-permute-start.9) | collective-permute-done | bytes 262176 | tf_op jit(solution)/shard_map/ppermute | solution.py:238
  128.6 3.8 %collective-permute-done.8.refs_4_ = bf16[256,512]{1,0:T(8,128)(2,1)S(1)} collective-permute-done((bf16[256,512]{1,0:T(8,128)(2,1)}, bf16[256,512]{1,0:T(8,128)(2,1)S(1)}, u32[]{:S(2)}, u32[]{:S(2)}) %collective-permute-start.8) | collective-permute-done | bytes 262176 | tf_op jit(solution)/shard_map/ppermute | solution.py:238
  132.4 1.3 collective-permute-done.6.refs_2_
  133.7 1.8 %shard_map.98 = (f32[512,256]{1,0:T(8,128)S(1)}, bf16[512,256]{1,0:T(8,128)(2,1)S(1)}) custom-call(s32[2]{0:T(128)S(1)} %pad_add_fusion.me_ref, s32[1,512]{1,0:T(1,128)S(1)} %reshape.35.wanted_ref, s32[1,256]{1,0:T(1,128)S(1)} %copy-done.16, bf16[512,512]{1,0:T(8,128)(2,1)S(1)} %bitcast.19, f32[512,512]{1,0:T(8,128)S(1)} %shard_map.97.base_ref, ...), custom_call_target="tpu_custom_call" | custom-call | tf_op jit(solution)/shard_map/pallas_call | solution.py:212
  135.5 0.1 collective-permute-start.10
  135.6 1.5 %collective-permute-done.10 = bf16[512,256]{1,0:T(8,128)(2,1)S(1)} collective-permute-done((bf16[512,256]{1,0:T(8,128)(2,1)S(1)}, bf16[512,256]{1,0:T(8,128)(2,1)S(1)}, u32[]{:S(2)}, u32[]{:S(2)}) %collective-permute-start.10) | collective-permute-done | bytes 262176 | tf_op jit(solution)/shard_map/ppermute | solution.py:317
  137.1 0.8 convert_add_fusion.2
  138.0 1.8 %convert_reduce_fusion = f32[4,32,512]{2,1,0:T(8,128)} fusion(bf16[4,4,32,512]{3,2,1,0:T(8,128)(2,1)} %all-to-all-done.3), kind=kLoop, calls=%fused_computation | loop fusion | flops 458752 | bytes 786432 | tf_op jit(solution)/shard_map/reduce_sum | solution.py:306
  (45 shorter events, 0.2 us)
Async XLA Ops:
  0.6 55.6 %copy-start = (bf16[4,512,512]{2,1,0:T(8,128)(2,1)S(1)}, bf16[4,512,512]{2,1,0:T(8,128)(2,1)}, u32[]{:S(2)}) copy-start(bf16[4,512,512]{2,1,0:T(8,128)(2,1)} %rel_ref.3) | copy-start | bytes 6291460
  0.6 0.8 copy-start.17
  1.5 0.7 copy-start.18
  17.9 1.0 copy-start.1
  19.0 5.0 %copy-start.16 = (s32[1,256]{1,0:T(1,128)S(1)}, s32[1,256]{1,0:T(1,128)}, u32[]{:S(2)}) copy-start(s32[1,256]{1,0:T(1,128)} %neg_ref.1) | copy-start | bytes 3076
  19.0 37.3 %copy-start.14 = (s32[256,4]{0,1:T(4,128)S(1)}, s32[256,4]{0,1:T(4,128)}, u32[]{:S(2)}) copy-start(s32[256,4]{0,1:T(4,128)} %param.11) | copy-start | bytes 12292
  20.4 35.0 %all-to-all-start.1 = ((bf16[16,32,512]{2,1,0:T(8,128)(2,1)}), bf16[16,32,512]{2,1,0:T(8,128)(2,1)S(1)}, u32[]{:S(2)}, u32[]{:S(2)}) async-start(bf16[16,32,512]{2,1,0:T(8,128)(2,1)} %bitcast.8), calls=%async_computation.1 | async-start | bytes 1048576 | tf_op jit(solution)/shard_map/all_to_all | solution.py:244
  24.0 1.0 copy-start.2
  26.1 32.4 %collective-permute-start.4 = (bf16[256,512]{1,0:T(8,128)(2,1)}, bf16[256,512]{1,0:T(8,128)(2,1)S(1)}, u32[]{:S(2)}, u32[]{:S(2)}) collective-permute-start(bf16[256,512]{1,0:T(8,128)(2,1)} %shard_map.89.own_ref), channel_id=1, source_target_pairs={{4,0},{6,2},{8,4},{10,6},{12,8},{14,10},{16,12},{18,14},{20,16},{2... | collective-permute-start | bytes 786440 | tf_op jit(solution)/shard_map/ppermute | solution.py:238
  30.7 29.4 %collective-permute-start.3 = (bf16[256,512]{1,0:T(8,128)(2,1)}, bf16[256,512]{1,0:T(8,128)(2,1)}, u32[]{:S(2)}, u32[]{:S(2)}) collective-permute-start(bf16[256,512]{1,0:T(8,128)(2,1)} %shard_map.89.own_ref), channel_id=1, source_target_pairs={{2,0},{4,2},{6,4},{8,6},{10,8},{12,10},{14,12},{16,14},{18,16},{20... | collective-permute-start | bytes 786440 | tf_op jit(solution)/shard_map/ppermute | solution.py:238
  32.2 30.4 %collective-permute-start.2 = (bf16[256,512]{1,0:T(8,128)(2,1)}, bf16[256,512]{1,0:T(8,128)(2,1)}, u32[]{:S(2)}, u32[]{:S(2)}) collective-permute-start(bf16[256,512]{1,0:T(8,128)(2,1)} %shard_map.89.own_ref), channel_id=1, source_target_pairs={{26,0},{28,2},{30,4},{0,6},{2,8},{4,10},{6,12},{8,14},{10,16},{12,... | collective-permute-start | bytes 786440 | tf_op jit(solution)/shard_map/ppermute | solution.py:238
  32.2 33.0 %collective-permute-start.1 = (bf16[256,512]{1,0:T(8,128)(2,1)}, bf16[256,512]{1,0:T(8,128)(2,1)}, u32[]{:S(2)}, u32[]{:S(2)}) collective-permute-start(bf16[256,512]{1,0:T(8,128)(2,1)} %shard_map.89.own_ref), channel_id=1, source_target_pairs={{28,0},{30,2},{0,4},{2,6},{4,8},{6,10},{8,12},{10,14},{12,16},{14,... | collective-permute-start | bytes 786440 | tf_op jit(solution)/shard_map/ppermute | solution.py:238
  33.6 34.0 %collective-permute-start = (bf16[256,512]{1,0:T(8,128)(2,1)}, bf16[256,512]{1,0:T(8,128)(2,1)}, u32[]{:S(2)}, u32[]{:S(2)}) collective-permute-start(bf16[256,512]{1,0:T(8,128)(2,1)} %shard_map.89.own_ref), channel_id=1, source_target_pairs={{30,0},{0,2},{2,4},{4,6},{6,8},{8,10},{10,12},{12,14},{14,16},{16,... | collective-permute-start | bytes 786440 | tf_op jit(solution)/shard_map/ppermute | solution.py:238
  55.5 0.8 copy-start.4
  56.3 1.0 copy-start.5
  62.6 7.5 %copy-start.3 = (bf16[512,512]{1,0:T(8,128)(2,1)S(1)}, bf16[512,512]{1,0:T(8,128)(2,1)}, u32[]{:S(2)}) copy-start(bf16[512,512]{1,0:T(8,128)(2,1)} %ent_ref.1) | copy-start | bytes 1572868
  62.6 7.5 %copy-start.15 = (s32[256,4]{0,1:T(4,128)S(1)}, s32[256,4]{0,1:T(4,128)}, u32[]{:S(2)}) copy-start(s32[256,4]{0,1:T(4,128)} %param.12) | copy-start | bytes 12292
  64.4 0.7 copy-start.19
  66.9 0.7 copy-start.20
  69.4 0.7 copy-start.21
  74.9 7.5 %copy-start.10 = (f32[4,256,1]{2,1,0:T(8,128)}, f32[4,256,1]{2,1,0:T(8,128)S(1)}, u32[]{:S(2)}) copy-start(f32[4,256,1]{2,1,0:T(8,128)S(1)} %get-tuple-element.34.pw_ref) | copy-start | bytes 12292
  74.9 7.5 %copy-start.12 = (f32[256,512]{1,0:T(8,128)}, f32[256,512]{1,0:T(8,128)S(1)}, u32[]{:S(2)}) copy-start(f32[256,512]{1,0:T(8,128)S(1)} %get-tuple-element.35.refs_0_) | copy-start | bytes 1572868
  76.6 1.0 copy-start.9
  77.6 10.3 %collective-permute-start.11 = (bf16[2,256,512]{2,1,0:T(8,128)(2,1)}, bf16[2,256,512]{2,1,0:T(8,128)(2,1)}, u32[]{:S(2)}, u32[]{:S(2)}) collective-permute-start(bf16[2,256,512]{2,1,0:T(8,128)(2,1)} %get-tuple-element.45), channel_id=1, source_target_pairs={{0,2},{2,0},{4,6},{6,4},{8,10},{10,8},{12,14},{14,12},{16,18},{18,... | collective-permute-start | bytes 1572872 | tf_op jit(solution)/shard_map/ppermute | solution.py:241
  79.4 1.0 copy-start.7
  80.4 17.3 %collective-permute-start.13 = (bf16[2,256,512]{2,1,0:T(8,128)(2,1)}, bf16[2,256,512]{2,1,0:T(8,128)(2,1)}, u32[]{:S(2)}, u32[]{:S(2)}) collective-permute-start(bf16[2,256,512]{2,1,0:T(8,128)(2,1)} %get-tuple-element.47), channel_id=1, source_target_pairs={{0,4},{2,6},{4,0},{6,2},{8,12},{10,14},{12,8},{14,10},{16,20},{18,... | collective-permute-start | bytes 1572872 | tf_op jit(solution)/shard_map/ppermute | solution.py:241
  82.4 0.8 copy-start.6
  83.2 14.5 %copy-start.8 = (f32[2,256,512]{2,1,0:T(8,128)S(1)}, f32[2,256,512]{2,1,0:T(8,128)}, u32[]{:S(2)}) copy-start(f32[2,256,512]{2,1,0:T(8,128)} %copy-done.7) | copy-start | bytes 3145732
  83.2 23.2 %all-to-all-start.2 = ((bf16[16,32,512]{2,1,0:T(8,128)(2,1)}), bf16[16,32,512]{2,1,0:T(8,128)(2,1)S(1)}, u32[]{:S(2)}, u32[]{:S(2)}) async-start(bf16[16,32,512]{2,1,0:T(8,128)(2,1)} %bitcast.20), calls=%async_computation.2 | async-start | bytes 1048576 | tf_op jit(solution)/shard_map/all_to_all | solution.py:244
  89.5 12.0 %collective-permute-start.12 = (bf16[2,128,512]{2,1,0:T(8,128)(2,1)S(1)}, bf16[2,128,512]{2,1,0:T(8,128)(2,1)S(1)}, u32[]{:S(2)}, u32[]{:S(2)}) collective-permute-start(bf16[2,128,512]{2,1,0:T(8,128)(2,1)S(1)} %slice.31), channel_id=1, source_target_pairs={{0,4},{2,6},{4,0},{6,2},{8,12},{10,14},{12,8},{14,10},{16,20},{18,... | collective-permute-start | bytes 786440 | tf_op jit(solution)/shard_map/ppermute | solution.py:241
  99.0 23.6 %copy-start.11 = (f32[4,256,1]{2,1,0:T(8,128)S(1)}, f32[4,256,1]{2,1,0:T(8,128)}, u32[]{:S(2)}) copy-start(f32[4,256,1]{2,1,0:T(8,128)} %copy-done.10) | copy-start | bytes 12292
  99.0 6.4 %collective-permute-start.14 = (bf16[2,128,512]{2,1,0:T(8,128)(2,1)S(1)}, bf16[2,128,512]{2,1,0:T(8,128)(2,1)S(1)}, u32[]{:S(2)}, u32[]{:S(2)}) collective-permute-start(bf16[2,128,512]{2,1,0:T(8,128)(2,1)S(1)} %slice.30), channel_id=1, source_target_pairs={{0,2},{2,0},{4,6},{6,4},{8,10},{10,8},{12,14},{14,12},{16,18},{18,... | collective-permute-start | bytes 786440 | tf_op jit(solution)/shard_map/ppermute | solution.py:241
  106.4 27.3 %copy-start.13 = (f32[256,512]{1,0:T(8,128)S(1)}, f32[256,512]{1,0:T(8,128)}, u32[]{:S(2)}) copy-start(f32[256,512]{1,0:T(8,128)} %copy-done.12) | copy-start | bytes 1572868
  106.4 31.6 %all-to-all-start.3 = ((bf16[4,4,32,512]{3,2,1,0:T(8,128)(2,1)}), bf16[4,4,32,512]{3,2,1,0:T(8,128)(2,1)}, u32[]{:S(2)}, u32[]{:S(2)}) async-start(bf16[4,4,32,512]{3,2,1,0:T(8,128)(2,1)} %copy_bitcast_fusion), calls=%async_computation.3 | async-start | bytes 1048576 | tf_op jit(solution)/shard_map/all_to_all | solution.py:244
  110.7 17.9 %collective-permute-start.9 = (bf16[256,512]{1,0:T(8,128)(2,1)}, bf16[256,512]{1,0:T(8,128)(2,1)S(1)}, u32[]{:S(2)}, u32[]{:S(2)}) collective-permute-start(bf16[256,512]{1,0:T(8,128)(2,1)} %get-tuple-element.40), channel_id=1, source_target_pairs={{28,0},{30,2},{0,4},{2,6},{4,8},{6,10},{8,12},{10,14},{12,16},{14,... | collective-permute-start | bytes 786440 | tf_op jit(solution)/shard_map/ppermute | solution.py:238
  111.5 20.9 %collective-permute-start.8 = (bf16[256,512]{1,0:T(8,128)(2,1)}, bf16[256,512]{1,0:T(8,128)(2,1)S(1)}, u32[]{:S(2)}, u32[]{:S(2)}) collective-permute-start(bf16[256,512]{1,0:T(8,128)(2,1)} %get-tuple-element.39), channel_id=1, source_target_pairs={{30,0},{0,2},{2,4},{4,6},{6,8},{8,10},{10,12},{12,14},{14,16},{16,... | collective-permute-start | bytes 786440 | tf_op jit(solution)/shard_map/ppermute | solution.py:238
  113.5 18.9 %collective-permute-start.7 = (bf16[256,512]{1,0:T(8,128)(2,1)}, bf16[256,512]{1,0:T(8,128)(2,1)S(1)}, u32[]{:S(2)}, u32[]{:S(2)}) collective-permute-start(bf16[256,512]{1,0:T(8,128)(2,1)} %copy-done.19), channel_id=1, source_target_pairs={{6,0},{8,2},{10,4},{12,6},{14,8},{16,10},{18,12},{20,14},{22,16},{... | collective-permute-start | bytes 786440 | tf_op jit(solution)/shard_map/ppermute | solution.py:238
  116.9 16.8 %collective-permute-start.6 = (bf16[256,512]{1,0:T(8,128)(2,1)}, bf16[256,512]{1,0:T(8,128)(2,1)}, u32[]{:S(2)}, u32[]{:S(2)}) collective-permute-start(bf16[256,512]{1,0:T(8,128)(2,1)} %copy-done.20), channel_id=1, source_target_pairs={{4,0},{6,2},{8,4},{10,6},{12,8},{14,10},{16,12},{18,14},{20,16},{2... | collective-permute-start | bytes 786440 | tf_op jit(solution)/shard_map/ppermute | solution.py:238
  119.0 14.7 %collective-permute-start.5 = (bf16[256,512]{1,0:T(8,128)(2,1)}, bf16[256,512]{1,0:T(8,128)(2,1)}, u32[]{:S(2)}, u32[]{:S(2)}) collective-permute-start(bf16[256,512]{1,0:T(8,128)(2,1)} %copy-done.21), channel_id=1, source_target_pairs={{2,0},{4,2},{6,4},{8,6},{10,8},{12,10},{14,12},{16,14},{18,16},{20... | collective-permute-start | bytes 786440 | tf_op jit(solution)/shard_map/ppermute | solution.py:238
  135.5 1.6 %collective-permute-start.10 = (bf16[512,256]{1,0:T(8,128)(2,1)S(1)}, bf16[512,256]{1,0:T(8,128)(2,1)S(1)}, u32[]{:S(2)}, u32[]{:S(2)}) collective-permute-start(bf16[512,256]{1,0:T(8,128)(2,1)S(1)} %get-tuple-element.42), channel_id=1, source_target_pairs={{0,1},{1,0},{2,3},{3,2},{4,5},{5,4},{6,7},{7,6},{8,9},{9,8},{10,11... | collective-permute-start | bytes 786440 | tf_op jit(solution)/shard_map/ppermute | solution.py:317

commit v4 on v3

--- a/solution.py
+++ b/solution.py
@@ -12,9 +12,10 @@
 FORE = STOPS // 2
 BACK = STOPS - 1 - FORE
 OFFSETS = tuple(range(1, FORE + 1)) + tuple(range(-1, -BACK - 1, -1))
-VMEM = 24 << 20
+VMEM = 12 << 20
 BF = jnp.bfloat16
 F32 = jnp.float32
+VM, HM = pltpu.VMEM, pltpu.HBM
 
 
 def iota(shape, dim):
@@ -28,6 +29,13 @@
     ).astype(jnp.int32)
 
 
+def as_row(col):
+    n = col.shape[0]
+    return jnp.sum(
+        jnp.where(iota((n, n), 0) == iota((n, n), 1), col.astype(F32), 0.0), axis=0, keepdims=True
+    ).astype(jnp.int32)
+
+
 def hot(index, shape, dim):
     return jnp.where(iota(shape, dim) == index, 1.0, 0.0).astype(BF)
 
@@ -49,7 +57,7 @@
     return top, (x - top.astype(F32)).astype(BF)
 
 
-def ask_kernel(owner_ref, row_ref, asked_ref, pos_ref):
+def ask_kernel(me_ref, owner_ref, row_ref, asked_ref, pos_ref):
     shards, cap = asked_ref.shape
     heads = owner_ref.shape[1]
     owner = owner_ref[...]
@@ -77,10 +85,14 @@
     out_ref[...] = dot(pick, entity_ref[...]).astype(BF)
 
 
+def wanted_column(wanted_ref):
+    return jnp.concatenate(
+        [column(wanted_ref[s : s + 1, :]) for s in range(wanted_ref.shape[0])], axis=0
+    )
+
+
 def serve_kernel(wanted_ref, entity_ref, out_ref):
-    shards, cap = wanted_ref.shape
-    cols = jnp.concatenate([column(wanted_ref[s : s + 1, :]) for s in range(shards)], axis=0)
-    pick = hot(cols, (shards * cap, entity_ref.shape[0]), 1)
+    pick = hot(wanted_column(wanted_ref), (out_ref.shape[0], entity_ref.shape[0]), 1)
     out_ref[...] = dot(pick, entity_ref[...]).astype(BF)
 
 
@@ -100,34 +112,23 @@
         q_ref[j * heads : (j + 1) * heads, :] = query.astype(BF)
 
 
-def weigh(q_ref, block_ref, weight, chunk):
-    for at in range(0, q_ref.shape[0], chunk):
-        seen = dot_t(q_ref[at : at + chunk, :], block_ref[...])
-        weight[at : at + chunk, :] = (jax.nn.sigmoid(seen) / STOPS).astype(BF)
-
-
-def visit_kernel(chunk, q_ref, block_ref, weight, term):
-    weigh(q_ref, block_ref, weight, chunk)
-    term[...] = t_dot(weight[...], q_ref[...]).astype(term.dtype)
-
-
-def pair_kernel(q_ref, qrel_ref, tail_ref, ent_ref, own_ref, *refs):
-    others = STOPS - 1
-    weights, blocks = refs[:others], refs[others : 2 * others]
-    pw_ref, pair_ref, term, weight, gq = refs[2 * others :]
+def pair_kernel(q_ref, qrel_ref, tail_ref, ent_ref, *refs):
+    blocks, refs = refs[:STOPS], refs[STOPS:]
+    weights, (pw_ref, pair_ref, gq) = refs[:STOPS], refs[STOPS:]
     per, heads = qrel_ref.shape
     ents = ent_ref.shape[0]
-    weigh(q_ref, own_ref, weight, heads)
-    term[...] = t_dot(weight[...], q_ref[...])
     for j in range(per):
         here = slice(j * heads, (j + 1) * heads)
+        query = q_ref[here, :]
         tail = dot(hot(column(tail_ref[j : j + 1, :]), (heads, ents), 1), ent_ref[...])
-        score = jnp.sum(q_ref[here, :].astype(F32) * tail, axis=1, keepdims=True)
+        score = jnp.sum(query.astype(F32) * tail, axis=1, keepdims=True)
         pw = jax.nn.sigmoid(score) - 1.0
         pw_ref[j] = pw
-        total = pw * tail + dot(weight[here, :], own_ref[...])
-        for one, block in zip(weights, blocks):
-            total = total + dot(one[here, :], block[...])
+        total = pw * tail
+        for weight, block in zip(weights, blocks):
+            w = (jax.nn.sigmoid(dot_t(query, block[...])) / STOPS).astype(BF)
+            weight[here, :] = w
+            total = total + dot(w, block[...])
         gq[j] = total
     kinds = [column(qrel_ref[j : j + 1, :]) for j in range(per)]
     for k in range(pair_ref.shape[0]):
@@ -137,26 +138,42 @@
         pair_ref[k] = total.astype(BF)
 
 
+def term_kernel(q_ref, weight_ref, term):
+    term[...] = t_dot(weight_ref[...], q_ref[...]).astype(term.dtype)
+
+
+def reversed_bits(value, count):
+    return int("0" + format(value, "b").zfill(count)[::-1][:count], 2) if count else 0
+
+
 def rel_kernel(step, first, outer, me_ref, vec_ref, pair_ref, keep, send, turned, side):
-    count, half = keep.shape[:2]
+    count, half, width = keep.shape
     inner = 1 - outer
-    me = me_ref[0]
-    bits = (me % 2, (me // 2) % 2)
+    bits = (width // step // 4).bit_length() - 1
     turned[...] = vec_ref[...].astype(F32).T
-    lines = half // 2 // step
-    for flips in range(4):
-        flip = (flips // 2, flips % 2)
-        bit = [0, 0]
-        bit[outer] = (bits[outer] + flip[0]) % 2
-        bit[inner] = (bits[inner] + flip[1]) % 2
-        for z in range(lines):
-            block = z * 4 + bit[1] * 2 + bit[0]
-            at = (flips * lines + z) * step
-            side[at : at + step, :] = turned[pl.ds(pl.multiple_of(block * step, step), step), :]
+    for at in range(width // step):
+        flips, line = divmod(at, 1 << bits)
+        mask = (flips // 2) << outer | (flips % 2) << inner | reversed_bits(line, bits) << 2
+        block = me_ref[0] ^ mask
+        side[at * step : (at + 1) * step, :] = turned[
+            pl.ds(pl.multiple_of(block * step, step), step), :
+        ]
     for k in range(count):
         send[k] = dot(side[half:, :].astype(BF), pair_ref[first + k]).astype(BF)
     for k in range(count):
         keep[k] = dot(side[:half, :].astype(BF), pair_ref[first + k])
+
+
+def fold_kernel(parts, *refs):
+    keeps, gots, refs = refs[:parts], refs[parts : 2 * parts], refs[2 * parts :]
+    for n in range(parts):
+        count = keeps[n].shape[0]
+        rows = slice(n * count, (n + 1) * count)
+        total = keeps[n][...] + gots[n][...].astype(F32)
+        half = refs[0].shape[1]
+        refs[0][rows] = total[:, :half]
+        if len(refs) > 1:
+            refs[1][rows] = total[:, half:].astype(BF)
 
 
 def head_kernel(pos_ref, pair_ref, rel_ref, bucket_ref):
@@ -168,7 +185,7 @@
     bucket_ref[...] = dot(hot(pos_ref[...], (slots, heads), 0), head.astype(BF)).astype(BF)
 
 
-def tail_kernel(tail_ref, q_ref, pw_ref, out_ref):
+def tail_kernel(tail_ref, q_ref, pw_ref, weight_ref, wanted_ref, out_ref, term, row_ref):
     ents, heads = out_ref.shape[0], tail_ref.shape[1]
     total = jnp.zeros(out_ref.shape, F32)
     for j in range(tail_ref.shape[0]):
@@ -176,6 +193,8 @@
         top, rest = halves(pw_ref[j] * q_ref[j * heads : (j + 1) * heads, :].astype(F32))
         total = total + dot(spot, top) + dot(spot, rest)
     out_ref[...] = total
+    term[...] = t_dot(weight_ref[...], q_ref[...])
+    row_ref[...] = as_row(wanted_column(wanted_ref))
 
 
 def sum_kernel(reps, me_ref, wanted_ref, neg_ref, returned_ref, base_ref, *refs):
@@ -204,21 +223,25 @@
         out[...] = pick((rep + shift + 1) % reps).astype(BF)
 
 
-def kernel(body, outs, scratch=(), smem=0):
+def kernel(body, outs, scratch=(), smem=0, limit=VMEM):
     def call(*args):
-        specs = [
-            pl.BlockSpec(memory_space=pltpu.SMEM if i < smem else pltpu.VMEM) for i in range(len(args))
-        ]
         return pl.pallas_call(
             body,
-            out_shape=[jax.ShapeDtypeStruct(s, d) for s, d in outs],
-            in_specs=specs,
+            out_shape=[o[2](*o[:2]) if len(o) > 2 else jax.ShapeDtypeStruct(*o) for o in outs],
+            in_specs=[
+                pl.BlockSpec(memory_space=pltpu.SMEM if i < smem else pltpu.VMEM)
+                for i in range(len(args))
+            ],
             out_specs=[pl.BlockSpec(memory_space=pltpu.VMEM)] * len(outs),
             scratch_shapes=[pltpu.VMEM(s, d) for s, d in scratch],
-            compiler_params=pltpu.CompilerParams(vmem_limit_bytes=VMEM),
+            compiler_params=pltpu.CompilerParams(vmem_limit_bytes=limit),
         )(*args)
 
     return call
+
+
+def far(value):
+    return pltpu.with_memory_space_constraint(value, pltpu.HBM)
 
 
 def per_device(entity, relation, head_owner, head_row, query_rel, tail_row, neg_row):
@@ -247,39 +270,31 @@
 
     owner_row = head_owner.reshape(1, heads)
     qrel, tail = query_rel.T, tail_row.T
-    (own_block,) = kernel(take_kernel, [((rows, width), BF)])(neg_row, entity)
+    (own_block,) = kernel(take_kernel, [((rows, width), BF, HM)], limit=None)(neg_row, entity)
     blocks = [own_block] + [moved(own_block, o) for o in OFFSETS]
-    asked, pos = kernel(ask_kernel, [((shards, cap), jnp.int32), ((1, heads), jnp.int32)])(
-        owner_row, head_row.reshape(1, heads)
+    asked, pos = kernel(ask_kernel, [((shards, cap), jnp.int32), ((1, heads), jnp.int32)], limit=None, smem=1)(
+        me, owner_row,
+        head_row.reshape(1, heads),
     )
     wanted = dealt(asked)
-    (served,) = kernel(serve_kernel, [((slots, width), BF)])(wanted, entity)
+    (served,) = kernel(serve_kernel, [((slots, width), BF, HM)], limit=None)(wanted, entity)
     fetched = dealt(served.reshape(shards, cap, width)).reshape(slots, width)
 
     many = per * heads
     vec, queries = kernel(
-        query_kernel, [((heads, width), BF), ((many, width), BF)], [((rels, heads, width), F32)]
+        query_kernel, [((heads, width), BF, VM), ((many, width), BF, VM)], [((rels, heads, width), F32)]
     )(pos, qrel, fetched, relation)
-    weights, back = [], []
-    for n, offset in enumerate(OFFSETS):
-        weight, term = kernel(
-            functools.partial(visit_kernel, heads), [((many, rows), BF), ((rows, width), BF)]
-        )(queries, blocks[n + 1])
-        weights.append(weight)
-        back.append(moved(term, -offset))
-    pos_weight, pair, own_term = kernel(
-        pair_kernel,
-        [((per, heads, 1), F32), ((rels, heads, width), BF), ((rows, width), F32)],
-        [((many, rows), BF), ((per, heads, width), F32)],
-    )(queries, qrel, tail, entity, own_block, *weights, *blocks[1:])
-    back = [own_term] + back
+    outs = [((many, rows), BF, HM)] * STOPS + [((per, heads, 1), F32, HM), ((rels, heads, width), BF, VM)]
+    *weights, pos_weight, pair = kernel(pair_kernel, outs, [((per, heads, width), F32)])(
+        queries, qrel, tail, entity, *blocks
+    )
 
     part = (rels // 2, width // 2, width)
 
     def relations(first, outer):
         return kernel(
             functools.partial(rel_kernel, step, first, outer),
-            [(part, F32), (part, BF)],
+            [(part, F32, HM), (part, BF, HM)],
             [((width, heads), F32)] * 2,
             smem=1,
         )(me, vec, pair)
@@ -288,29 +303,40 @@
     got_a = flipped(send_a, 1)
     keep_b, send_b = relations(rels // 2, 1)
     got_b = flipped(send_b, 2)
-    (buckets,) = kernel(head_kernel, [((slots, width), BF)])(pos, pair, relation)
+    (buckets,) = kernel(head_kernel, [((slots, width), BF, HM)])(pos, pair, relation)
     returned = dealt(buckets.reshape(shards, cap, width)).reshape(slots, width)
-    (base,) = kernel(tail_kernel, [((ents, width), F32)])(tail, queries, pos_weight)
-
-    quarter = width // 4
-    sum_a = keep_a + got_a.astype(F32)
-    sum_b = keep_b + got_b.astype(F32)
-    next_a, next_b = sum_a[:, quarter:].astype(BF), sum_b[:, quarter:].astype(BF)
-    more_a = flipped(next_a, 2)
-    more_b = flipped(next_b, 1)
-    sum_a = sum_a[:, :quarter] + more_a.astype(F32)
-    sum_b = sum_b[:, :quarter] + more_b.astype(F32)
-    both = jnp.concatenate([sum_a, sum_b]).astype(BF).reshape(rels, lines, step, width)
-    both = both.transpose(1, 0, 2, 3)
-    lined = dealt(both, [[c + 4 * z for z in range(lines)] for c in range(4)])
-    grad_rel = jnp.sum(lined.astype(F32), axis=0)
+    back = []
+    for n, offset in enumerate(OFFSETS):
+        (term,) = kernel(term_kernel, [((rows, width), BF, HM)])(queries, weights[n + 1])
+        back.append(moved(term, -offset))
+    base, own_term, wanted_row = kernel(
+        tail_kernel, [((ents, width), F32, HM), ((rows, width), F32, HM), ((1, slots), jnp.int32)]
+    )(tail, queries, pos_weight, weights[0], wanted)
+    back = [own_term] + back
+
+    def fold(keeps, gots):
+        count, size = len(keeps) * keeps[0].shape[0], keeps[0].shape[1]
+        outs = [((count, size, width), F32)]
+        if size > step:
+            outs = [((count, size // 2, width), F32), ((count, size // 2, width), BF, HM)]
+        return kernel(functools.partial(fold_kernel, len(keeps)), outs)(*keeps, *gots)
+
+    keep_a, send_a = fold([keep_a], [got_a])
+    more_a = flipped(send_a, 2)
+    keep_b, send_b = fold([keep_b], [got_b])
+    more_b = flipped(send_b, 1)
+    keep, *send = fold([keep_a, keep_b], [more_a, more_b])
+    for n in range(lines.bit_length() - 1):
+        got = flipped(send[0], 4 << n)
+        keep, *send = fold([keep], [got])
+    grad_rel = keep
 
     chunk = width // reps
     own, *others = kernel(
         functools.partial(sum_kernel, reps),
         [((ents, chunk), F32)] + [((ents, chunk), BF)] * (reps - 1),
         smem=1,
-    )(me, wanted.reshape(1, slots), neg_row, returned, base, *back)
+    )(me, wanted_row, neg_row, *[far(value) for value in (returned, base, *back)])
     grad_entity = own
     for shift, other in enumerate(others):
         route = [(i, (i + shift + 1) % reps) for i in range(reps)]

time: 142 us -> 137 us (0.965)
  Pallas kernels: 25.9 us -> 37.5 us
  local copies, waits for them, and re-layouts: 11 us -> 5.14 us
  other arithmetic: 7.18 us -> 1.49 us
  starting transfers between devices: 35.6 us -> 31.3 us
    pallas_call x15 -> x20, Pallas kernels: 25.9 us -> 37.5 us  [call(): pl.pallas_call(body, out_shape=[o[2](*o[:2]) if len(o) > 2 else jax.Shape...]
    unnamed x44 -> x54, local copies, waits for them, and re-layouts: 10.4 us -> 5.14 us
    all_to_all x3 -> x2, starting transfers between devices: 12.6 us -> 8.48 us  [dealt(): lax.all_to_all(value, 'blk', split_axis=0, concat_axis=0, tiled=True, axi...]
    add x2 -> x0, other arithmetic: 2.74 us -> none  [the longest x1 1.53 us: per_device(): sum_a = keep_a + got_a.astype(F32)]
    ppermute x10, starting transfers between devices: 18.3 us -> 16.2 us  [moved(): lax.ppermute(value, 'blk', [((i - distance) % shards, i) for i in range(s...]
    ppermute x4 -> x6, starting transfers between devices: 4.59 us -> 6.47 us  [flipped(): return lax.ppermute(value, 'blk', [(i, i ^ bit) for i in range(shards)])]
    reduce_sum x1 -> x0, other arithmetic: 1.84 us -> none  [per_device(): grad_rel = jnp.sum(lined.astype(F32), axis=0)]
    ppermute x1, waiting for transfers between devices: 1.52 us -> 0.01 us  [per_device(): grad_entity = grad_entity + lax.ppermute(other, 'rep', route).astype(F32)]
  transfers between devices with their start and end apart: 18 -> 19, of which waited for: 8 -> 4; matrix products, arithmetic and copies ran while one was open for 4% -> 0% of each run, Pallas kernels for 11% -> 18%
where the time goes in v4:
time: 137 us; the launch traced here: 136 us
  waiting for transfers between devices  44 us (32%)
  Pallas kernels  37.5 us (27%)
  starting transfers between devices  31.3 us (23%)
  blocking collectives  15.7 us (11%)
  local copies, waits for them, and re-layouts  5.14 us (4%)
  other arithmetic  1.49 us (1%)
    pallas_call x20, Pallas kernels, call(): pl.pallas_call(body, out_shape=[o[2](*o[:2]) if len(o) > 2 else jax.Shape...  37.5 us
    all_to_all x2, waiting for transfers between devices, dealt(): lax.all_to_all(value, 'blk', split_axis=0, concat_axis=0, tiled=True, axi...  22 us
    ppermute x10, starting transfers between devices, moved(): lax.ppermute(value, 'blk', [((i - distance) % shards, i) for i in range(s...  16.2 us
    all_to_all x1, blocking collectives, dealt(): lax.all_to_all(value, 'blk', split_axis=0, concat_axis=0, tiled=True, axi...  15.7 us
    ppermute x6, waiting for transfers between devices, flipped(): return lax.ppermute(value, 'blk', [(i, i ^ bit) for i in range(shards)])  12.3 us
    ppermute x10, waiting for transfers between devices, moved(): lax.ppermute(value, 'blk', [((i - distance) % shards, i) for i in range(s...  9.76 us
    all_to_all x2, starting transfers between devices, dealt(): lax.all_to_all(value, 'blk', split_axis=0, concat_axis=0, tiled=True, axi...  8.48 us
    ppermute x6, starting transfers between devices, flipped(): return lax.ppermute(value, 'blk', [(i, i ^ bit) for i in range(shards)])  6.47 us
  transfers between devices with their start and end apart: 19, of which 4 were waited for; matrix products, arithmetic and copies ran while one was open for 0% of the time, Pallas kernels for 18%

profile of v4, /device:TPU:0, one launch (start us, length us, event | category | flops | bytes accessed | tf_op | source)
XLA Modules:
  0.0 136.0 jit_solution(6947276334133457062)
XLA Ops:
  0.7 0.6 pad_add_fusion.me_ref
  1.3 1.6 %shard_map.86 = (s32[16,32]{1,0:T(8,128)}, s32[1,256]{1,0:T(1,128)}) custom-call(s32[2]{0:T(128)} %pad_add_fusion.me_ref, s32[1,256]{1,0:T(1,128)} %bitcast.25, s32[1,256]{1,0:T(1,128)} %bitcast.26), custom_call_target="tpu_custom_call" | custom-call | tf_op jit(solution)/shard_map/pallas_call | solution.py:228
  2.9 15.7 %all_to_all.21 = s32[16,1,32]{2,1,0:T(1,128)} all-to-all(s32[16,1,32]{2,1,0:T(1,128)} %bitcast.24), channel_id=1, replica_groups=mesh['blk'=16,'rep'=2] {'blk'}, dimensions={0} | all-to-all | bytes 4096 | tf_op jit(solution)/shard_map/all_to_all | solution.py:267
  18.6 2.5 %shard_map.87 = bf16[512,512]{1,0:T(8,128)(2,1)} custom-call(s32[16,32]{1,0:T(8,128)} %bitcast.15, bf16[512,512]{1,0:T(8,128)(2,1)} %ent_ref.1), custom_call_target="tpu_custom_call" | custom-call | tf_op jit(solution)/shard_map/pallas_call | solution.py:228
  21.1 3.7 %all-to-all-start.1 = ((bf16[16,32,512]{2,1,0:T(8,128)(2,1)}), bf16[16,32,512]{2,1,0:T(8,128)(2,1)S(1)}, u32[]{:S(2)}, u32[]{:S(2)}) async-start(bf16[16,32,512]{2,1,0:T(8,128)(2,1)} %bitcast.21), calls=%async_computation.1 | async-start | bytes 1048576 | tf_op jit(solution)/shard_map/all_to_all | solution.py:267
  24.8 2.1 %shard_map.89.refs_0_ = bf16[256,512]{1,0:T(8,128)(2,1)} custom-call(s32[1,256]{1,0:T(1,128)} %neg_ref.1, bf16[512,512]{1,0:T(8,128)(2,1)} %ent_ref.1), custom_call_target="tpu_custom_call" | custom-call | tf_op jit(solution)/shard_map/pallas_call | solution.py:228
  26.9 4.6 %collective-permute-start.4 = (bf16[256,512]{1,0:T(8,128)(2,1)}, bf16[256,512]{1,0:T(8,128)(2,1)S(1)}, u32[]{:S(2)}, u32[]{:S(2)}) collective-permute-start(bf16[256,512]{1,0:T(8,128)(2,1)} %shard_map.89.refs_0_), channel_id=1, source_target_pairs={{4,0},{6,2},{8,4},{10,6},{12,8},{14,10},{16,12},{18,14},{20,16},{2... | collective-permute-start | bytes 786440 | tf_op jit(solution)/shard_map/ppermute | solution.py:261
  31.5 1.5 %collective-permute-start.3 = (bf16[256,512]{1,0:T(8,128)(2,1)}, bf16[256,512]{1,0:T(8,128)(2,1)}, u32[]{:S(2)}, u32[]{:S(2)}) collective-permute-start(bf16[256,512]{1,0:T(8,128)(2,1)} %shard_map.89.refs_0_), channel_id=1, source_target_pairs={{2,0},{4,2},{6,4},{8,6},{10,8},{12,10},{14,12},{16,14},{18,16},{20... | collective-permute-start | bytes 786440 | tf_op jit(solution)/shard_map/ppermute | solution.py:261
  33.0 0.0 collective-permute-start.2
  33.0 1.5 %collective-permute-start.1 = (bf16[256,512]{1,0:T(8,128)(2,1)}, bf16[256,512]{1,0:T(8,128)(2,1)}, u32[]{:S(2)}, u32[]{:S(2)}) collective-permute-start(bf16[256,512]{1,0:T(8,128)(2,1)} %shard_map.89.refs_0_), channel_id=1, source_target_pairs={{28,0},{30,2},{0,4},{2,6},{4,8},{6,10},{8,12},{10,14},{12,16},{14,... | collective-permute-start | bytes 786440 | tf_op jit(solution)/shard_map/ppermute | solution.py:261
  34.5 0.1 collective-permute-start
  34.6 22.0 %all-to-all-done.1 = bf16[16,32,512]{2,1,0:T(8,128)(2,1)S(1)} async-done(((bf16[16,32,512]{2,1,0:T(8,128)(2,1)}), bf16[16,32,512]{2,1,0:T(8,128)(2,1)S(1)}, u32[]{:S(2)}, u32[]{:S(2)}) %all-to-all-start.1) | async-done | bytes 524320 | tf_op jit(solution)/shard_map/all_to_all | solution.py:267
  56.6 0.8 copy-done.2
  57.4 1.0 copy-done.3
  58.5 1.2 shard_map.88
  59.7 0.0 collective-permute-done.4.refs_5_
  59.7 0.0 collective-permute-done.3.refs_4_
  59.7 0.0 collective-permute-done.refs_1_
  59.8 0.0 copy-start.1
  59.8 1.0 copy-done.1
  60.8 6.8 %shard_map.90 = (bf16[1024,256]{1,0:T(8,128)(2,1)}, bf16[1024,256]{1,0:T(8,128)(2,1)}, bf16[1024,256]{1,0:T(8,128)(2,1)}, bf16[1024,256]{1,0:T(8,128)(2,1)}, bf1...) custom-call(bf16[1024,512]{1,0:T(8,128)(2,1)S(1)} %get-tuple-element, ...), custom_call_target="tpu_custom_call" | custom-call | tf_op jit(solution)/shard_map/pallas_call | solution.py:228
  67.6 2.2 %shard_map.99 = (f32[2,256,512]{2,1,0:T(8,128)}, bf16[2,256,512]{2,1,0:T(8,128)(2,1)}) custom-call(s32[2]{0:T(128)S(1)} %copy-done.17, bf16[256,512]{1,0:T(8,128)(2,1)S(1)} %get-tuple-element.47.vec_ref, bf16[4,256,512]{2,1,0:T(8,128)(2,1)S(1)} %get-tuple-element.37.pair_ref), custom_call_target="tpu_custom_call" | custom-call | tf_op jit(solution)/shard_map/pallas_call | solution.py:228
  69.8 2.2 %shard_map.101 = (f32[2,256,512]{2,1,0:T(8,128)}, bf16[2,256,512]{2,1,0:T(8,128)(2,1)}) custom-call(s32[2]{0:T(128)S(1)} %copy-done.17, bf16[256,512]{1,0:T(8,128)(2,1)S(1)} %get-tuple-element.47.vec_ref, bf16[4,256,512]{2,1,0:T(8,128)(2,1)S(1)} %get-tuple-element.37.pair_ref), custom_call_target="tpu_custom_call" | custom-call | tf_op jit(solution)/shard_map/pallas_call | solution.py:228
  71.9 0.9 collective-permute-start.12
  72.9 1.8 %shard_map.92 = bf16[512,512]{1,0:T(8,128)(2,1)} custom-call(s32[1,256]{1,0:T(1,128)S(1)} %copy-done.19, bf16[4,256,512]{2,1,0:T(8,128)(2,1)S(1)} %get-tuple-element.37.pair_ref, bf16[4,512,512]{2,1,0:T(8,128)(2,1)S(1)} %copy-done), custom_call_target="tpu_custom_call" | custom-call | tf_op jit(solution)/shard_map/pallas_call | solution.py:228
  74.7 4.8 %all-to-all-start.2 = ((bf16[16,32,512]{2,1,0:T(8,128)(2,1)}), bf16[16,32,512]{2,1,0:T(8,128)(2,1)S(1)}, u32[]{:S(2)}, u32[]{:S(2)}) async-start(bf16[16,32,512]{2,1,0:T(8,128)(2,1)} %bitcast.23), calls=%async_computation.2 | async-start | bytes 1048576 | tf_op jit(solution)/shard_map/all_to_all | solution.py:267
  79.5 1.2 copy-done.6
  80.7 1.9 %shard_map.100 = (f32[2,128,512]{2,1,0:T(8,128)S(1)}, bf16[2,128,512]{2,1,0:T(8,128)(2,1)}) custom-call(f32[2,256,512]{2,1,0:T(8,128)S(1)} %copy-done.6, bf16[2,256,512]{2,1,0:T(8,128)(2,1)} %collective-permute-done.11.refs_1_), custom_call_target="tpu_custom_call" | custom-call | tf_op jit(solution)/shard_map/pallas_call | solution.py:228
  82.6 2.0 %collective-permute-start.13 = (bf16[2,128,512]{2,1,0:T(8,128)(2,1)}, bf16[2,128,512]{2,1,0:T(8,128)(2,1)S(1)}, u32[]{:S(2)}, u32[]{:S(2)}) collective-permute-start(bf16[2,128,512]{2,1,0:T(8,128)(2,1)} %get-tuple-element.54), channel_id=1, source_target_pairs={{0,4},{2,6},{4,0},{6,2},{8,12},{10,14},{12,8},{14,10},{16,20},{18,... | collective-permute-start | bytes 786440 | tf_op jit(solution)/shard_map/ppermute | solution.py:264
  84.6 4.6 %collective-permute-done.12.refs_1_ = bf16[2,256,512]{2,1,0:T(8,128)(2,1)} collective-permute-done((bf16[2,256,512]{2,1,0:T(8,128)(2,1)}, bf16[2,256,512]{2,1,0:T(8,128)(2,1)}, u32[]{:S(2)}, u32[]{:S(2)}) %collective-permute-start.12) | collective-permute-done | bytes 524320 | tf_op jit(solution)/shard_map/ppermute | solution.py:264
  89.2 1.8 %shard_map.102 = (f32[2,128,512]{2,1,0:T(8,128)S(1)}, bf16[2,128,512]{2,1,0:T(8,128)(2,1)}) custom-call(f32[2,256,512]{2,1,0:T(8,128)S(1)} %copy-done.5, bf16[2,256,512]{2,1,0:T(8,128)(2,1)} %collective-permute-done.12.refs_1_), custom_call_target="tpu_custom_call" | custom-call | tf_op jit(solution)/shard_map/pallas_call | solution.py:228
  91.0 0.0 collective-permute-start.14
  91.0 1.2 shard_map.97
  92.2 2.6 %collective-permute-start.9 = (bf16[256,512]{1,0:T(8,128)(2,1)}, bf16[256,512]{1,0:T(8,128)(2,1)S(1)}, u32[]{:S(2)}, u32[]{:S(2)}) collective-permute-start(bf16[256,512]{1,0:T(8,128)(2,1)} %shard_map.97), channel_id=1, source_target_pairs={{28,0},{30,2},{0,4},{2,6},{4,8},{6,10},{8,12},{10,14},{12,16},{14,... | collective-permute-start | bytes 786440 | tf_op jit(solution)/shard_map/ppermute | solution.py:261
  94.8 1.2 shard_map.93
  96.0 1.2 shard_map.94
  97.2 1.2 shard_map.95
  98.3 1.2 shard_map.96
  99.5 2.0 %collective-permute-start.8 = (bf16[256,512]{1,0:T(8,128)(2,1)}, bf16[256,512]{1,0:T(8,128)(2,1)S(1)}, u32[]{:S(2)}, u32[]{:S(2)}) collective-permute-start(bf16[256,512]{1,0:T(8,128)(2,1)} %shard_map.96), channel_id=1, source_target_pairs={{30,0},{0,2},{2,4},{4,6},{6,8},{8,10},{10,12},{12,14},{14,16},{16,... | collective-permute-start | bytes 786440 | tf_op jit(solution)/shard_map/ppermute | solution.py:261
  101.5 1.5 %collective-permute-start.7 = (bf16[256,512]{1,0:T(8,128)(2,1)}, bf16[256,512]{1,0:T(8,128)(2,1)S(1)}, u32[]{:S(2)}, u32[]{:S(2)}) collective-permute-start(bf16[256,512]{1,0:T(8,128)(2,1)} %shard_map.95), channel_id=1, source_target_pairs={{6,0},{8,2},{10,4},{12,6},{14,8},{16,10},{18,12},{20,14},{22,16},{... | collective-permute-start | bytes 786440 | tf_op jit(solution)/shard_map/ppermute | solution.py:261
  103.1 0.0 collective-permute-done.13.refs_2_
  103.1 0.6 collective-permute-start.6
  103.7 0.0 collective-permute-done.14.refs_3_
  103.7 1.8 %collective-permute-start.5 = (bf16[256,512]{1,0:T(8,128)(2,1)S(1)}, bf16[256,512]{1,0:T(8,128)(2,1)}, u32[]{:S(2)}, u32[]{:S(2)}) collective-permute-start(bf16[256,512]{1,0:T(8,128)(2,1)S(1)} %copy-done.24), channel_id=1, source_target_pairs={{2,0},{4,2},{6,4},{8,6},{10,8},{12,10},{14,12},{16,14},{18,16},{20... | collective-permute-start | bytes 786440 | tf_op jit(solution)/shard_map/ppermute | solution.py:261
  105.5 0.8 shard_map.103
  106.2 9.7 %collective-permute-done.9.refs_5_ = bf16[256,512]{1,0:T(8,128)(2,1)S(1)} collective-permute-done((bf16[256,512]{1,0:T(8,128)(2,1)}, bf16[256,512]{1,0:T(8,128)(2,1)S(1)}, u32[]{:S(2)}, u32[]{:S(2)}) %collective-permute-start.9) | collective-permute-done | bytes 262176 | tf_op jit(solution)/shard_map/ppermute | solution.py:261
  116.0 2.0 %collective-permute-start.15 = (bf16[4,64,512]{2,1,0:T(8,128)(2,1)}, bf16[4,64,512]{2,1,0:T(8,128)(2,1)S(1)}, u32[]{:S(2)}, u32[]{:S(2)}) collective-permute-start(bf16[4,64,512]{2,1,0:T(8,128)(2,1)} %get-tuple-element.57), channel_id=1, source_target_pairs={{0,8},{2,10},{4,12},{6,14},{8,0},{10,2},{12,4},{14,6},{16,24},{18,... | collective-permute-start | bytes 786440 | tf_op jit(solution)/shard_map/ppermute | solution.py:264
  118.0 2.7 %shard_map.91 = (f32[512,512]{1,0:T(8,128)}, f32[256,512]{1,0:T(8,128)}, s32[1,512]{1,0:T(1,128)S(1)}) custom-call(s32[4,256]{1,0:T(4,128)S(1)} %bitcast.20, bf16[1024,512]{1,0:T(8,128)(2,1)S(1)} %get-tuple-element.33.q_ref, f32[4,256,1]{2,1,0:T(8,128)S(1)} %copy-done.13, bf16[1024,256]{1,0:T(8,128)(2,1)S(1)} %copy-done.12, s32[16,32]{1,0:T(8,128)S(1)} %bitcast.16), custom_call_target="tpu_custom_call" | custom-call | tf_op jit(solution)/shard_map/pallas_call | solution.py:228
  120.6 0.0 collective-permute-done.8.refs_4_
  120.6 0.0 collective-permute-done.7.refs_3_
  120.7 0.0 copy-start.25
  120.7 0.0 collective-permute-done.5.refs_1_
  120.7 0.6 copy-done.22
  121.3 0.1 copy-done.23
  121.4 0.1 copy-done.25
  121.5 0.2 copy-done.20
  121.7 2.7 %shard_map.98 = (f32[512,256]{1,0:T(8,128)S(1)}, bf16[512,256]{1,0:T(8,128)(2,1)S(1)}) custom-call(s32[2]{0:T(128)S(1)} %copy-done.17, s32[1,512]{1,0:T(1,128)S(1)} %get-tuple-element.36.wanted_ref, s32[1,256]{1,0:T(1,128)S(1)} %copy-done.18, bf16[512,512]{1,0:T(8,128)(2,1)} %bitcast.22, f32[512,512]{1,0:T(8,128)} %get-tuple-element.38.base_ref, ...), custom_call_target="tpu_custom_call" | custom-call | tf_op jit(solution)/shard_map/pallas_call | solution.py:228
  124.4 0.1 collective-permute-start.10
  124.4 0.0 collective-permute-done.15.refs_1_
  124.4 0.7 shard_map.104
  125.1 1.6 %collective-permute-start.16 = (bf16[4,32,512]{2,1,0:T(8,128)(2,1)}, bf16[4,32,512]{2,1,0:T(8,128)(2,1)S(1)}, u32[]{:S(2)}, u32[]{:S(2)}) collective-permute-start(bf16[4,32,512]{2,1,0:T(8,128)(2,1)} %get-tuple-element.59), channel_id=1, source_target_pairs={{0,16},{2,18},{4,20},{6,22},{8,24},{10,26},{12,28},{14,30},{16,0},... | collective-permute-start | bytes 393224 | tf_op jit(solution)/shard_map/ppermute | solution.py:264
  126.8 7.7 %collective-permute-done.16.refs_1_ = bf16[4,32,512]{2,1,0:T(8,128)(2,1)S(1)} collective-permute-done((bf16[4,32,512]{2,1,0:T(8,128)(2,1)}, bf16[4,32,512]{2,1,0:T(8,128)(2,1)S(1)}, u32[]{:S(2)}, u32[]{:S(2)}) %collective-permute-start.16) | collective-permute-done | bytes 131104 | tf_op jit(solution)/shard_map/ppermute | solution.py:264
  134.4 0.7 shard_map.105
  135.1 0.8 convert_add_fusion
  (51 shorter events, 0.1 us)
Async XLA Ops:
  0.6 56.8 %copy-start = (bf16[4,512,512]{2,1,0:T(8,128)(2,1)S(1)}, bf16[4,512,512]{2,1,0:T(8,128)(2,1)}, u32[]{:S(2)}) copy-start(bf16[4,512,512]{2,1,0:T(8,128)(2,1)} %rel_ref.3) | copy-start | bytes 6291460
  0.6 56.8 %copy-start.15 = (s32[256,4]{0,1:T(4,128)S(1)}, s32[256,4]{0,1:T(4,128)}, u32[]{:S(2)}) copy-start(s32[256,4]{0,1:T(4,128)} %param.11) | copy-start | bytes 12292
  2.9 54.5 %copy-start.19 = (s32[1,256]{1,0:T(1,128)S(1)}, s32[1,256]{1,0:T(1,128)}, u32[]{:S(2)}) copy-start(s32[1,256]{1,0:T(1,128)} %get-tuple-element.31.pos_ref) | copy-start | bytes 3076
  21.1 38.6 %copy-start.16 = (s32[256,4]{0,1:T(4,128)S(1)}, s32[256,4]{0,1:T(4,128)}, u32[]{:S(2)}) copy-start(s32[256,4]{0,1:T(4,128)} %param.12) | copy-start | bytes 12292
  21.1 35.5 %all-to-all-start.1 = ((bf16[16,32,512]{2,1,0:T(8,128)(2,1)}), bf16[16,32,512]{2,1,0:T(8,128)(2,1)S(1)}, u32[]{:S(2)}, u32[]{:S(2)}) async-start(bf16[16,32,512]{2,1,0:T(8,128)(2,1)} %bitcast.21), calls=%async_computation.1 | async-start | bytes 1048576 | tf_op jit(solution)/shard_map/all_to_all | solution.py:267
  26.9 32.8 %collective-permute-start.4 = (bf16[256,512]{1,0:T(8,128)(2,1)}, bf16[256,512]{1,0:T(8,128)(2,1)S(1)}, u32[]{:S(2)}, u32[]{:S(2)}) collective-permute-start(bf16[256,512]{1,0:T(8,128)(2,1)} %shard_map.89.refs_0_), channel_id=1, source_target_pairs={{4,0},{6,2},{8,4},{10,6},{12,8},{14,10},{16,12},{18,14},{20,16},{2... | collective-permute-start | bytes 786440 | tf_op jit(solution)/shard_map/ppermute | solution.py:261
  31.5 28.2 %collective-permute-start.3 = (bf16[256,512]{1,0:T(8,128)(2,1)}, bf16[256,512]{1,0:T(8,128)(2,1)}, u32[]{:S(2)}, u32[]{:S(2)}) collective-permute-start(bf16[256,512]{1,0:T(8,128)(2,1)} %shard_map.89.refs_0_), channel_id=1, source_target_pairs={{2,0},{4,2},{6,4},{8,6},{10,8},{12,10},{14,12},{16,14},{18,16},{20... | collective-permute-start | bytes 786440 | tf_op jit(solution)/shard_map/ppermute | solution.py:261
  33.0 26.7 %collective-permute-start.2 = (bf16[256,512]{1,0:T(8,128)(2,1)}, bf16[256,512]{1,0:T(8,128)(2,1)}, u32[]{:S(2)}, u32[]{:S(2)}) collective-permute-start(bf16[256,512]{1,0:T(8,128)(2,1)} %shard_map.89.refs_0_), channel_id=1, source_target_pairs={{26,0},{28,2},{30,4},{0,6},{2,8},{4,10},{6,12},{8,14},{10,16},{12,... | collective-permute-start | bytes 786440 | tf_op jit(solution)/shard_map/ppermute | solution.py:261
  33.0 26.7 %collective-permute-start.1 = (bf16[256,512]{1,0:T(8,128)(2,1)}, bf16[256,512]{1,0:T(8,128)(2,1)}, u32[]{:S(2)}, u32[]{:S(2)}) collective-permute-start(bf16[256,512]{1,0:T(8,128)(2,1)} %shard_map.89.refs_0_), channel_id=1, source_target_pairs={{28,0},{30,2},{0,4},{2,6},{4,8},{6,10},{8,12},{10,14},{12,16},{14,... | collective-permute-start | bytes 786440 | tf_op jit(solution)/shard_map/ppermute | solution.py:261
  34.5 25.3 %collective-permute-start = (bf16[256,512]{1,0:T(8,128)(2,1)}, bf16[256,512]{1,0:T(8,128)(2,1)}, u32[]{:S(2)}, u32[]{:S(2)}) collective-permute-start(bf16[256,512]{1,0:T(8,128)(2,1)} %shard_map.89.refs_0_), channel_id=1, source_target_pairs={{30,0},{0,2},{2,4},{4,6},{6,8},{8,10},{10,12},{12,14},{14,16},{16,... | collective-permute-start | bytes 786440 | tf_op jit(solution)/shard_map/ppermute | solution.py:261
  56.6 0.8 copy-start.2
  57.4 1.0 copy-start.3
  58.5 1.3 copy-start.4
  59.7 7.9 %copy-start.17 = (s32[2]{0:T(128)S(1)}, s32[2]{0:T(128)}, u32[]{:S(2)}) copy-start(s32[2]{0:T(128)} %pad_add_fusion.me_ref) | copy-start | bytes 28
  59.8 1.0 copy-start.1
  69.8 9.7 %collective-permute-start.11 = (bf16[2,256,512]{2,1,0:T(8,128)(2,1)}, bf16[2,256,512]{2,1,0:T(8,128)(2,1)}, u32[]{:S(2)}, u32[]{:S(2)}) collective-permute-start(bf16[2,256,512]{2,1,0:T(8,128)(2,1)} %get-tuple-element.49), channel_id=1, source_target_pairs={{0,2},{2,0},{4,6},{6,4},{8,10},{10,8},{12,14},{14,12},{16,18},{18,... | collective-permute-start | bytes 1572872 | tf_op jit(solution)/shard_map/ppermute | solution.py:264
  71.9 17.2 %collective-permute-start.12 = (bf16[2,256,512]{2,1,0:T(8,128)(2,1)}, bf16[2,256,512]{2,1,0:T(8,128)(2,1)}, u32[]{:S(2)}, u32[]{:S(2)}) collective-permute-start(bf16[2,256,512]{2,1,0:T(8,128)(2,1)} %get-tuple-element.52), channel_id=1, source_target_pairs={{0,4},{2,6},{4,0},{6,2},{8,12},{10,14},{12,8},{14,10},{16,20},{18,... | collective-permute-start | bytes 1572872 | tf_op jit(solution)/shard_map/ppermute | solution.py:264
  74.7 14.5 %copy-start.5 = (f32[2,256,512]{2,1,0:T(8,128)S(1)}, f32[2,256,512]{2,1,0:T(8,128)}, u32[]{:S(2)}) copy-start(f32[2,256,512]{2,1,0:T(8,128)} %get-tuple-element.51.refs_0_) | copy-start | bytes 3145732
  74.7 46.0 %all-to-all-start.2 = ((bf16[16,32,512]{2,1,0:T(8,128)(2,1)}), bf16[16,32,512]{2,1,0:T(8,128)(2,1)S(1)}, u32[]{:S(2)}, u32[]{:S(2)}) async-start(bf16[16,32,512]{2,1,0:T(8,128)(2,1)} %bitcast.23), calls=%async_computation.2 | async-start | bytes 1048576 | tf_op jit(solution)/shard_map/all_to_all | solution.py:267
  79.5 1.2 copy-start.6
  80.7 10.3 %copy-start.11 = (bf16[1024,256]{1,0:T(8,128)(2,1)S(1)}, bf16[1024,256]{1,0:T(8,128)(2,1)}, u32[]{:S(2)}) copy-start(bf16[1024,256]{1,0:T(8,128)(2,1)} %get-tuple-element.44.weight_ref) | copy-start | bytes 1572868
  82.6 12.2 %copy-start.10 = (bf16[1024,256]{1,0:T(8,128)(2,1)S(1)}, bf16[1024,256]{1,0:T(8,128)(2,1)}, u32[]{:S(2)}) copy-start(bf16[1024,256]{1,0:T(8,128)(2,1)} %get-tuple-element.40.weight_ref) | copy-start | bytes 1572868
  82.6 20.5 %collective-permute-start.13 = (bf16[2,128,512]{2,1,0:T(8,128)(2,1)}, bf16[2,128,512]{2,1,0:T(8,128)(2,1)S(1)}, u32[]{:S(2)}, u32[]{:S(2)}) collective-permute-start(bf16[2,128,512]{2,1,0:T(8,128)(2,1)} %get-tuple-element.54), channel_id=1, source_target_pairs={{0,4},{2,6},{4,0},{6,2},{8,12},{10,14},{12,8},{14,10},{16,20},{18,... | collective-permute-start | bytes 786440 | tf_op jit(solution)/shard_map/ppermute | solution.py:264
  91.0 5.0 %copy-start.9 = (bf16[1024,256]{1,0:T(8,128)(2,1)S(1)}, bf16[1024,256]{1,0:T(8,128)(2,1)}, u32[]{:S(2)}) copy-start(bf16[1024,256]{1,0:T(8,128)(2,1)} %get-tuple-element.41.weight_ref) | copy-start | bytes 1572868
  91.0 12.7 %collective-permute-start.14 = (bf16[2,128,512]{2,1,0:T(8,128)(2,1)}, bf16[2,128,512]{2,1,0:T(8,128)(2,1)S(1)}, u32[]{:S(2)}, u32[]{:S(2)}) collective-permute-start(bf16[2,128,512]{2,1,0:T(8,128)(2,1)} %get-tuple-element.55), channel_id=1, source_target_pairs={{0,2},{2,0},{4,6},{6,4},{8,10},{10,8},{12,14},{14,12},{16,18},{18,... | collective-permute-start | bytes 786440 | tf_op jit(solution)/shard_map/ppermute | solution.py:264
  92.2 5.0 %copy-start.8 = (bf16[1024,256]{1,0:T(8,128)(2,1)S(1)}, bf16[1024,256]{1,0:T(8,128)(2,1)}, u32[]{:S(2)}) copy-start(bf16[1024,256]{1,0:T(8,128)(2,1)} %get-tuple-element.42.weight_ref) | copy-start | bytes 1572868
  92.2 23.8 %collective-permute-start.9 = (bf16[256,512]{1,0:T(8,128)(2,1)}, bf16[256,512]{1,0:T(8,128)(2,1)S(1)}, u32[]{:S(2)}, u32[]{:S(2)}) collective-permute-start(bf16[256,512]{1,0:T(8,128)(2,1)} %shard_map.97), channel_id=1, source_target_pairs={{28,0},{30,2},{0,4},{2,6},{4,8},{6,10},{8,12},{10,14},{12,16},{14,... | collective-permute-start | bytes 786440 | tf_op jit(solution)/shard_map/ppermute | solution.py:261
  96.0 2.3 %copy-start.7 = (bf16[1024,256]{1,0:T(8,128)(2,1)S(1)}, bf16[1024,256]{1,0:T(8,128)(2,1)}, u32[]{:S(2)}) copy-start(bf16[1024,256]{1,0:T(8,128)(2,1)} %get-tuple-element.43.weight_ref) | copy-start | bytes 1572868
  97.2 5.9 %copy-start.26 = (bf16[256,512]{1,0:T(8,128)(2,1)S(1)}, bf16[256,512]{1,0:T(8,128)(2,1)}, u32[]{:S(2)}) copy-start(bf16[256,512]{1,0:T(8,128)(2,1)} %shard_map.94) | copy-start | bytes 786436
  97.2 6.5 %copy-start.24 = (bf16[256,512]{1,0:T(8,128)(2,1)S(1)}, bf16[256,512]{1,0:T(8,128)(2,1)}, u32[]{:S(2)}) copy-start(bf16[256,512]{1,0:T(8,128)(2,1)} %shard_map.93) | copy-start | bytes 786436
  98.3 19.6 %copy-start.12 = (bf16[1024,256]{1,0:T(8,128)(2,1)S(1)}, bf16[1024,256]{1,0:T(8,128)(2,1)}, u32[]{:S(2)}) copy-start(bf16[1024,256]{1,0:T(8,128)(2,1)} %get-tuple-element.35.weight_ref) | copy-start | bytes 1572868
  98.3 19.6 %copy-start.13 = (f32[4,256,1]{2,1,0:T(8,128)S(1)}, f32[4,256,1]{2,1,0:T(8,128)}, u32[]{:S(2)}) copy-start(f32[4,256,1]{2,1,0:T(8,128)} %get-tuple-element.34.pw_ref) | copy-start | bytes 12292
  98.3 19.6 %copy-start.14 = (s32[16,1,32]{2,1,0:T(1,128)S(1)}, s32[16,1,32]{2,1,0:T(1,128)}, u32[]{:S(2)}) copy-start(s32[16,1,32]{2,1,0:T(1,128)} %all_to_all.21) | copy-start | bytes 6148
  99.5 22.2 %copy-start.18 = (s32[1,256]{1,0:T(1,128)S(1)}, s32[1,256]{1,0:T(1,128)}, u32[]{:S(2)}) copy-start(s32[1,256]{1,0:T(1,128)} %neg_ref.1) | copy-start | bytes 3076
  99.5 21.1 %collective-permute-start.8 = (bf16[256,512]{1,0:T(8,128)(2,1)}, bf16[256,512]{1,0:T(8,128)(2,1)S(1)}, u32[]{:S(2)}, u32[]{:S(2)}) collective-permute-start(bf16[256,512]{1,0:T(8,128)(2,1)} %shard_map.96), channel_id=1, source_target_pairs={{30,0},{0,2},{2,4},{4,6},{6,8},{8,10},{10,12},{12,14},{14,16},{16,... | collective-permute-start | bytes 786440 | tf_op jit(solution)/shard_map/ppermute | solution.py:261
  101.5 19.1 %collective-permute-start.7 = (bf16[256,512]{1,0:T(8,128)(2,1)}, bf16[256,512]{1,0:T(8,128)(2,1)S(1)}, u32[]{:S(2)}, u32[]{:S(2)}) collective-permute-start(bf16[256,512]{1,0:T(8,128)(2,1)} %shard_map.95), channel_id=1, source_target_pairs={{6,0},{8,2},{10,4},{12,6},{14,8},{16,10},{18,12},{20,14},{22,16},{... | collective-permute-start | bytes 786440 | tf_op jit(solution)/shard_map/ppermute | solution.py:261
  103.1 17.6 %collective-permute-start.6 = (bf16[256,512]{1,0:T(8,128)(2,1)S(1)}, bf16[256,512]{1,0:T(8,128)(2,1)S(1)}, u32[]{:S(2)}, u32[]{:S(2)}) collective-permute-start(bf16[256,512]{1,0:T(8,128)(2,1)S(1)} %copy-done.26), channel_id=1, source_target_pairs={{4,0},{6,2},{8,4},{10,6},{12,8},{14,10},{16,12},{18,14},{20,16},{2... | collective-permute-start | bytes 786440 | tf_op jit(solution)/shard_map/ppermute | solution.py:261
  103.7 17.0 %collective-permute-start.5 = (bf16[256,512]{1,0:T(8,128)(2,1)S(1)}, bf16[256,512]{1,0:T(8,128)(2,1)}, u32[]{:S(2)}, u32[]{:S(2)}) collective-permute-start(bf16[256,512]{1,0:T(8,128)(2,1)S(1)} %copy-done.24), channel_id=1, source_target_pairs={{2,0},{4,2},{6,4},{8,6},{10,8},{12,10},{14,12},{16,14},{18,16},{20... | collective-permute-start | bytes 786440 | tf_op jit(solution)/shard_map/ppermute | solution.py:261
  116.0 4.7 %copy-start.21 = (bf16[256,512]{1,0:T(8,128)(2,1)}, bf16[256,512]{1,0:T(8,128)(2,1)S(1)}, u32[]{:S(2)}) copy-start(bf16[256,512]{1,0:T(8,128)(2,1)S(1)} %collective-permute-done.9.refs_5_) | copy-start | bytes 786436
  116.0 8.5 %collective-permute-start.15 = (bf16[4,64,512]{2,1,0:T(8,128)(2,1)}, bf16[4,64,512]{2,1,0:T(8,128)(2,1)S(1)}, u32[]{:S(2)}, u32[]{:S(2)}) collective-permute-start(bf16[4,64,512]{2,1,0:T(8,128)(2,1)} %get-tuple-element.57), channel_id=1, source_target_pairs={{0,8},{2,10},{4,12},{6,14},{8,0},{10,2},{12,4},{14,6},{16,24},{18,... | collective-permute-start | bytes 786440 | tf_op jit(solution)/shard_map/ppermute | solution.py:264
  120.6 0.7 copy-start.22
  120.6 0.8 copy-start.23
  120.7 0.8 copy-start.25
  120.7 1.0 copy-start.20
  124.4 10.8 %collective-permute-start.10 = (bf16[512,256]{1,0:T(8,128)(2,1)S(1)}, bf16[512,256]{1,0:T(8,128)(2,1)S(1)}, u32[]{:S(2)}, u32[]{:S(2)}) collective-permute-start(bf16[512,256]{1,0:T(8,128)(2,1)S(1)} %get-tuple-element.46), channel_id=1, source_target_pairs={{0,1},{1,0},{2,3},{3,2},{4,5},{5,4},{6,7},{7,6},{8,9},{9,8},{10,11... | collective-permute-start | bytes 786440 | tf_op jit(solution)/shard_map/ppermute | solution.py:343
  125.1 9.3 %collective-permute-start.16 = (bf16[4,32,512]{2,1,0:T(8,128)(2,1)}, bf16[4,32,512]{2,1,0:T(8,128)(2,1)S(1)}, u32[]{:S(2)}, u32[]{:S(2)}) collective-permute-start(bf16[4,32,512]{2,1,0:T(8,128)(2,1)} %get-tuple-element.59), channel_id=1, source_target_pairs={{0,16},{2,18},{4,20},{6,22},{8,24},{10,26},{12,28},{14,30},{16,0},... | collective-permute-start | bytes 393224 | tf_op jit(solution)/shard_map/ppermute | solution.py:264

commit v5 on v4

--- a/solution.py
+++ b/solution.py
@@ -12,7 +12,7 @@
 FORE = STOPS // 2
 BACK = STOPS - 1 - FORE
 OFFSETS = tuple(range(1, FORE + 1)) + tuple(range(-1, -BACK - 1, -1))
-VMEM = 12 << 20
+VMEM, WIDE = 12 << 20, 16 << 20
 BF = jnp.bfloat16
 F32 = jnp.float32
 VM, HM = pltpu.VMEM, pltpu.HBM
@@ -96,14 +96,13 @@
     out_ref[...] = dot(pick, entity_ref[...]).astype(BF)
 
 
-def query_kernel(pos_ref, qrel_ref, fetched_ref, rel_ref, vec_ref, q_ref, prod):
-    heads = vec_ref.shape[0]
-    rels = rel_ref.shape[0]
-    slots = fetched_ref.shape[0]
-    vec = dot(hot(column(pos_ref[...]), (heads, slots), 1), fetched_ref[...]).astype(BF)
-    vec_ref[...] = vec
+def query_kernel(pos_ref, qrel_ref, fetched_ref, rel_ref, turned, q_ref, prod):
+    rels, _ = rel_ref.shape[:2]
+    heads = qrel_ref.shape[1]
+    vec = dot(hot(column(pos_ref[...]), (heads, fetched_ref.shape[0]), 1), fetched_ref[...]).astype(BF)
     for k in range(rels):
         prod[k] = dot(vec, rel_ref[k])
+    turned[...] = vec.astype(F32).T
     for j in range(qrel_ref.shape[0]):
         kind = column(qrel_ref[j : j + 1, :])
         query = prod[0]
@@ -112,56 +111,80 @@
         q_ref[j * heads : (j + 1) * heads, :] = query.astype(BF)
 
 
-def pair_kernel(q_ref, qrel_ref, tail_ref, ent_ref, *refs):
+def reversed_bits(value, count):
+    return int("0" + format(value, "b").zfill(count)[::-1][:count], 2) if count else 0
+
+
+def arrange(step, outer, upper, me, turned, side):
+    width = turned.shape[0]
+    bits = (width // step // 4).bit_length() - 1
+    for at in range(width // step // 2):
+        flip, line = divmod(at, 1 << bits)
+        mask = upper << outer | flip << (1 - outer) | reversed_bits(line, bits) << 2
+        side[at * step : (at + 1) * step, :] = turned[
+            pl.ds(pl.multiple_of((me ^ mask) * step, step), step), :
+        ]
+
+
+def visit_kernel(step, me_ref, turned, q_ref, qrel_ref, tail_ref, ent_ref, *refs):
     blocks, refs = refs[:STOPS], refs[STOPS:]
-    weights, (pw_ref, pair_ref, gq) = refs[:STOPS], refs[STOPS:]
+    pw_ref, pair_ref, *sends = refs[:4]
+    weights, refs = refs[4 : 4 + STOPS], refs[4 + STOPS :]
+    near, weight, gq, side, load_sems, store_sems = refs
     per, heads = qrel_ref.shape
-    ents = ent_ref.shape[0]
+    rels = pair_ref.shape[0]
+    rows = blocks[0].shape[0]
+    loads = [
+        pltpu.make_async_copy(block, near.at[n * rows : (n + 1) * rows], load_sems.at[n])
+        for n, block in enumerate(blocks)
+    ]
+    for load in loads:
+        load.start()
+    kinds = [column(qrel_ref[j : j + 1, :]) for j in range(per)]
     for j in range(per):
         here = slice(j * heads, (j + 1) * heads)
         query = q_ref[here, :]
-        tail = dot(hot(column(tail_ref[j : j + 1, :]), (heads, ents), 1), ent_ref[...])
+        tail = dot(hot(column(tail_ref[j : j + 1, :]), (heads, ent_ref.shape[0]), 1), ent_ref[...])
         score = jnp.sum(query.astype(F32) * tail, axis=1, keepdims=True)
         pw = jax.nn.sigmoid(score) - 1.0
         pw_ref[j] = pw
-        total = pw * tail
-        for weight, block in zip(weights, blocks):
-            w = (jax.nn.sigmoid(dot_t(query, block[...])) / STOPS).astype(BF)
-            weight[here, :] = w
-            total = total + dot(w, block[...])
-        gq[j] = total
-    kinds = [column(qrel_ref[j : j + 1, :]) for j in range(per)]
-    for k in range(pair_ref.shape[0]):
+        gq[j] = pw * tail
+    for load in loads:
+        load.wait()
+    stores = []
+    for j in range(per):
+        here = slice(j * heads, (j + 1) * heads)
+        weight[here, :] = (jax.nn.sigmoid(dot_t(q_ref[here, :], near[...])) / STOPS).astype(BF)
+        gq[j] = gq[j] + dot(weight[here, :], near[...])
+        for n, out in enumerate(weights):
+            stores.append(
+                pltpu.make_async_copy(
+                    weight.at[here, n * rows : (n + 1) * rows], out.at[here], store_sems.at[n, j]
+                )
+            )
+            stores[-1].start()
+    for k in range(rels):
         total = jnp.where(kinds[0] == k, gq[0], 0.0)
         for j in range(1, per):
             total = total + jnp.where(kinds[j] == k, gq[j], 0.0)
         pair_ref[k] = total.astype(BF)
+    for outer, send in enumerate(sends):
+        arrange(step, outer, 1, me_ref[0], turned, side)
+        for k in range(send.shape[0]):
+            send[k] = dot(side[...].astype(BF), pair_ref[outer * send.shape[0] + k]).astype(BF)
+    for store in stores:
+        store.wait()
 
 
 def term_kernel(q_ref, weight_ref, term):
     term[...] = t_dot(weight_ref[...], q_ref[...]).astype(term.dtype)
 
 
-def reversed_bits(value, count):
-    return int("0" + format(value, "b").zfill(count)[::-1][:count], 2) if count else 0
-
-
-def rel_kernel(step, first, outer, me_ref, vec_ref, pair_ref, keep, send, turned, side):
-    count, half, width = keep.shape
-    inner = 1 - outer
-    bits = (width // step // 4).bit_length() - 1
-    turned[...] = vec_ref[...].astype(F32).T
-    for at in range(width // step):
-        flips, line = divmod(at, 1 << bits)
-        mask = (flips // 2) << outer | (flips % 2) << inner | reversed_bits(line, bits) << 2
-        block = me_ref[0] ^ mask
-        side[at * step : (at + 1) * step, :] = turned[
-            pl.ds(pl.multiple_of(block * step, step), step), :
-        ]
-    for k in range(count):
-        send[k] = dot(side[half:, :].astype(BF), pair_ref[first + k]).astype(BF)
-    for k in range(count):
-        keep[k] = dot(side[:half, :].astype(BF), pair_ref[first + k])
+def keep_kernel(step, me_ref, turned, pair_ref, keep_a, keep_b, side):
+    for outer, keep in enumerate((keep_a, keep_b)):
+        arrange(step, outer, 0, me_ref[0], turned, side)
+        for k in range(keep.shape[0]):
+            keep[k] = dot(side[...].astype(BF), pair_ref[outer * keep.shape[0] + k])
 
 
 def fold_kernel(parts, *refs):
@@ -223,17 +246,24 @@
         out[...] = pick((rep + shift + 1) % reps).astype(BF)
 
 
-def kernel(body, outs, scratch=(), smem=0, limit=VMEM):
+def kernel(body, outs, scratch=(), smem=0, limit=VMEM, wild=0, wild_outs=0):
     def call(*args):
+        count = len(args)
+
+        def place(i):
+            if i < smem:
+                return pltpu.SMEM
+            return pl.ANY if i >= count - wild else pltpu.VMEM
+
         return pl.pallas_call(
             body,
             out_shape=[o[2](*o[:2]) if len(o) > 2 else jax.ShapeDtypeStruct(*o) for o in outs],
-            in_specs=[
-                pl.BlockSpec(memory_space=pltpu.SMEM if i < smem else pltpu.VMEM)
-                for i in range(len(args))
+            in_specs=[pl.BlockSpec(memory_space=place(i)) for i in range(count)],
+            out_specs=[
+                pl.BlockSpec(memory_space=pl.ANY if i >= len(outs) - wild_outs else pltpu.VMEM)
+                for i in range(len(outs))
             ],
-            out_specs=[pl.BlockSpec(memory_space=pltpu.VMEM)] * len(outs),
-            scratch_shapes=[pltpu.VMEM(s, d) for s, d in scratch],
+            scratch_shapes=[pltpu.VMEM(*s) if isinstance(s, tuple) else s for s in scratch],
             compiler_params=pltpu.CompilerParams(vmem_limit_bytes=limit),
         )(*args)
 
@@ -281,28 +311,37 @@
     fetched = dealt(served.reshape(shards, cap, width)).reshape(slots, width)
 
     many = per * heads
-    vec, queries = kernel(
-        query_kernel, [((heads, width), BF, VM), ((many, width), BF, VM)], [((rels, heads, width), F32)]
+    turned, queries = kernel(
+        query_kernel,
+        [((width, heads), F32, VM), ((many, width), BF, VM)],
+        [((rels, heads, width), F32)],
     )(pos, qrel, fetched, relation)
-    outs = [((many, rows), BF, HM)] * STOPS + [((per, heads, 1), F32, HM), ((rels, heads, width), BF, VM)]
-    *weights, pos_weight, pair = kernel(pair_kernel, outs, [((per, heads, width), F32)])(
-        queries, qrel, tail, entity, *blocks
+    part = (rels // 2, width // 2, width)
+    side = ((width // 2, heads), F32)
+    pos_weight, pair, send_a, send_b, *weights = kernel(
+        functools.partial(visit_kernel, step),
+        [((per, heads, 1), F32, HM), ((rels, heads, width), BF, VM)]
+        + [(part, BF, HM)] * 2
+        + [((many, rows), BF, HM)] * STOPS,
+        [
+            ((STOPS * rows, width), BF),
+            ((many, STOPS * rows), BF),
+            ((per, heads, width), F32),
+            side,
+            pltpu.SemaphoreType.DMA((STOPS,)),
+            pltpu.SemaphoreType.DMA((STOPS, per)),
+        ],
+        smem=1,
+        wild=STOPS,
+        wild_outs=STOPS,
+        limit=WIDE,
+    )(me, turned, queries, qrel, tail, entity, *[far(block) for block in blocks])
+
+    got_a = flipped(send_a, 1)
+    got_b = flipped(send_b, 2)
+    keep_a, keep_b = kernel(functools.partial(keep_kernel, step), [(part, F32, HM)] * 2, [side], smem=1)(
+        me, turned, pair,
     )
-
-    part = (rels // 2, width // 2, width)
-
-    def relations(first, outer):
-        return kernel(
-            functools.partial(rel_kernel, step, first, outer),
-            [(part, F32, HM), (part, BF, HM)],
-            [((width, heads), F32)] * 2,
-            smem=1,
-        )(me, vec, pair)
-
-    keep_a, send_a = relations(0, 0)
-    got_a = flipped(send_a, 1)
-    keep_b, send_b = relations(rels // 2, 1)
-    got_b = flipped(send_b, 2)
     (buckets,) = kernel(head_kernel, [((slots, width), BF, HM)])(pos, pair, relation)
     returned = dealt(buckets.reshape(shards, cap, width)).reshape(slots, width)
     back = []

time: 137 us -> 134 us (0.978)
  waiting for transfers between devices: 44 us -> 37.6 us
  local copies, waits for them, and re-layouts: 5.14 us -> 7.99 us
    ppermute x6, waiting for transfers between devices: 12.3 us -> 7.64 us  [flipped(): return lax.ppermute(value, 'blk', [(i, i ^ bit) for i in range(shards)])]
    unnamed x54 -> x62, local copies, waits for them, and re-layouts: 5.14 us -> 7.99 us
    ppermute x6, starting transfers between devices: 6.47 us -> 8.03 us  [flipped(): return lax.ppermute(value, 'blk', [(i, i ^ bit) for i in range(shards)])]
    pallas_call x20 -> x19, Pallas kernels: 37.5 us -> 37.3 us  [call(): pl.pallas_call(body, out_shape=[o[2](*o[:2]) if len(o) > 2 else jax.Shape...]
where the time goes in v5:
time: 134 us
  waiting for transfers between devices  37.6 us (28%)
  Pallas kernels  37.3 us (28%)
  starting transfers between devices  32.4 us (24%)
  blocking collectives  15.8 us (12%)
  local copies, waits for them, and re-layouts  7.99 us (6%)
  other arithmetic  1.51 us (1%)
    pallas_call x19, Pallas kernels, call(): pl.pallas_call(body, out_shape=[o[2](*o[:2]) if len(o) > 2 else jax.Shape...  37.3 us
    all_to_all x2, waiting for transfers between devices, dealt(): lax.all_to_all(value, 'blk', split_axis=0, concat_axis=0, tiled=True, axi...  21.2 us
    ppermute x10, starting transfers between devices, moved(): lax.ppermute(value, 'blk', [((i - distance) % shards, i) for i in range(s...  16.1 us
    all_to_all x1, blocking collectives, dealt(): lax.all_to_all(value, 'blk', split_axis=0, concat_axis=0, tiled=True, axi...  15.8 us
    ppermute x10, waiting for transfers between devices, moved(): lax.ppermute(value, 'blk', [((i - distance) % shards, i) for i in range(s...  8.78 us
    all_to_all x2, starting transfers between devices, dealt(): lax.all_to_all(value, 'blk', split_axis=0, concat_axis=0, tiled=True, axi...  8.22 us
    ppermute x6, starting transfers between devices, flipped(): return lax.ppermute(value, 'blk', [(i, i ^ bit) for i in range(shards)])  8.03 us
    unnamed x62, local copies, waits for them, and re-layouts  7.99 us
  transfers between devices with their start and end apart: 19, of which 4 were waited for; matrix products, arithmetic and copies ran while one was open for 0% of the time, Pallas kernels for 18%

profile of v5, /device:TPU:0, one launch (start us, length us, event | category | flops | bytes accessed | tf_op | source)
XLA Modules:
  0.0 133.5 jit_solution(5431805182810407972)
XLA Ops:
  0.7 0.7 pad_add_fusion.me_ref
  1.3 1.6 %shard_map.86 = (s32[16,32]{1,0:T(8,128)}, s32[1,256]{1,0:T(1,128)}) custom-call(s32[2]{0:T(128)} %pad_add_fusion.me_ref, s32[1,256]{1,0:T(1,128)} %bitcast.25, s32[1,256]{1,0:T(1,128)} %bitcast.26), custom_call_target="tpu_custom_call" | custom-call | tf_op jit(solution)/shard_map/pallas_call | solution.py:258
  3.0 15.8 %all_to_all.21 = s32[16,1,32]{2,1,0:T(1,128)} all-to-all(s32[16,1,32]{2,1,0:T(1,128)} %bitcast.24), channel_id=1, replica_groups=mesh['blk'=16,'rep'=2] {'blk'}, dimensions={0} | all-to-all | bytes 4096 | tf_op jit(solution)/shard_map/all_to_all | solution.py:297
  18.8 2.5 %shard_map.87 = bf16[512,512]{1,0:T(8,128)(2,1)} custom-call(s32[16,32]{1,0:T(8,128)} %bitcast.15, bf16[512,512]{1,0:T(8,128)(2,1)} %ent_ref.1), custom_call_target="tpu_custom_call" | custom-call | tf_op jit(solution)/shard_map/pallas_call | solution.py:258
  21.3 3.7 %all-to-all-start.1 = ((bf16[16,32,512]{2,1,0:T(8,128)(2,1)}), bf16[16,32,512]{2,1,0:T(8,128)(2,1)S(1)}, u32[]{:S(2)}, u32[]{:S(2)}) async-start(bf16[16,32,512]{2,1,0:T(8,128)(2,1)} %bitcast.21), calls=%async_computation.1 | async-start | bytes 1048576 | tf_op jit(solution)/shard_map/all_to_all | solution.py:297
  25.0 2.1 %shard_map.89.refs_0_ = bf16[256,512]{1,0:T(8,128)(2,1)} custom-call(s32[1,256]{1,0:T(1,128)} %neg_ref.1, bf16[512,512]{1,0:T(8,128)(2,1)} %ent_ref.1), custom_call_target="tpu_custom_call" | custom-call | tf_op jit(solution)/shard_map/pallas_call | solution.py:258
  27.1 4.6 %collective-permute-start.4 = (bf16[256,512]{1,0:T(8,128)(2,1)}, bf16[256,512]{1,0:T(8,128)(2,1)S(1)}, u32[]{:S(2)}, u32[]{:S(2)}) collective-permute-start(bf16[256,512]{1,0:T(8,128)(2,1)} %shard_map.89.refs_0_), channel_id=1, source_target_pairs={{4,0},{6,2},{8,4},{10,6},{12,8},{14,10},{16,12},{18,14},{20,16},{2... | collective-permute-start | bytes 786440 | tf_op jit(solution)/shard_map/ppermute | solution.py:291
  31.7 1.5 %collective-permute-start.3 = (bf16[256,512]{1,0:T(8,128)(2,1)}, bf16[256,512]{1,0:T(8,128)(2,1)}, u32[]{:S(2)}, u32[]{:S(2)}) collective-permute-start(bf16[256,512]{1,0:T(8,128)(2,1)} %shard_map.89.refs_0_), channel_id=1, source_target_pairs={{2,0},{4,2},{6,4},{8,6},{10,8},{12,10},{14,12},{16,14},{18,16},{20... | collective-permute-start | bytes 786440 | tf_op jit(solution)/shard_map/ppermute | solution.py:291
  33.2 0.0 collective-permute-start.2
  33.2 1.5 %collective-permute-start.1 = (bf16[256,512]{1,0:T(8,128)(2,1)}, bf16[256,512]{1,0:T(8,128)(2,1)}, u32[]{:S(2)}, u32[]{:S(2)}) collective-permute-start(bf16[256,512]{1,0:T(8,128)(2,1)} %shard_map.89.refs_0_), channel_id=1, source_target_pairs={{28,0},{30,2},{0,4},{2,6},{4,8},{6,10},{8,12},{10,14},{12,16},{14,... | collective-permute-start | bytes 786440 | tf_op jit(solution)/shard_map/ppermute | solution.py:291
  34.6 0.1 collective-permute-start
  34.8 21.2 %all-to-all-done.1 = bf16[16,32,512]{2,1,0:T(8,128)(2,1)S(1)} async-done(((bf16[16,32,512]{2,1,0:T(8,128)(2,1)}), bf16[16,32,512]{2,1,0:T(8,128)(2,1)S(1)}, u32[]{:S(2)}, u32[]{:S(2)}) %all-to-all-start.1) | async-done | bytes 524320 | tf_op jit(solution)/shard_map/all_to_all | solution.py:297
  56.0 0.8 copy-done.4
  56.8 1.0 copy-done.5
  57.8 1.2 shard_map.88
  59.0 0.0 collective-permute-done.4.refs_5_
  59.0 0.0 collective-permute-done.3.refs_4_
  59.1 0.0 collective-permute-done.2.refs_3_
  59.1 0.0 collective-permute-done.1.refs_2_
  59.1 0.0 collective-permute-done.refs_1_
  59.1 0.7 copy-done.30
  59.8 1.0 copy-done.1
  60.8 8.8 %shard_map.90 = (f32[4,256,1]{2,1,0:T(8,128)}, bf16[4,256,512]{2,1,0:T(8,128)(2,1)S(1)}, bf16[2,256,512]{2,1,0:T(8,128)(2,1)}, bf16[2,256,512]{2,1,0:T(8,128)(2,...) custom-call(s32[2]{0:T(128)S(1)} %copy-done.20, ...), custom_call_target="tpu_custom_call" | custom-call | tf_op jit(solution)/shard_map/pallas_call | solution.py:258
  69.6 0.1 collective-permute-start.11
  69.7 1.0 collective-permute-start.12
  70.7 1.8 %shard_map.92 = bf16[512,512]{1,0:T(8,128)(2,1)} custom-call(s32[1,256]{1,0:T(1,128)S(1)} %copy-done.22, bf16[4,256,512]{2,1,0:T(8,128)(2,1)S(1)} %get-tuple-element.38.pair_ref, bf16[4,512,512]{2,1,0:T(8,128)(2,1)S(1)} %copy-done), custom_call_target="tpu_custom_call" | custom-call | tf_op jit(solution)/shard_map/pallas_call | solution.py:258
  72.5 4.5 %all-to-all-start.2 = ((bf16[16,32,512]{2,1,0:T(8,128)(2,1)}), bf16[16,32,512]{2,1,0:T(8,128)(2,1)S(1)}, u32[]{:S(2)}, u32[]{:S(2)}) async-start(bf16[16,32,512]{2,1,0:T(8,128)(2,1)} %bitcast.23), calls=%async_computation.2 | async-start | bytes 1048576 | tf_op jit(solution)/shard_map/all_to_all | solution.py:297
  77.0 1.2 copy-done.3
  78.2 1.0 copy-done.7
  79.3 2.2 %shard_map.99 = (f32[2,256,512]{2,1,0:T(8,128)}, f32[2,256,512]{2,1,0:T(8,128)}) custom-call(s32[2]{0:T(128)S(1)} %copy-done.20, f32[512,256]{1,0:T(8,128)S(1)} %copy-done.7, bf16[4,256,512]{2,1,0:T(8,128)(2,1)S(1)} %copy-done.3), custom_call_target="tpu_custom_call" | custom-call | tf_op jit(solution)/shard_map/pallas_call | solution.py:258
  81.5 0.0 collective-permute-done.11.refs_1_
  81.5 1.3 copy-done.9
  82.8 1.8 %shard_map.100 = (f32[2,128,512]{2,1,0:T(8,128)S(1)}, bf16[2,128,512]{2,1,0:T(8,128)(2,1)}) custom-call(f32[2,256,512]{2,1,0:T(8,128)S(1)} %copy-done.9, bf16[2,256,512]{2,1,0:T(8,128)(2,1)} %collective-permute-done.11.refs_1_), custom_call_target="tpu_custom_call" | custom-call | tf_op jit(solution)/shard_map/pallas_call | solution.py:258
  84.6 1.9 %collective-permute-start.13 = (bf16[2,128,512]{2,1,0:T(8,128)(2,1)}, bf16[2,128,512]{2,1,0:T(8,128)(2,1)S(1)}, u32[]{:S(2)}, u32[]{:S(2)}) collective-permute-start(bf16[2,128,512]{2,1,0:T(8,128)(2,1)} %get-tuple-element.54), channel_id=1, source_target_pairs={{0,4},{2,6},{4,0},{6,2},{8,12},{10,14},{12,8},{14,10},{16,20},{18,... | collective-permute-start | bytes 786440 | tf_op jit(solution)/shard_map/ppermute | solution.py:294
  86.6 0.0 collective-permute-done.12.refs_1_
  86.6 1.8 %shard_map.101 = (f32[2,128,512]{2,1,0:T(8,128)S(1)}, bf16[2,128,512]{2,1,0:T(8,128)(2,1)}) custom-call(f32[2,256,512]{2,1,0:T(8,128)S(1)} %copy-done.8, bf16[2,256,512]{2,1,0:T(8,128)(2,1)} %collective-permute-done.12.refs_1_), custom_call_target="tpu_custom_call" | custom-call | tf_op jit(solution)/shard_map/pallas_call | solution.py:258
  88.4 2.1 %collective-permute-start.14 = (bf16[2,128,512]{2,1,0:T(8,128)(2,1)}, bf16[2,128,512]{2,1,0:T(8,128)(2,1)S(1)}, u32[]{:S(2)}, u32[]{:S(2)}) collective-permute-start(bf16[2,128,512]{2,1,0:T(8,128)(2,1)} %get-tuple-element.55), channel_id=1, source_target_pairs={{0,2},{2,0},{4,6},{6,4},{8,10},{10,8},{12,14},{14,12},{16,18},{18,... | collective-permute-start | bytes 786440 | tf_op jit(solution)/shard_map/ppermute | solution.py:294
  90.5 1.2 shard_map.97
  91.7 0.1 collective-permute-start.9
  91.8 1.2 shard_map.93
  93.0 1.2 shard_map.94
  94.1 1.2 shard_map.95
  95.3 1.2 shard_map.96
  96.5 0.5 collective-permute-start.8
  97.0 5.6 %collective-permute-start.7 = (bf16[256,512]{1,0:T(8,128)(2,1)}, bf16[256,512]{1,0:T(8,128)(2,1)S(1)}, u32[]{:S(2)}, u32[]{:S(2)}) collective-permute-start(bf16[256,512]{1,0:T(8,128)(2,1)} %shard_map.95), channel_id=1, source_target_pairs={{6,0},{8,2},{10,4},{12,6},{14,8},{16,10},{18,12},{20,14},{22,16},{... | collective-permute-start | bytes 786440 | tf_op jit(solution)/shard_map/ppermute | solution.py:291
  102.6 0.8 collective-permute-start.6
  103.4 0.0 collective-permute-done.14.refs_3_
  103.4 1.5 %collective-permute-start.5 = (bf16[256,512]{1,0:T(8,128)(2,1)S(1)}, bf16[256,512]{1,0:T(8,128)(2,1)}, u32[]{:S(2)}, u32[]{:S(2)}) collective-permute-start(bf16[256,512]{1,0:T(8,128)(2,1)S(1)} %copy-done.27), channel_id=1, source_target_pairs={{2,0},{4,2},{6,4},{8,6},{10,8},{12,10},{14,12},{16,14},{18,16},{20... | collective-permute-start | bytes 786440 | tf_op jit(solution)/shard_map/ppermute | solution.py:291
  104.9 0.8 shard_map.102
  105.7 7.8 %collective-permute-done.9.refs_5_ = bf16[256,512]{1,0:T(8,128)(2,1)S(1)} collective-permute-done((bf16[256,512]{1,0:T(8,128)(2,1)}, bf16[256,512]{1,0:T(8,128)(2,1)S(1)}, u32[]{:S(2)}, u32[]{:S(2)}) %collective-permute-start.9) | collective-permute-done | bytes 262176 | tf_op jit(solution)/shard_map/ppermute | solution.py:291
  113.5 1.3 collective-permute-start.15
  114.8 2.7 %shard_map.91 = (f32[512,512]{1,0:T(8,128)}, f32[256,512]{1,0:T(8,128)}, s32[1,512]{1,0:T(1,128)S(1)}) custom-call(s32[4,256]{1,0:T(4,128)S(1)} %bitcast.20, bf16[1024,512]{1,0:T(8,128)(2,1)S(1)} %get-tuple-element.33.q_ref, f32[4,256,1]{2,1,0:T(8,128)S(1)} %copy-done.15, bf16[1024,256]{1,0:T(8,128)(2,1)S(1)} %copy-done.16, s32[16,32]{1,0:T(8,128)S(1)} %bitcast.16), custom_call_target="tpu_custom_call" | custom-call | tf_op jit(solution)/shard_map/pallas_call | solution.py:258
  117.5 0.0 collective-permute-done.6.refs_2_
  117.5 0.0 copy-start.28
  117.5 0.9 collective-permute-done.5.refs_1_
  118.5 0.8 copy-done.23
  119.3 2.7 %shard_map.98 = (f32[512,256]{1,0:T(8,128)S(1)}, bf16[512,256]{1,0:T(8,128)(2,1)S(1)}) custom-call(s32[2]{0:T(128)S(1)} %copy-done.20, s32[1,512]{1,0:T(1,128)S(1)} %get-tuple-element.37.wanted_ref, s32[1,256]{1,0:T(1,128)S(1)} %copy-done.21, bf16[512,512]{1,0:T(8,128)(2,1)} %bitcast.22, f32[512,512]{1,0:T(8,128)} %get-tuple-element.39.base_ref, ...), custom_call_target="tpu_custom_call" | custom-call | tf_op jit(solution)/shard_map/pallas_call | solution.py:258
  121.9 0.1 collective-permute-start.10
  122.0 0.7 shard_map.103
  122.7 1.6 %collective-permute-start.16 = (bf16[4,32,512]{2,1,0:T(8,128)(2,1)}, bf16[4,32,512]{2,1,0:T(8,128)(2,1)S(1)}, u32[]{:S(2)}, u32[]{:S(2)}) collective-permute-start(bf16[4,32,512]{2,1,0:T(8,128)(2,1)} %get-tuple-element.59), channel_id=1, source_target_pairs={{0,16},{2,18},{4,20},{6,22},{8,24},{10,26},{12,28},{14,30},{16,0},... | collective-permute-start | bytes 393224 | tf_op jit(solution)/shard_map/ppermute | solution.py:294
  124.3 7.6 %collective-permute-done.16.refs_1_ = bf16[4,32,512]{2,1,0:T(8,128)(2,1)S(1)} collective-permute-done((bf16[4,32,512]{2,1,0:T(8,128)(2,1)}, bf16[4,32,512]{2,1,0:T(8,128)(2,1)S(1)}, u32[]{:S(2)}, u32[]{:S(2)}) %collective-permute-start.16) | collective-permute-done | bytes 131104 | tf_op jit(solution)/shard_map/ppermute | solution.py:294
  132.0 0.7 shard_map.104
  132.7 0.0 collective-permute-done.10
  132.7 0.8 convert_add_fusion
  (58 shorter events, 0.1 us)
Async XLA Ops:
  0.6 56.1 %copy-start = (bf16[4,512,512]{2,1,0:T(8,128)(2,1)S(1)}, bf16[4,512,512]{2,1,0:T(8,128)(2,1)}, u32[]{:S(2)}) copy-start(bf16[4,512,512]{2,1,0:T(8,128)(2,1)} %rel_ref.3) | copy-start | bytes 6291460
  0.6 56.1 %copy-start.18 = (s32[256,4]{0,1:T(4,128)S(1)}, s32[256,4]{0,1:T(4,128)}, u32[]{:S(2)}) copy-start(s32[256,4]{0,1:T(4,128)} %param.11) | copy-start | bytes 12292
  3.0 53.8 %copy-start.22 = (s32[1,256]{1,0:T(1,128)S(1)}, s32[1,256]{1,0:T(1,128)}, u32[]{:S(2)}) copy-start(s32[1,256]{1,0:T(1,128)} %get-tuple-element.31.pos_ref) | copy-start | bytes 3076
  21.3 38.5 %copy-start.19 = (s32[256,4]{0,1:T(4,128)S(1)}, s32[256,4]{0,1:T(4,128)}, u32[]{:S(2)}) copy-start(s32[256,4]{0,1:T(4,128)} %param.12) | copy-start | bytes 12292
  21.3 38.5 %copy-start.20 = (s32[2]{0:T(128)S(1)}, s32[2]{0:T(128)}, u32[]{:S(2)}) copy-start(s32[2]{0:T(128)} %pad_add_fusion.me_ref) | copy-start | bytes 28
  21.3 34.7 %all-to-all-start.1 = ((bf16[16,32,512]{2,1,0:T(8,128)(2,1)}), bf16[16,32,512]{2,1,0:T(8,128)(2,1)S(1)}, u32[]{:S(2)}, u32[]{:S(2)}) async-start(bf16[16,32,512]{2,1,0:T(8,128)(2,1)} %bitcast.21), calls=%async_computation.1 | async-start | bytes 1048576 | tf_op jit(solution)/shard_map/all_to_all | solution.py:297
  27.1 31.9 %collective-permute-start.4 = (bf16[256,512]{1,0:T(8,128)(2,1)}, bf16[256,512]{1,0:T(8,128)(2,1)S(1)}, u32[]{:S(2)}, u32[]{:S(2)}) collective-permute-start(bf16[256,512]{1,0:T(8,128)(2,1)} %shard_map.89.refs_0_), channel_id=1, source_target_pairs={{4,0},{6,2},{8,4},{10,6},{12,8},{14,10},{16,12},{18,14},{20,16},{2... | collective-permute-start | bytes 786440 | tf_op jit(solution)/shard_map/ppermute | solution.py:291
  31.7 27.4 %collective-permute-start.3 = (bf16[256,512]{1,0:T(8,128)(2,1)}, bf16[256,512]{1,0:T(8,128)(2,1)}, u32[]{:S(2)}, u32[]{:S(2)}) collective-permute-start(bf16[256,512]{1,0:T(8,128)(2,1)} %shard_map.89.refs_0_), channel_id=1, source_target_pairs={{2,0},{4,2},{6,4},{8,6},{10,8},{12,10},{14,12},{16,14},{18,16},{20... | collective-permute-start | bytes 786440 | tf_op jit(solution)/shard_map/ppermute | solution.py:291
  33.2 25.9 %collective-permute-start.2 = (bf16[256,512]{1,0:T(8,128)(2,1)}, bf16[256,512]{1,0:T(8,128)(2,1)}, u32[]{:S(2)}, u32[]{:S(2)}) collective-permute-start(bf16[256,512]{1,0:T(8,128)(2,1)} %shard_map.89.refs_0_), channel_id=1, source_target_pairs={{26,0},{28,2},{30,4},{0,6},{2,8},{4,10},{6,12},{8,14},{10,16},{12,... | collective-permute-start | bytes 786440 | tf_op jit(solution)/shard_map/ppermute | solution.py:291
  33.2 25.9 %collective-permute-start.1 = (bf16[256,512]{1,0:T(8,128)(2,1)}, bf16[256,512]{1,0:T(8,128)(2,1)}, u32[]{:S(2)}, u32[]{:S(2)}) collective-permute-start(bf16[256,512]{1,0:T(8,128)(2,1)} %shard_map.89.refs_0_), channel_id=1, source_target_pairs={{28,0},{30,2},{0,4},{2,6},{4,8},{6,10},{8,12},{10,14},{12,16},{14,... | collective-permute-start | bytes 786440 | tf_op jit(solution)/shard_map/ppermute | solution.py:291
  34.6 24.4 %collective-permute-start = (bf16[256,512]{1,0:T(8,128)(2,1)}, bf16[256,512]{1,0:T(8,128)(2,1)}, u32[]{:S(2)}, u32[]{:S(2)}) collective-permute-start(bf16[256,512]{1,0:T(8,128)(2,1)} %shard_map.89.refs_0_), channel_id=1, source_target_pairs={{30,0},{0,2},{2,4},{4,6},{6,8},{8,10},{10,12},{12,14},{14,16},{16,... | collective-permute-start | bytes 786440 | tf_op jit(solution)/shard_map/ppermute | solution.py:291
  56.0 0.8 copy-start.4
  56.8 1.0 copy-start.5
  59.0 13.5 %copy-start.6 = (f32[512,256]{1,0:T(8,128)}, f32[512,256]{1,0:T(8,128)S(1)}, u32[]{:S(2)}) copy-start(f32[512,256]{1,0:T(8,128)S(1)} %get-tuple-element.34.turned) | copy-start | bytes 1572868
  59.0 0.7 copy-start.30
  59.8 1.0 copy-start.1
  69.6 2.9 %copy-start.2 = (bf16[4,256,512]{2,1,0:T(8,128)(2,1)}, bf16[4,256,512]{2,1,0:T(8,128)(2,1)S(1)}, u32[]{:S(2)}) copy-start(bf16[4,256,512]{2,1,0:T(8,128)(2,1)S(1)} %get-tuple-element.38.pair_ref) | copy-start | bytes 3145732
  69.6 11.9 %collective-permute-start.11 = (bf16[2,256,512]{2,1,0:T(8,128)(2,1)}, bf16[2,256,512]{2,1,0:T(8,128)(2,1)}, u32[]{:S(2)}, u32[]{:S(2)}) collective-permute-start(bf16[2,256,512]{2,1,0:T(8,128)(2,1)} %get-tuple-element.49), channel_id=1, source_target_pairs={{0,2},{2,0},{4,6},{6,4},{8,10},{10,8},{12,14},{14,12},{16,18},{18,... | collective-permute-start | bytes 1572872 | tf_op jit(solution)/shard_map/ppermute | solution.py:294
  69.7 16.9 %collective-permute-start.12 = (bf16[2,256,512]{2,1,0:T(8,128)(2,1)}, bf16[2,256,512]{2,1,0:T(8,128)(2,1)}, u32[]{:S(2)}, u32[]{:S(2)}) collective-permute-start(bf16[2,256,512]{2,1,0:T(8,128)(2,1)} %get-tuple-element.52), channel_id=1, source_target_pairs={{0,4},{2,6},{4,0},{6,2},{8,12},{10,14},{12,8},{14,10},{16,20},{18,... | collective-permute-start | bytes 1572872 | tf_op jit(solution)/shard_map/ppermute | solution.py:294
  72.5 46.0 %all-to-all-start.2 = ((bf16[16,32,512]{2,1,0:T(8,128)(2,1)}), bf16[16,32,512]{2,1,0:T(8,128)(2,1)S(1)}, u32[]{:S(2)}, u32[]{:S(2)}) async-start(bf16[16,32,512]{2,1,0:T(8,128)(2,1)} %bitcast.23), calls=%async_computation.2 | async-start | bytes 1048576 | tf_op jit(solution)/shard_map/all_to_all | solution.py:297
  77.0 1.2 copy-start.3
  78.2 1.0 copy-start.7
  79.3 11.3 %copy-start.14 = (bf16[1024,256]{1,0:T(8,128)(2,1)S(1)}, bf16[1024,256]{1,0:T(8,128)(2,1)}, u32[]{:S(2)}) copy-start(bf16[1024,256]{1,0:T(8,128)(2,1)} %get-tuple-element.45.weight_ref) | copy-start | bytes 1572868
  81.5 5.1 %copy-start.8 = (f32[2,256,512]{2,1,0:T(8,128)S(1)}, f32[2,256,512]{2,1,0:T(8,128)}, u32[]{:S(2)}) copy-start(f32[2,256,512]{2,1,0:T(8,128)} %get-tuple-element.51.refs_0_) | copy-start | bytes 3145732
  81.5 1.3 copy-start.9
  84.6 7.1 %copy-start.13 = (bf16[1024,256]{1,0:T(8,128)(2,1)S(1)}, bf16[1024,256]{1,0:T(8,128)(2,1)}, u32[]{:S(2)}) copy-start(bf16[1024,256]{1,0:T(8,128)(2,1)} %get-tuple-element.41.weight_ref) | copy-start | bytes 1572868
  84.6 18.0 %collective-permute-start.13 = (bf16[2,128,512]{2,1,0:T(8,128)(2,1)}, bf16[2,128,512]{2,1,0:T(8,128)(2,1)S(1)}, u32[]{:S(2)}, u32[]{:S(2)}) collective-permute-start(bf16[2,128,512]{2,1,0:T(8,128)(2,1)} %get-tuple-element.54), channel_id=1, source_target_pairs={{0,4},{2,6},{4,0},{6,2},{8,12},{10,14},{12,8},{14,10},{16,20},{18,... | collective-permute-start | bytes 786440 | tf_op jit(solution)/shard_map/ppermute | solution.py:294
  88.4 4.6 %copy-start.12 = (bf16[1024,256]{1,0:T(8,128)(2,1)S(1)}, bf16[1024,256]{1,0:T(8,128)(2,1)}, u32[]{:S(2)}) copy-start(bf16[1024,256]{1,0:T(8,128)(2,1)} %get-tuple-element.42.weight_ref) | copy-start | bytes 1572868
  88.4 15.0 %collective-permute-start.14 = (bf16[2,128,512]{2,1,0:T(8,128)(2,1)}, bf16[2,128,512]{2,1,0:T(8,128)(2,1)S(1)}, u32[]{:S(2)}, u32[]{:S(2)}) collective-permute-start(bf16[2,128,512]{2,1,0:T(8,128)(2,1)} %get-tuple-element.55), channel_id=1, source_target_pairs={{0,2},{2,0},{4,6},{6,4},{8,10},{10,8},{12,14},{14,12},{16,18},{18,... | collective-permute-start | bytes 786440 | tf_op jit(solution)/shard_map/ppermute | solution.py:294
  91.7 2.4 %copy-start.11 = (bf16[1024,256]{1,0:T(8,128)(2,1)S(1)}, bf16[1024,256]{1,0:T(8,128)(2,1)}, u32[]{:S(2)}) copy-start(bf16[1024,256]{1,0:T(8,128)(2,1)} %get-tuple-element.43.weight_ref) | copy-start | bytes 1572868
  91.7 21.8 %collective-permute-start.9 = (bf16[256,512]{1,0:T(8,128)(2,1)}, bf16[256,512]{1,0:T(8,128)(2,1)S(1)}, u32[]{:S(2)}, u32[]{:S(2)}) collective-permute-start(bf16[256,512]{1,0:T(8,128)(2,1)} %shard_map.97), channel_id=1, source_target_pairs={{28,0},{30,2},{0,4},{2,6},{4,8},{6,10},{8,12},{10,14},{12,16},{14,... | collective-permute-start | bytes 786440 | tf_op jit(solution)/shard_map/ppermute | solution.py:291
  93.0 2.4 %copy-start.10 = (bf16[1024,256]{1,0:T(8,128)(2,1)S(1)}, bf16[1024,256]{1,0:T(8,128)(2,1)}, u32[]{:S(2)}) copy-start(bf16[1024,256]{1,0:T(8,128)(2,1)} %get-tuple-element.44.weight_ref) | copy-start | bytes 1572868
  94.1 8.5 %copy-start.29 = (bf16[256,512]{1,0:T(8,128)(2,1)S(1)}, bf16[256,512]{1,0:T(8,128)(2,1)}, u32[]{:S(2)}) copy-start(bf16[256,512]{1,0:T(8,128)(2,1)} %shard_map.94) | copy-start | bytes 786436
  94.1 9.3 %copy-start.27 = (bf16[256,512]{1,0:T(8,128)(2,1)S(1)}, bf16[256,512]{1,0:T(8,128)(2,1)}, u32[]{:S(2)}) copy-start(bf16[256,512]{1,0:T(8,128)(2,1)} %shard_map.93) | copy-start | bytes 786436
  95.3 19.5 %copy-start.15 = (f32[4,256,1]{2,1,0:T(8,128)S(1)}, f32[4,256,1]{2,1,0:T(8,128)}, u32[]{:S(2)}) copy-start(f32[4,256,1]{2,1,0:T(8,128)} %get-tuple-element.35.pw_ref) | copy-start | bytes 12292
  95.3 19.5 %copy-start.16 = (bf16[1024,256]{1,0:T(8,128)(2,1)S(1)}, bf16[1024,256]{1,0:T(8,128)(2,1)}, u32[]{:S(2)}) copy-start(bf16[1024,256]{1,0:T(8,128)(2,1)} %get-tuple-element.36.weight_ref) | copy-start | bytes 1572868
  95.3 19.5 %copy-start.17 = (s32[16,1,32]{2,1,0:T(1,128)S(1)}, s32[16,1,32]{2,1,0:T(1,128)}, u32[]{:S(2)}) copy-start(s32[16,1,32]{2,1,0:T(1,128)} %all_to_all.21) | copy-start | bytes 6148
  96.5 22.8 %copy-start.21 = (s32[1,256]{1,0:T(1,128)S(1)}, s32[1,256]{1,0:T(1,128)}, u32[]{:S(2)}) copy-start(s32[1,256]{1,0:T(1,128)} %neg_ref.1) | copy-start | bytes 3076
  96.5 21.0 %collective-permute-start.8 = (bf16[256,512]{1,0:T(8,128)(2,1)}, bf16[256,512]{1,0:T(8,128)(2,1)S(1)}, u32[]{:S(2)}, u32[]{:S(2)}) collective-permute-start(bf16[256,512]{1,0:T(8,128)(2,1)} %shard_map.96), channel_id=1, source_target_pairs={{30,0},{0,2},{2,4},{4,6},{6,8},{8,10},{10,12},{12,14},{14,16},{16,... | collective-permute-start | bytes 786440 | tf_op jit(solution)/shard_map/ppermute | solution.py:291
  97.0 20.5 %collective-permute-start.7 = (bf16[256,512]{1,0:T(8,128)(2,1)}, bf16[256,512]{1,0:T(8,128)(2,1)S(1)}, u32[]{:S(2)}, u32[]{:S(2)}) collective-permute-start(bf16[256,512]{1,0:T(8,128)(2,1)} %shard_map.95), channel_id=1, source_target_pairs={{6,0},{8,2},{10,4},{12,6},{14,8},{16,10},{18,12},{20,14},{22,16},{... | collective-permute-start | bytes 786440 | tf_op jit(solution)/shard_map/ppermute | solution.py:291
  102.6 14.9 %collective-permute-start.6 = (bf16[256,512]{1,0:T(8,128)(2,1)S(1)}, bf16[256,512]{1,0:T(8,128)(2,1)S(1)}, u32[]{:S(2)}, u32[]{:S(2)}) collective-permute-start(bf16[256,512]{1,0:T(8,128)(2,1)S(1)} %copy-done.29), channel_id=1, source_target_pairs={{4,0},{6,2},{8,4},{10,6},{12,8},{14,10},{16,12},{18,14},{20,16},{2... | collective-permute-start | bytes 786440 | tf_op jit(solution)/shard_map/ppermute | solution.py:291
  103.4 15.0 %collective-permute-start.5 = (bf16[256,512]{1,0:T(8,128)(2,1)S(1)}, bf16[256,512]{1,0:T(8,128)(2,1)}, u32[]{:S(2)}, u32[]{:S(2)}) collective-permute-start(bf16[256,512]{1,0:T(8,128)(2,1)S(1)} %copy-done.27), channel_id=1, source_target_pairs={{2,0},{4,2},{6,4},{8,6},{10,8},{12,10},{14,12},{16,14},{18,16},{20... | collective-permute-start | bytes 786440 | tf_op jit(solution)/shard_map/ppermute | solution.py:291
  113.5 5.0 %copy-start.24 = (bf16[256,512]{1,0:T(8,128)(2,1)}, bf16[256,512]{1,0:T(8,128)(2,1)S(1)}, u32[]{:S(2)}) copy-start(bf16[256,512]{1,0:T(8,128)(2,1)S(1)} %collective-permute-done.9.refs_5_) | copy-start | bytes 786436
  113.5 8.5 %collective-permute-start.15 = (bf16[4,64,512]{2,1,0:T(8,128)(2,1)}, bf16[4,64,512]{2,1,0:T(8,128)(2,1)S(1)}, u32[]{:S(2)}, u32[]{:S(2)}) collective-permute-start(bf16[4,64,512]{2,1,0:T(8,128)(2,1)} %get-tuple-element.57), channel_id=1, source_target_pairs={{0,8},{2,10},{4,12},{6,14},{8,0},{10,2},{12,4},{14,6},{16,24},{18,... | collective-permute-start | bytes 786440 | tf_op jit(solution)/shard_map/ppermute | solution.py:294
  117.5 1.0 copy-start.25
  117.5 1.0 copy-start.26
  117.5 1.0 copy-start.28
  118.5 0.8 copy-start.23
  121.9 10.8 %collective-permute-start.10 = (bf16[512,256]{1,0:T(8,128)(2,1)S(1)}, bf16[512,256]{1,0:T(8,128)(2,1)S(1)}, u32[]{:S(2)}, u32[]{:S(2)}) collective-permute-start(bf16[512,256]{1,0:T(8,128)(2,1)S(1)} %get-tuple-element.47), channel_id=1, source_target_pairs={{0,1},{1,0},{2,3},{3,2},{4,5},{5,4},{6,7},{7,6},{8,9},{9,8},{10,11... | collective-permute-start | bytes 786440 | tf_op jit(solution)/shard_map/ppermute | solution.py:382
  122.7 9.2 %collective-permute-start.16 = (bf16[4,32,512]{2,1,0:T(8,128)(2,1)}, bf16[4,32,512]{2,1,0:T(8,128)(2,1)S(1)}, u32[]{:S(2)}, u32[]{:S(2)}) collective-permute-start(bf16[4,32,512]{2,1,0:T(8,128)(2,1)} %get-tuple-element.59), channel_id=1, source_target_pairs={{0,16},{2,18},{4,20},{6,22},{8,24},{10,26},{12,28},{14,30},{16,0},... | collective-permute-start | bytes 393224 | tf_op jit(solution)/shard_map/ppermute | solution.py:294

commit v6 on v5

--- a/solution.py
+++ b/solution.py
@@ -91,9 +91,12 @@
     )
 
 
-def serve_kernel(wanted_ref, entity_ref, out_ref):
-    pick = hot(wanted_column(wanted_ref), (out_ref.shape[0], entity_ref.shape[0]), 1)
-    out_ref[...] = dot(pick, entity_ref[...]).astype(BF)
+def serve_kernel(wanted_ref, entity_ref, out_ref, table, sem):
+    load = pltpu.make_async_copy(entity_ref, table, sem.at[0])
+    load.start()
+    pick = hot(wanted_column(wanted_ref), (out_ref.shape[0], table.shape[0]), 1)
+    load.wait()
+    out_ref[...] = dot(pick, table[...]).astype(BF)
 
 
 def query_kernel(pos_ref, qrel_ref, fetched_ref, rel_ref, turned, q_ref, prod):
@@ -180,13 +183,6 @@
     term[...] = t_dot(weight_ref[...], q_ref[...]).astype(term.dtype)
 
 
-def keep_kernel(step, me_ref, turned, pair_ref, keep_a, keep_b, side):
-    for outer, keep in enumerate((keep_a, keep_b)):
-        arrange(step, outer, 0, me_ref[0], turned, side)
-        for k in range(keep.shape[0]):
-            keep[k] = dot(side[...].astype(BF), pair_ref[outer * keep.shape[0] + k])
-
-
 def fold_kernel(parts, *refs):
     keeps, gots, refs = refs[:parts], refs[parts : 2 * parts], refs[2 * parts :]
     for n in range(parts):
@@ -199,13 +195,17 @@
             refs[1][rows] = total[:, half:].astype(BF)
 
 
-def head_kernel(pos_ref, pair_ref, rel_ref, bucket_ref):
+def head_kernel(step, me_ref, pos_ref, pair_ref, rel_ref, turned, bucket_ref, keep_a, keep_b, side):
     rels, heads, _ = pair_ref.shape
     head = dot_t(pair_ref[0], rel_ref[0])
     for k in range(1, rels):
         head = head + dot_t(pair_ref[k], rel_ref[k])
     slots = bucket_ref.shape[0]
     bucket_ref[...] = dot(hot(pos_ref[...], (slots, heads), 0), head.astype(BF)).astype(BF)
+    for outer, keep in enumerate((keep_a, keep_b)):
+        arrange(step, outer, 0, me_ref[0], turned, side)
+        for k in range(keep.shape[0]):
+            keep[k] = dot(side[...].astype(BF), pair_ref[outer * keep.shape[0] + k])
 
 
 def tail_kernel(tail_ref, q_ref, pw_ref, weight_ref, wanted_ref, out_ref, term, row_ref):
@@ -307,7 +307,12 @@
         head_row.reshape(1, heads),
     )
     wanted = dealt(asked)
-    (served,) = kernel(serve_kernel, [((slots, width), BF, HM)], limit=None)(wanted, entity)
+    (served,) = kernel(
+        serve_kernel,
+        [((slots, width), BF, HM)],
+        [((ents, width), BF), pltpu.SemaphoreType.DMA((1,))],
+        wild=1,
+    )(wanted, far(entity))
     fetched = dealt(served.reshape(shards, cap, width)).reshape(slots, width)
 
     many = per * heads
@@ -339,10 +344,12 @@
 
     got_a = flipped(send_a, 1)
     got_b = flipped(send_b, 2)
-    keep_a, keep_b = kernel(functools.partial(keep_kernel, step), [(part, F32, HM)] * 2, [side], smem=1)(
-        me, turned, pair,
-    )
-    (buckets,) = kernel(head_kernel, [((slots, width), BF, HM)])(pos, pair, relation)
+    buckets, keep_a, keep_b = kernel(
+        functools.partial(head_kernel, step),
+        [((slots, width), BF, HM), (part, F32, HM), (part, F32, HM)],
+        [side],
+        smem=1,
+    )(me, pos, pair, relation, turned)
     returned = dealt(buckets.reshape(shards, cap, width)).reshape(slots, width)
     back = []
     for n, offset in enumerate(OFFSETS):

time: 134 us -> 137 us (1.022)
  waiting for transfers between devices: 37.6 us -> 45.9 us
  starting transfers between devices: 32.4 us -> 30 us
  local copies, waits for them, and re-layouts: 7.99 us -> 5.81 us
    ppermute x6, waiting for transfers between devices: 7.64 us -> 19.7 us  [flipped(): return lax.ppermute(value, 'blk', [(i, i ^ bit) for i in range(shards)])]
    ppermute x10, waiting for transfers between devices: 8.78 us -> 4.47 us  [moved(): lax.ppermute(value, 'blk', [((i - distance) % shards, i) for i in range(s...]
    unnamed x62 -> x52, local copies, waits for them, and re-layouts: 7.99 us -> 5.81 us
    ppermute x10, starting transfers between devices: 16.1 us -> 14.6 us  [moved(): lax.ppermute(value, 'blk', [((i - distance) % shards, i) for i in range(s...]
    pallas_call x19 -> x18, Pallas kernels: 37.3 us -> 36.1 us  [call(): pl.pallas_call(body, out_shape=[o[2](*o[:2]) if len(o) > 2 else jax.Shape...]
  transfers between devices with their start and end apart: 19 -> 19, of which waited for: 4 -> 6; matrix products, arithmetic and copies ran while one was open for 0% -> 0% of each run, Pallas kernels for 18% -> 17%
where the time goes in v6:
time: 137 us; the launch traced here: 136 us
  waiting for transfers between devices  45.9 us (34%)
  Pallas kernels  36.1 us (26%)
  starting transfers between devices  30 us (22%)
  blocking collectives  15.7 us (11%)
  local copies, waits for them, and re-layouts  5.81 us (4%)
  other arithmetic  1.5 us (1%)
    pallas_call x18, Pallas kernels, call(): pl.pallas_call(body, out_shape=[o[2](*o[:2]) if len(o) > 2 else jax.Shape...  36.1 us
    all_to_all x2, waiting for transfers between devices, dealt(): lax.all_to_all(value, 'blk', split_axis=0, concat_axis=0, tiled=True, axi...  21.7 us
    ppermute x6, waiting for transfers between devices, flipped(): return lax.ppermute(value, 'blk', [(i, i ^ bit) for i in range(shards)])  19.7 us
    all_to_all x1, blocking collectives, dealt(): lax.all_to_all(value, 'blk', split_axis=0, concat_axis=0, tiled=True, axi...  15.7 us
    ppermute x10, starting transfers between devices, moved(): lax.ppermute(value, 'blk', [((i - distance) % shards, i) for i in range(s...  14.6 us
    all_to_all x2, starting transfers between devices, dealt(): lax.all_to_all(value, 'blk', split_axis=0, concat_axis=0, tiled=True, axi...  8.31 us
    ppermute x6, starting transfers between devices, flipped(): return lax.ppermute(value, 'blk', [(i, i ^ bit) for i in range(shards)])  6.99 us
    unnamed x52, local copies, waits for them, and re-layouts  5.81 us
  transfers between devices with their start and end apart: 19, of which 6 were waited for; matrix products, arithmetic and copies ran while one was open for 0% of the time, Pallas kernels for 17%

profile of v6, /device:TPU:0, one launch (start us, length us, event | category | flops | bytes accessed | tf_op | source)
XLA Modules:
  0.0 135.9 jit_solution(1664693841897977390)
XLA Ops:
  0.7 0.7 pad_add_fusion.me_ref
  1.3 1.6 %shard_map.86 = (s32[16,32]{1,0:T(8,128)}, s32[1,256]{1,0:T(1,128)}) custom-call(s32[2]{0:T(128)} %pad_add_fusion.me_ref, s32[1,256]{1,0:T(1,128)} %bitcast.25, s32[1,256]{1,0:T(1,128)} %bitcast.26), custom_call_target="tpu_custom_call" | custom-call | tf_op jit(solution)/shard_map/pallas_call | solution.py:258
  2.9 15.7 %all_to_all.21 = s32[16,1,32]{2,1,0:T(1,128)S(1)} all-to-all(s32[16,1,32]{2,1,0:T(1,128)} %bitcast.24), channel_id=1, replica_groups=mesh['blk'=16,'rep'=2] {'blk'}, dimensions={0} | all-to-all | bytes 4096 | tf_op jit(solution)/shard_map/all_to_all | solution.py:297
  18.6 2.3 %shard_map.87 = bf16[512,512]{1,0:T(8,128)(2,1)} custom-call(s32[16,32]{1,0:T(8,128)S(1)} %bitcast.15, bf16[512,512]{1,0:T(8,128)(2,1)} %ent_ref.1), custom_call_target="tpu_custom_call" | custom-call | tf_op jit(solution)/shard_map/pallas_call | solution.py:258
  21.0 0.0 copy-start.14
  21.0 3.6 %all-to-all-start.1 = ((bf16[16,32,512]{2,1,0:T(8,128)(2,1)}), bf16[16,32,512]{2,1,0:T(8,128)(2,1)S(1)}, u32[]{:S(2)}, u32[]{:S(2)}) async-start(bf16[16,32,512]{2,1,0:T(8,128)(2,1)} %bitcast.21), calls=%async_computation.1 | async-start | bytes 1048576 | tf_op jit(solution)/shard_map/all_to_all | solution.py:297
  24.6 2.1 %shard_map.89.refs_0_ = bf16[256,512]{1,0:T(8,128)(2,1)} custom-call(s32[1,256]{1,0:T(1,128)} %neg_ref.1, bf16[512,512]{1,0:T(8,128)(2,1)} %ent_ref.1), custom_call_target="tpu_custom_call" | custom-call | tf_op jit(solution)/shard_map/pallas_call | solution.py:258
  26.7 4.6 %collective-permute-start.4 = (bf16[256,512]{1,0:T(8,128)(2,1)}, bf16[256,512]{1,0:T(8,128)(2,1)S(1)}, u32[]{:S(2)}, u32[]{:S(2)}) collective-permute-start(bf16[256,512]{1,0:T(8,128)(2,1)} %shard_map.89.refs_0_), channel_id=1, source_target_pairs={{4,0},{6,2},{8,4},{10,6},{12,8},{14,10},{16,12},{18,14},{20,16},{2... | collective-permute-start | bytes 786440 | tf_op jit(solution)/shard_map/ppermute | solution.py:291
  31.3 1.5 %collective-permute-start.3 = (bf16[256,512]{1,0:T(8,128)(2,1)}, bf16[256,512]{1,0:T(8,128)(2,1)}, u32[]{:S(2)}, u32[]{:S(2)}) collective-permute-start(bf16[256,512]{1,0:T(8,128)(2,1)} %shard_map.89.refs_0_), channel_id=1, source_target_pairs={{2,0},{4,2},{6,4},{8,6},{10,8},{12,10},{14,12},{16,14},{18,16},{20... | collective-permute-start | bytes 786440 | tf_op jit(solution)/shard_map/ppermute | solution.py:291
  32.8 0.0 collective-permute-start.2
  32.8 1.5 %collective-permute-start.1 = (bf16[256,512]{1,0:T(8,128)(2,1)}, bf16[256,512]{1,0:T(8,128)(2,1)}, u32[]{:S(2)}, u32[]{:S(2)}) collective-permute-start(bf16[256,512]{1,0:T(8,128)(2,1)} %shard_map.89.refs_0_), channel_id=1, source_target_pairs={{28,0},{30,2},{0,4},{2,6},{4,8},{6,10},{8,12},{10,14},{12,16},{14,... | collective-permute-start | bytes 786440 | tf_op jit(solution)/shard_map/ppermute | solution.py:291
  34.2 0.1 collective-permute-start
  34.4 21.7 %all-to-all-done.1 = bf16[16,32,512]{2,1,0:T(8,128)(2,1)S(1)} async-done(((bf16[16,32,512]{2,1,0:T(8,128)(2,1)}), bf16[16,32,512]{2,1,0:T(8,128)(2,1)S(1)}, u32[]{:S(2)}, u32[]{:S(2)}) %all-to-all-start.1) | async-done | bytes 524320 | tf_op jit(solution)/shard_map/all_to_all | solution.py:297
  56.1 0.8 copy-done.2
  56.9 1.0 copy-done.3
  57.9 1.2 shard_map.88
  59.1 0.0 collective-permute-done.4.refs_5_
  59.1 0.0 collective-permute-done.3.refs_4_
  59.2 0.0 collective-permute-done.1.refs_2_
  59.2 0.0 collective-permute-done.refs_1_
  59.2 0.7 copy-done.25
  59.8 1.0 copy-done.1
  60.9 8.7 %shard_map.90 = (f32[4,256,1]{2,1,0:T(8,128)}, bf16[4,256,512]{2,1,0:T(8,128)(2,1)S(1)}, bf16[2,256,512]{2,1,0:T(8,128)(2,1)}, bf16[2,256,512]{2,1,0:T(8,128)(2,...) custom-call(s32[2]{0:T(128)S(1)} %copy-done.15, ...), custom_call_target="tpu_custom_call" | custom-call | tf_op jit(solution)/shard_map/pallas_call | solution.py:258
  69.6 1.0 collective-permute-start.12
  70.6 3.1 %shard_map.92 = (bf16[512,512]{1,0:T(8,128)(2,1)}, f32[2,256,512]{2,1,0:T(8,128)}, f32[2,256,512]{2,1,0:T(8,128)}) custom-call(s32[2]{0:T(128)S(1)} %copy-done.15, s32[1,256]{1,0:T(1,128)S(1)} %copy-done.17, bf16[4,256,512]{2,1,0:T(8,128)(2,1)S(1)} %get-tuple-element.39.pair_ref, bf16[4,512,512]{2,1,0:T(8,128)(2,1)S(1)} %copy-done, ...), custom_call_target="tpu_custom_call" | custom-call | tf_op jit(solution)/shard_map/pallas_call | solution.py:258
  73.7 4.7 %all-to-all-start.2 = ((bf16[16,32,512]{2,1,0:T(8,128)(2,1)}), bf16[16,32,512]{2,1,0:T(8,128)(2,1)S(1)}, u32[]{:S(2)}, u32[]{:S(2)}) async-start(bf16[16,32,512]{2,1,0:T(8,128)(2,1)} %bitcast.23), calls=%async_computation.2 | async-start | bytes 1048576 | tf_op jit(solution)/shard_map/all_to_all | solution.py:297
  78.4 2.5 %collective-permute-done.12.refs_1_ = bf16[2,256,512]{2,1,0:T(8,128)(2,1)} collective-permute-done((bf16[2,256,512]{2,1,0:T(8,128)(2,1)}, bf16[2,256,512]{2,1,0:T(8,128)(2,1)}, u32[]{:S(2)}, u32[]{:S(2)}) %collective-permute-start.12) | collective-permute-done | bytes 524320 | tf_op jit(solution)/shard_map/ppermute | solution.py:294
  80.9 1.2 copy-done.5
  82.1 1.9 %shard_map.100 = (f32[2,128,512]{2,1,0:T(8,128)S(1)}, bf16[2,128,512]{2,1,0:T(8,128)(2,1)}) custom-call(f32[2,256,512]{2,1,0:T(8,128)S(1)} %copy-done.5, bf16[2,256,512]{2,1,0:T(8,128)(2,1)} %collective-permute-done.12.refs_1_), custom_call_target="tpu_custom_call" | custom-call | tf_op jit(solution)/shard_map/pallas_call | solution.py:258
  84.0 1.5 %collective-permute-start.14 = (bf16[2,128,512]{2,1,0:T(8,128)(2,1)}, bf16[2,128,512]{2,1,0:T(8,128)(2,1)S(1)}, u32[]{:S(2)}, u32[]{:S(2)}) collective-permute-start(bf16[2,128,512]{2,1,0:T(8,128)(2,1)} %get-tuple-element.57), channel_id=1, source_target_pairs={{0,2},{2,0},{4,6},{6,4},{8,10},{10,8},{12,14},{14,12},{16,18},{18,... | collective-permute-start | bytes 786440 | tf_op jit(solution)/shard_map/ppermute | solution.py:294
  85.5 0.0 collective-permute-done.11.refs_1_
  85.5 1.8 %shard_map.99 = (f32[2,128,512]{2,1,0:T(8,128)S(1)}, bf16[2,128,512]{2,1,0:T(8,128)(2,1)}) custom-call(f32[2,256,512]{2,1,0:T(8,128)S(1)} %copy-done.4, bf16[2,256,512]{2,1,0:T(8,128)(2,1)} %collective-permute-done.11.refs_1_), custom_call_target="tpu_custom_call" | custom-call | tf_op jit(solution)/shard_map/pallas_call | solution.py:258
  87.3 2.1 %collective-permute-start.13 = (bf16[2,128,512]{2,1,0:T(8,128)(2,1)}, bf16[2,128,512]{2,1,0:T(8,128)(2,1)S(1)}, u32[]{:S(2)}, u32[]{:S(2)}) collective-permute-start(bf16[2,128,512]{2,1,0:T(8,128)(2,1)} %get-tuple-element.56), channel_id=1, source_target_pairs={{0,4},{2,6},{4,0},{6,2},{8,12},{10,14},{12,8},{14,10},{16,20},{18,... | collective-permute-start | bytes 786440 | tf_op jit(solution)/shard_map/ppermute | solution.py:294
  89.4 1.2 shard_map.97
  90.6 0.0 collective-permute-start.9
  90.6 1.2 shard_map.93
  91.8 1.2 shard_map.94
  92.9 1.2 shard_map.95
  94.1 1.2 shard_map.96
  95.3 0.4 collective-permute-start.8
  95.7 5.7 %collective-permute-start.7 = (bf16[256,512]{1,0:T(8,128)(2,1)}, bf16[256,512]{1,0:T(8,128)(2,1)S(1)}, u32[]{:S(2)}, u32[]{:S(2)}) collective-permute-start(bf16[256,512]{1,0:T(8,128)(2,1)} %shard_map.95), channel_id=1, source_target_pairs={{6,0},{8,2},{10,4},{12,6},{14,8},{16,10},{18,12},{20,14},{22,16},{... | collective-permute-start | bytes 786440 | tf_op jit(solution)/shard_map/ppermute | solution.py:291
  101.5 0.8 collective-permute-start.6
  102.3 8.2 %collective-permute-done.13.refs_2_ = bf16[2,128,512]{2,1,0:T(8,128)(2,1)S(1)} collective-permute-done((bf16[2,128,512]{2,1,0:T(8,128)(2,1)}, bf16[2,128,512]{2,1,0:T(8,128)(2,1)S(1)}, u32[]{:S(2)}, u32[]{:S(2)}) %collective-permute-start.13) | collective-permute-done | bytes 262176 | tf_op jit(solution)/shard_map/ppermute | solution.py:294
  110.5 0.0 collective-permute-start.5
  110.5 0.8 shard_map.101
  111.3 4.4 %collective-permute-done.9.refs_5_ = bf16[256,512]{1,0:T(8,128)(2,1)S(1)} collective-permute-done((bf16[256,512]{1,0:T(8,128)(2,1)}, bf16[256,512]{1,0:T(8,128)(2,1)S(1)}, u32[]{:S(2)}, u32[]{:S(2)}) %collective-permute-start.9) | collective-permute-done | bytes 262176 | tf_op jit(solution)/shard_map/ppermute | solution.py:291
  115.7 1.6 %collective-permute-start.15 = (bf16[4,64,512]{2,1,0:T(8,128)(2,1)}, bf16[4,64,512]{2,1,0:T(8,128)(2,1)S(1)}, u32[]{:S(2)}, u32[]{:S(2)}) collective-permute-start(bf16[4,64,512]{2,1,0:T(8,128)(2,1)} %get-tuple-element.59), channel_id=1, source_target_pairs={{0,8},{2,10},{4,12},{6,14},{8,0},{10,2},{12,4},{14,6},{16,24},{18,... | collective-permute-start | bytes 786440 | tf_op jit(solution)/shard_map/ppermute | solution.py:294
  117.4 2.6 %shard_map.91 = (f32[512,512]{1,0:T(8,128)}, f32[256,512]{1,0:T(8,128)}, s32[1,512]{1,0:T(1,128)S(1)}) custom-call(s32[4,256]{1,0:T(4,128)S(1)} %bitcast.20, bf16[1024,512]{1,0:T(8,128)(2,1)S(1)} %get-tuple-element.34.q_ref, f32[4,256,1]{2,1,0:T(8,128)S(1)} %copy-done.11, bf16[1024,256]{1,0:T(8,128)(2,1)S(1)} %copy-done.12, s32[16,32]{1,0:T(8,128)S(1)} %bitcast.16), custom_call_target="tpu_custom_call" | custom-call | tf_op jit(solution)/shard_map/pallas_call | solution.py:258
  120.0 0.0 collective-permute-done.8.refs_4_
  120.0 0.0 collective-permute-done.6.refs_2_
  120.0 0.0 copy-start.23
  120.0 0.0 all-to-all-done.2
  120.1 0.6 copy-done.20
  120.7 0.1 copy-done.21
  120.8 0.1 copy-done.23
  120.9 0.2 copy-done.18
  121.1 2.7 %shard_map.98 = (f32[512,256]{1,0:T(8,128)S(1)}, bf16[512,256]{1,0:T(8,128)(2,1)S(1)}) custom-call(s32[2]{0:T(128)S(1)} %copy-done.15, s32[1,512]{1,0:T(1,128)S(1)} %get-tuple-element.38.wanted_ref, s32[1,256]{1,0:T(1,128)S(1)} %copy-done.16, bf16[512,512]{1,0:T(8,128)(2,1)} %bitcast.22, f32[512,512]{1,0:T(8,128)} %get-tuple-element.41.base_ref, ...), custom_call_target="tpu_custom_call" | custom-call | tf_op jit(solution)/shard_map/pallas_call | solution.py:258
  123.7 0.1 collective-permute-start.10
  123.8 0.5 collective-permute-done.15.refs_1_
  124.3 0.7 shard_map.102
  125.0 0.8 collective-permute-start.16
  125.8 8.5 %collective-permute-done.16.refs_1_ = bf16[4,32,512]{2,1,0:T(8,128)(2,1)S(1)} collective-permute-done((bf16[4,32,512]{2,1,0:T(8,128)(2,1)}, bf16[4,32,512]{2,1,0:T(8,128)(2,1)S(1)}, u32[]{:S(2)}, u32[]{:S(2)}) %collective-permute-start.16) | collective-permute-done | bytes 131104 | tf_op jit(solution)/shard_map/ppermute | solution.py:294
  134.3 0.7 shard_map.103
  135.0 0.8 convert_add_fusion
  (47 shorter events, 0.1 us)
Async XLA Ops:
  0.6 56.2 %copy-start = (bf16[4,512,512]{2,1,0:T(8,128)(2,1)S(1)}, bf16[4,512,512]{2,1,0:T(8,128)(2,1)}, u32[]{:S(2)}) copy-start(bf16[4,512,512]{2,1,0:T(8,128)(2,1)} %rel_ref.3) | copy-start | bytes 6291460
  0.6 56.2 %copy-start.13 = (s32[256,4]{0,1:T(4,128)S(1)}, s32[256,4]{0,1:T(4,128)}, u32[]{:S(2)}) copy-start(s32[256,4]{0,1:T(4,128)} %param.11) | copy-start | bytes 12292
  2.9 53.9 %copy-start.17 = (s32[1,256]{1,0:T(1,128)S(1)}, s32[1,256]{1,0:T(1,128)}, u32[]{:S(2)}) copy-start(s32[1,256]{1,0:T(1,128)} %get-tuple-element.32.pos_ref) | copy-start | bytes 3076
  21.0 38.9 %copy-start.14 = (s32[256,4]{0,1:T(4,128)S(1)}, s32[256,4]{0,1:T(4,128)}, u32[]{:S(2)}) copy-start(s32[256,4]{0,1:T(4,128)} %param.12) | copy-start | bytes 12292
  21.0 38.8 %copy-start.15 = (s32[2]{0:T(128)S(1)}, s32[2]{0:T(128)}, u32[]{:S(2)}) copy-start(s32[2]{0:T(128)} %pad_add_fusion.me_ref) | copy-start | bytes 28
  21.0 35.1 %all-to-all-start.1 = ((bf16[16,32,512]{2,1,0:T(8,128)(2,1)}), bf16[16,32,512]{2,1,0:T(8,128)(2,1)S(1)}, u32[]{:S(2)}, u32[]{:S(2)}) async-start(bf16[16,32,512]{2,1,0:T(8,128)(2,1)} %bitcast.21), calls=%async_computation.1 | async-start | bytes 1048576 | tf_op jit(solution)/shard_map/all_to_all | solution.py:297
  26.7 32.4 %collective-permute-start.4 = (bf16[256,512]{1,0:T(8,128)(2,1)}, bf16[256,512]{1,0:T(8,128)(2,1)S(1)}, u32[]{:S(2)}, u32[]{:S(2)}) collective-permute-start(bf16[256,512]{1,0:T(8,128)(2,1)} %shard_map.89.refs_0_), channel_id=1, source_target_pairs={{4,0},{6,2},{8,4},{10,6},{12,8},{14,10},{16,12},{18,14},{20,16},{2... | collective-permute-start | bytes 786440 | tf_op jit(solution)/shard_map/ppermute | solution.py:291
  31.3 27.8 %collective-permute-start.3 = (bf16[256,512]{1,0:T(8,128)(2,1)}, bf16[256,512]{1,0:T(8,128)(2,1)}, u32[]{:S(2)}, u32[]{:S(2)}) collective-permute-start(bf16[256,512]{1,0:T(8,128)(2,1)} %shard_map.89.refs_0_), channel_id=1, source_target_pairs={{2,0},{4,2},{6,4},{8,6},{10,8},{12,10},{14,12},{16,14},{18,16},{20... | collective-permute-start | bytes 786440 | tf_op jit(solution)/shard_map/ppermute | solution.py:291
  32.8 26.4 %collective-permute-start.2 = (bf16[256,512]{1,0:T(8,128)(2,1)}, bf16[256,512]{1,0:T(8,128)(2,1)}, u32[]{:S(2)}, u32[]{:S(2)}) collective-permute-start(bf16[256,512]{1,0:T(8,128)(2,1)} %shard_map.89.refs_0_), channel_id=1, source_target_pairs={{26,0},{28,2},{30,4},{0,6},{2,8},{4,10},{6,12},{8,14},{10,16},{12,... | collective-permute-start | bytes 786440 | tf_op jit(solution)/shard_map/ppermute | solution.py:291
  32.8 26.4 %collective-permute-start.1 = (bf16[256,512]{1,0:T(8,128)(2,1)}, bf16[256,512]{1,0:T(8,128)(2,1)}, u32[]{:S(2)}, u32[]{:S(2)}) collective-permute-start(bf16[256,512]{1,0:T(8,128)(2,1)} %shard_map.89.refs_0_), channel_id=1, source_target_pairs={{28,0},{30,2},{0,4},{2,6},{4,8},{6,10},{8,12},{10,14},{12,16},{14,... | collective-permute-start | bytes 786440 | tf_op jit(solution)/shard_map/ppermute | solution.py:291
  34.2 24.9 %collective-permute-start = (bf16[256,512]{1,0:T(8,128)(2,1)}, bf16[256,512]{1,0:T(8,128)(2,1)}, u32[]{:S(2)}, u32[]{:S(2)}) collective-permute-start(bf16[256,512]{1,0:T(8,128)(2,1)} %shard_map.89.refs_0_), channel_id=1, source_target_pairs={{30,0},{0,2},{2,4},{4,6},{6,8},{8,10},{10,12},{12,14},{14,16},{16,... | collective-permute-start | bytes 786440 | tf_op jit(solution)/shard_map/ppermute | solution.py:291
  56.1 0.8 copy-start.2
  56.9 1.0 copy-start.3
  59.1 0.7 copy-start.25
  59.8 1.0 copy-start.1
  69.6 11.3 %collective-permute-start.12 = (bf16[2,256,512]{2,1,0:T(8,128)(2,1)}, bf16[2,256,512]{2,1,0:T(8,128)(2,1)}, u32[]{:S(2)}, u32[]{:S(2)}) collective-permute-start(bf16[2,256,512]{2,1,0:T(8,128)(2,1)} %get-tuple-element.54), channel_id=1, source_target_pairs={{0,4},{2,6},{4,0},{6,2},{8,12},{10,14},{12,8},{14,10},{16,20},{18,... | collective-permute-start | bytes 1572872 | tf_op jit(solution)/shard_map/ppermute | solution.py:294
  70.6 14.9 %collective-permute-start.11 = (bf16[2,256,512]{2,1,0:T(8,128)(2,1)}, bf16[2,256,512]{2,1,0:T(8,128)(2,1)}, u32[]{:S(2)}, u32[]{:S(2)}) collective-permute-start(bf16[2,256,512]{2,1,0:T(8,128)(2,1)} %get-tuple-element.51), channel_id=1, source_target_pairs={{0,2},{2,0},{4,6},{6,4},{8,10},{10,8},{12,14},{14,12},{16,18},{18,... | collective-permute-start | bytes 1572872 | tf_op jit(solution)/shard_map/ppermute | solution.py:294
  73.7 11.8 %copy-start.4 = (f32[2,256,512]{2,1,0:T(8,128)S(1)}, f32[2,256,512]{2,1,0:T(8,128)}, u32[]{:S(2)}) copy-start(f32[2,256,512]{2,1,0:T(8,128)} %get-tuple-element.50.refs_0_) | copy-start | bytes 3145732
  73.7 46.3 %all-to-all-start.2 = ((bf16[16,32,512]{2,1,0:T(8,128)(2,1)}), bf16[16,32,512]{2,1,0:T(8,128)(2,1)S(1)}, u32[]{:S(2)}, u32[]{:S(2)}) async-start(bf16[16,32,512]{2,1,0:T(8,128)(2,1)} %bitcast.23), calls=%async_computation.2 | async-start | bytes 1048576 | tf_op jit(solution)/shard_map/all_to_all | solution.py:297
  80.9 1.2 copy-start.5
  82.1 7.3 %copy-start.10 = (bf16[1024,256]{1,0:T(8,128)(2,1)S(1)}, bf16[1024,256]{1,0:T(8,128)(2,1)}, u32[]{:S(2)}) copy-start(bf16[1024,256]{1,0:T(8,128)(2,1)} %get-tuple-element.47.weight_ref) | copy-start | bytes 1572868
  84.0 6.6 %copy-start.9 = (bf16[1024,256]{1,0:T(8,128)(2,1)S(1)}, bf16[1024,256]{1,0:T(8,128)(2,1)}, u32[]{:S(2)}) copy-start(bf16[1024,256]{1,0:T(8,128)(2,1)} %get-tuple-element.43.weight_ref) | copy-start | bytes 1572868
  84.0 17.5 %collective-permute-start.14 = (bf16[2,128,512]{2,1,0:T(8,128)(2,1)}, bf16[2,128,512]{2,1,0:T(8,128)(2,1)S(1)}, u32[]{:S(2)}, u32[]{:S(2)}) collective-permute-start(bf16[2,128,512]{2,1,0:T(8,128)(2,1)} %get-tuple-element.57), channel_id=1, source_target_pairs={{0,2},{2,0},{4,6},{6,4},{8,10},{10,8},{12,14},{14,12},{16,18},{18,... | collective-permute-start | bytes 786440 | tf_op jit(solution)/shard_map/ppermute | solution.py:294
  87.3 4.4 %copy-start.8 = (bf16[1024,256]{1,0:T(8,128)(2,1)S(1)}, bf16[1024,256]{1,0:T(8,128)(2,1)}, u32[]{:S(2)}) copy-start(bf16[1024,256]{1,0:T(8,128)(2,1)} %get-tuple-element.44.weight_ref) | copy-start | bytes 1572868
  87.3 23.2 %collective-permute-start.13 = (bf16[2,128,512]{2,1,0:T(8,128)(2,1)}, bf16[2,128,512]{2,1,0:T(8,128)(2,1)S(1)}, u32[]{:S(2)}, u32[]{:S(2)}) collective-permute-start(bf16[2,128,512]{2,1,0:T(8,128)(2,1)} %get-tuple-element.56), channel_id=1, source_target_pairs={{0,4},{2,6},{4,0},{6,2},{8,12},{10,14},{12,8},{14,10},{16,20},{18,... | collective-permute-start | bytes 786440 | tf_op jit(solution)/shard_map/ppermute | solution.py:294
  90.6 2.4 %copy-start.7 = (bf16[1024,256]{1,0:T(8,128)(2,1)S(1)}, bf16[1024,256]{1,0:T(8,128)(2,1)}, u32[]{:S(2)}) copy-start(bf16[1024,256]{1,0:T(8,128)(2,1)} %get-tuple-element.45.weight_ref) | copy-start | bytes 1572868
  90.6 25.1 %collective-permute-start.9 = (bf16[256,512]{1,0:T(8,128)(2,1)}, bf16[256,512]{1,0:T(8,128)(2,1)S(1)}, u32[]{:S(2)}, u32[]{:S(2)}) collective-permute-start(bf16[256,512]{1,0:T(8,128)(2,1)} %shard_map.97), channel_id=1, source_target_pairs={{28,0},{30,2},{0,4},{2,6},{4,8},{6,10},{8,12},{10,14},{12,16},{14,... | collective-permute-start | bytes 786440 | tf_op jit(solution)/shard_map/ppermute | solution.py:291
  91.8 2.4 %copy-start.6 = (bf16[1024,256]{1,0:T(8,128)(2,1)S(1)}, bf16[1024,256]{1,0:T(8,128)(2,1)}, u32[]{:S(2)}) copy-start(bf16[1024,256]{1,0:T(8,128)(2,1)} %get-tuple-element.46.weight_ref) | copy-start | bytes 1572868
  92.9 8.6 %copy-start.24 = (bf16[256,512]{1,0:T(8,128)(2,1)S(1)}, bf16[256,512]{1,0:T(8,128)(2,1)}, u32[]{:S(2)}) copy-start(bf16[256,512]{1,0:T(8,128)(2,1)} %shard_map.94) | copy-start | bytes 786436
  92.9 17.6 %copy-start.22 = (bf16[256,512]{1,0:T(8,128)(2,1)S(1)}, bf16[256,512]{1,0:T(8,128)(2,1)}, u32[]{:S(2)}) copy-start(bf16[256,512]{1,0:T(8,128)(2,1)} %shard_map.93) | copy-start | bytes 786436
  94.1 23.2 %copy-start.11 = (f32[4,256,1]{2,1,0:T(8,128)S(1)}, f32[4,256,1]{2,1,0:T(8,128)}, u32[]{:S(2)}) copy-start(f32[4,256,1]{2,1,0:T(8,128)} %get-tuple-element.36.pw_ref) | copy-start | bytes 12292
  94.1 23.2 %copy-start.12 = (bf16[1024,256]{1,0:T(8,128)(2,1)S(1)}, bf16[1024,256]{1,0:T(8,128)(2,1)}, u32[]{:S(2)}) copy-start(bf16[1024,256]{1,0:T(8,128)(2,1)} %get-tuple-element.37.weight_ref) | copy-start | bytes 1572868
  95.3 25.8 %copy-start.16 = (s32[1,256]{1,0:T(1,128)S(1)}, s32[1,256]{1,0:T(1,128)}, u32[]{:S(2)}) copy-start(s32[1,256]{1,0:T(1,128)} %neg_ref.1) | copy-start | bytes 3076
  95.3 24.7 %collective-permute-start.8 = (bf16[256,512]{1,0:T(8,128)(2,1)}, bf16[256,512]{1,0:T(8,128)(2,1)S(1)}, u32[]{:S(2)}, u32[]{:S(2)}) collective-permute-start(bf16[256,512]{1,0:T(8,128)(2,1)} %shard_map.96), channel_id=1, source_target_pairs={{30,0},{0,2},{2,4},{4,6},{6,8},{8,10},{10,12},{12,14},{14,16},{16,... | collective-permute-start | bytes 786440 | tf_op jit(solution)/shard_map/ppermute | solution.py:291
  95.7 24.2 %collective-permute-start.7 = (bf16[256,512]{1,0:T(8,128)(2,1)}, bf16[256,512]{1,0:T(8,128)(2,1)S(1)}, u32[]{:S(2)}, u32[]{:S(2)}) collective-permute-start(bf16[256,512]{1,0:T(8,128)(2,1)} %shard_map.95), channel_id=1, source_target_pairs={{6,0},{8,2},{10,4},{12,6},{14,8},{16,10},{18,12},{20,14},{22,16},{... | collective-permute-start | bytes 786440 | tf_op jit(solution)/shard_map/ppermute | solution.py:291
  101.5 18.5 %collective-permute-start.6 = (bf16[256,512]{1,0:T(8,128)(2,1)S(1)}, bf16[256,512]{1,0:T(8,128)(2,1)S(1)}, u32[]{:S(2)}, u32[]{:S(2)}) collective-permute-start(bf16[256,512]{1,0:T(8,128)(2,1)S(1)} %copy-done.24), channel_id=1, source_target_pairs={{4,0},{6,2},{8,4},{10,6},{12,8},{14,10},{16,12},{18,14},{20,16},{2... | collective-permute-start | bytes 786440 | tf_op jit(solution)/shard_map/ppermute | solution.py:291
  110.5 9.5 %collective-permute-start.5 = (bf16[256,512]{1,0:T(8,128)(2,1)S(1)}, bf16[256,512]{1,0:T(8,128)(2,1)}, u32[]{:S(2)}, u32[]{:S(2)}) collective-permute-start(bf16[256,512]{1,0:T(8,128)(2,1)S(1)} %copy-done.22), channel_id=1, source_target_pairs={{2,0},{4,2},{6,4},{8,6},{10,8},{12,10},{14,12},{16,14},{18,16},{20... | collective-permute-start | bytes 786440 | tf_op jit(solution)/shard_map/ppermute | solution.py:291
  115.7 4.3 %copy-start.19 = (bf16[256,512]{1,0:T(8,128)(2,1)}, bf16[256,512]{1,0:T(8,128)(2,1)S(1)}, u32[]{:S(2)}) copy-start(bf16[256,512]{1,0:T(8,128)(2,1)S(1)} %collective-permute-done.9.refs_5_) | copy-start | bytes 786436
  115.7 8.5 %collective-permute-start.15 = (bf16[4,64,512]{2,1,0:T(8,128)(2,1)}, bf16[4,64,512]{2,1,0:T(8,128)(2,1)S(1)}, u32[]{:S(2)}, u32[]{:S(2)}) collective-permute-start(bf16[4,64,512]{2,1,0:T(8,128)(2,1)} %get-tuple-element.59), channel_id=1, source_target_pairs={{0,8},{2,10},{4,12},{6,14},{8,0},{10,2},{12,4},{14,6},{16,24},{18,... | collective-permute-start | bytes 786440 | tf_op jit(solution)/shard_map/ppermute | solution.py:294
  120.0 0.7 copy-start.20
  120.0 0.8 copy-start.21
  120.0 0.8 copy-start.23
  120.1 1.0 copy-start.18
  123.7 11.3 %collective-permute-start.10 = (bf16[512,256]{1,0:T(8,128)(2,1)S(1)}, bf16[512,256]{1,0:T(8,128)(2,1)S(1)}, u32[]{:S(2)}, u32[]{:S(2)}) collective-permute-start(bf16[512,256]{1,0:T(8,128)(2,1)S(1)} %get-tuple-element.49), channel_id=1, source_target_pairs={{0,1},{1,0},{2,3},{3,2},{4,5},{5,4},{6,7},{7,6},{8,9},{9,8},{10,11... | collective-permute-start | bytes 786440 | tf_op jit(solution)/shard_map/ppermute | solution.py:389
  125.0 9.3 %collective-permute-start.16 = (bf16[4,32,512]{2,1,0:T(8,128)(2,1)}, bf16[4,32,512]{2,1,0:T(8,128)(2,1)S(1)}, u32[]{:S(2)}, u32[]{:S(2)}) collective-permute-start(bf16[4,32,512]{2,1,0:T(8,128)(2,1)} %get-tuple-element.61), channel_id=1, source_target_pairs={{0,16},{2,18},{4,20},{6,22},{8,24},{10,26},{12,28},{14,30},{16,0},... | collective-permute-start | bytes 393224 | tf_op jit(solution)/shard_map/ppermute | solution.py:294

commit v7 on v6

--- a/solution.py
+++ b/solution.py
@@ -208,29 +208,30 @@
             keep[k] = dot(side[...].astype(BF), pair_ref[outer * keep.shape[0] + k])
 
 
-def tail_kernel(tail_ref, q_ref, pw_ref, weight_ref, wanted_ref, out_ref, term, row_ref):
+def tail_kernel(tail_ref, q_ref, pw_ref, weight_ref, wanted_ref, neg_ref, returned_ref, out_ref):
     ents, heads = out_ref.shape[0], tail_ref.shape[1]
     total = jnp.zeros(out_ref.shape, F32)
     for j in range(tail_ref.shape[0]):
         spot = hot(tail_ref[j : j + 1, :], (ents, heads), 0)
         top, rest = halves(pw_ref[j] * q_ref[j * heads : (j + 1) * heads, :].astype(F32))
         total = total + dot(spot, top) + dot(spot, rest)
-    out_ref[...] = total
-    term[...] = t_dot(weight_ref[...], q_ref[...])
-    row_ref[...] = as_row(wanted_column(wanted_ref))
-
-
-def sum_kernel(reps, me_ref, wanted_ref, neg_ref, returned_ref, base_ref, *refs):
-    terms = refs[:STOPS]
-    own_ref, outs = refs[STOPS], refs[STOPS + 1 :]
+    spot = hot(neg_ref[...], (ents, neg_ref.shape[1]), 0)
+    top, rest = halves(t_dot(weight_ref[...], q_ref[...]))
+    total = total + dot(spot, top) + dot(spot, rest)
+    row = as_row(wanted_column(wanted_ref))
+    out_ref[...] = total + dot(hot(row, (ents, row.shape[1]), 0), returned_ref[...])
+
+
+def sum_kernel(reps, me_ref, neg_ref, base_ref, *refs):
+    terms = refs[: STOPS - 1]
+    own_ref, outs = refs[STOPS - 1], refs[STOPS:]
     ents = base_ref.shape[0]
-    total = terms[0][...]
+    total = terms[0][...].astype(F32)
     for term in terms[1:]:
         total = total + term[...].astype(F32)
     top, rest = halves(total)
     spot = hot(neg_ref[...], (ents, neg_ref.shape[1]), 0)
-    back = hot(wanted_ref[...], (ents, wanted_ref.shape[1]), 0)
-    full = base_ref[...] + dot(back, returned_ref[...]) + dot(spot, top) + dot(spot, rest)
+    full = base_ref[...] + dot(spot, top) + dot(spot, rest)
     chunk = own_ref.shape[1]
     rep = me_ref[1]
     parts = [full[:, c * chunk : (c + 1) * chunk] for c in range(reps)]
@@ -355,10 +356,9 @@
     for n, offset in enumerate(OFFSETS):
         (term,) = kernel(term_kernel, [((rows, width), BF, HM)])(queries, weights[n + 1])
         back.append(moved(term, -offset))
-    base, own_term, wanted_row = kernel(
-        tail_kernel, [((ents, width), F32, HM), ((rows, width), F32, HM), ((1, slots), jnp.int32)]
-    )(tail, queries, pos_weight, weights[0], wanted)
-    back = [own_term] + back
+    (base,) = kernel(tail_kernel, [((ents, width), F32, HM)])(
+        tail, queries, pos_weight, weights[0], wanted, neg_row, returned,
+    )
 
     def fold(keeps, gots):
         count, size = len(keeps) * keeps[0].shape[0], keeps[0].shape[1]
@@ -382,11 +382,12 @@
         functools.partial(sum_kernel, reps),
         [((ents, chunk), F32)] + [((ents, chunk), BF)] * (reps - 1),
         smem=1,
-    )(me, wanted_row, neg_row, *[far(value) for value in (returned, base, *back)])
+    )(me, neg_row, *[far(value) for value in (base, *back)])
     grad_entity = own
     for shift, other in enumerate(others):
         route = [(i, (i + shift + 1) % reps) for i in range(reps)]
-        grad_entity = grad_entity + lax.ppermute(other, "rep", route).astype(F32)
+        got = lax.ppermute(other, "rep", route)
+        grad_entity = grad_entity + got.astype(F32)
     return (grad_entity, grad_rel)
 
 

time: 137 us -> 137 us (level)
    unnamed x52 -> x40, local copies, waits for them, and re-layouts: 5.81 us -> 5.52 us
  transfers between devices with their start and end apart: 19 -> 19, of which waited for: 6 -> 6; matrix products, arithmetic and copies ran while one was open for 0% -> 0% of each run, Pallas kernels for 17% -> 18%
where the time goes in v7:
time: 137 us; the launch traced here: 136 us
  waiting for transfers between devices  45.9 us (34%)
  Pallas kernels  36.6 us (27%)
  starting transfers between devices  29.8 us (22%)
  blocking collectives  15.7 us (11%)
  local copies, waits for them, and re-layouts  5.52 us (4%)
  other arithmetic  1.46 us (1%)
    pallas_call x18, Pallas kernels, call(): pl.pallas_call(body, out_shape=[o[2](*o[:2]) if len(o) > 2 else jax.Shape...  36.6 us
    all_to_all x2, waiting for transfers between devices, dealt(): lax.all_to_all(value, 'blk', split_axis=0, concat_axis=0, tiled=True, axi...  21.7 us
    ppermute x6, waiting for transfers between devices, flipped(): return lax.ppermute(value, 'blk', [(i, i ^ bit) for i in range(shards)])  19.7 us
    all_to_all x1, blocking collectives, dealt(): lax.all_to_all(value, 'blk', split_axis=0, concat_axis=0, tiled=True, axi...  15.7 us
    ppermute x10, starting transfers between devices, moved(): lax.ppermute(value, 'blk', [((i - distance) % shards, i) for i in range(s...  14.6 us
    all_to_all x2, starting transfers between devices, dealt(): lax.all_to_all(value, 'blk', split_axis=0, concat_axis=0, tiled=True, axi...  8.32 us
    ppermute x6, starting transfers between devices, flipped(): return lax.ppermute(value, 'blk', [(i, i ^ bit) for i in range(shards)])  6.75 us
    unnamed x40, local copies, waits for them, and re-layouts  5.52 us
  transfers between devices with their start and end apart: 19, of which 6 were waited for; matrix products, arithmetic and copies ran while one was open for 0% of the time, Pallas kernels for 18%

profile of v7, /device:TPU:0, one launch (start us, length us, event | category | flops | bytes accessed | tf_op | source)
XLA Modules:
  0.0 135.8 jit_solution(17496249916273662107)
XLA Ops:
  0.7 0.6 pad_add_fusion.me_ref
  1.3 1.7 %shard_map.86 = (s32[16,32]{1,0:T(8,128)}, s32[1,256]{1,0:T(1,128)}) custom-call(s32[2]{0:T(128)} %pad_add_fusion.me_ref, s32[1,256]{1,0:T(1,128)} %bitcast.25, s32[1,256]{1,0:T(1,128)} %bitcast.26), custom_call_target="tpu_custom_call" | custom-call | tf_op jit(solution)/shard_map/pallas_call | solution.py:259
  3.0 15.7 %all_to_all.21 = s32[16,1,32]{2,1,0:T(1,128)S(1)} all-to-all(s32[16,1,32]{2,1,0:T(1,128)} %bitcast.24), channel_id=1, replica_groups=mesh['blk'=16,'rep'=2] {'blk'}, dimensions={0} | all-to-all | bytes 4096 | tf_op jit(solution)/shard_map/all_to_all | solution.py:298
  18.7 2.3 %shard_map.87 = bf16[512,512]{1,0:T(8,128)(2,1)} custom-call(s32[16,32]{1,0:T(8,128)S(1)} %bitcast.16, bf16[512,512]{1,0:T(8,128)(2,1)} %ent_ref.1), custom_call_target="tpu_custom_call" | custom-call | tf_op jit(solution)/shard_map/pallas_call | solution.py:259
  21.0 0.0 copy-start.14
  21.1 3.6 %all-to-all-start.1 = ((bf16[16,32,512]{2,1,0:T(8,128)(2,1)}), bf16[16,32,512]{2,1,0:T(8,128)(2,1)S(1)}, u32[]{:S(2)}, u32[]{:S(2)}) async-start(bf16[16,32,512]{2,1,0:T(8,128)(2,1)} %bitcast.22), calls=%async_computation.1 | async-start | bytes 1048576 | tf_op jit(solution)/shard_map/all_to_all | solution.py:298
  24.7 2.1 %shard_map.89.refs_0_ = bf16[256,512]{1,0:T(8,128)(2,1)} custom-call(s32[1,256]{1,0:T(1,128)} %neg_ref.3, bf16[512,512]{1,0:T(8,128)(2,1)} %ent_ref.1), custom_call_target="tpu_custom_call" | custom-call | tf_op jit(solution)/shard_map/pallas_call | solution.py:259
  26.8 4.6 %collective-permute-start.4 = (bf16[256,512]{1,0:T(8,128)(2,1)}, bf16[256,512]{1,0:T(8,128)(2,1)S(1)}, u32[]{:S(2)}, u32[]{:S(2)}) collective-permute-start(bf16[256,512]{1,0:T(8,128)(2,1)} %shard_map.89.refs_0_), channel_id=1, source_target_pairs={{4,0},{6,2},{8,4},{10,6},{12,8},{14,10},{16,12},{18,14},{20,16},{2... | collective-permute-start | bytes 786440 | tf_op jit(solution)/shard_map/ppermute | solution.py:292
  31.4 1.5 %collective-permute-start.3 = (bf16[256,512]{1,0:T(8,128)(2,1)}, bf16[256,512]{1,0:T(8,128)(2,1)}, u32[]{:S(2)}, u32[]{:S(2)}) collective-permute-start(bf16[256,512]{1,0:T(8,128)(2,1)} %shard_map.89.refs_0_), channel_id=1, source_target_pairs={{2,0},{4,2},{6,4},{8,6},{10,8},{12,10},{14,12},{16,14},{18,16},{20... | collective-permute-start | bytes 786440 | tf_op jit(solution)/shard_map/ppermute | solution.py:292
  32.8 0.0 collective-permute-start.2
  32.8 1.5 %collective-permute-start.1 = (bf16[256,512]{1,0:T(8,128)(2,1)}, bf16[256,512]{1,0:T(8,128)(2,1)}, u32[]{:S(2)}, u32[]{:S(2)}) collective-permute-start(bf16[256,512]{1,0:T(8,128)(2,1)} %shard_map.89.refs_0_), channel_id=1, source_target_pairs={{28,0},{30,2},{0,4},{2,6},{4,8},{6,10},{8,12},{10,14},{12,16},{14,... | collective-permute-start | bytes 786440 | tf_op jit(solution)/shard_map/ppermute | solution.py:292
  34.3 0.1 collective-permute-start
  34.4 21.7 %all-to-all-done.1 = bf16[16,32,512]{2,1,0:T(8,128)(2,1)S(1)} async-done(((bf16[16,32,512]{2,1,0:T(8,128)(2,1)}), bf16[16,32,512]{2,1,0:T(8,128)(2,1)S(1)}, u32[]{:S(2)}, u32[]{:S(2)}) %all-to-all-start.1) | async-done | bytes 524320 | tf_op jit(solution)/shard_map/all_to_all | solution.py:298
  56.1 0.8 copy-done.2
  56.9 1.0 copy-done.3
  58.0 1.2 shard_map.88
  59.2 0.0 collective-permute-done.4.refs_5_
  59.2 0.0 collective-permute-done.3.refs_4_
  59.2 0.0 collective-permute-done.2.refs_3_
  59.2 0.0 collective-permute-done.1.refs_2_
  59.2 0.0 collective-permute-done.refs_1_
  59.2 0.7 copy-done.19
  59.9 1.0 copy-done.1
  60.9 8.8 %shard_map.90 = (f32[4,256,1]{2,1,0:T(8,128)}, bf16[4,256,512]{2,1,0:T(8,128)(2,1)S(1)}, bf16[2,256,512]{2,1,0:T(8,128)(2,1)}, bf16[2,256,512]{2,1,0:T(8,128)(2,...) custom-call(s32[2]{0:T(128)S(1)} %copy-done.16, ...), custom_call_target="tpu_custom_call" | custom-call | tf_op jit(solution)/shard_map/pallas_call | solution.py:259
  69.7 1.0 collective-permute-start.12
  70.7 0.0 collective-permute-start.11
  70.7 3.1 %shard_map.91 = (bf16[512,512]{1,0:T(8,128)(2,1)}, f32[2,256,512]{2,1,0:T(8,128)}, f32[2,256,512]{2,1,0:T(8,128)}) custom-call(s32[2]{0:T(128)S(1)} %copy-done.16, s32[1,256]{1,0:T(1,128)S(1)} %copy-done.17, bf16[4,256,512]{2,1,0:T(8,128)(2,1)S(1)} %get-tuple-element.35.pair_ref, bf16[4,512,512]{2,1,0:T(8,128)(2,1)S(1)} %copy-done, ...), custom_call_target="tpu_custom_call" | custom-call | tf_op jit(solution)/shard_map/pallas_call | solution.py:259
  73.8 4.7 %all-to-all-start.2 = ((bf16[16,32,512]{2,1,0:T(8,128)(2,1)}), bf16[16,32,512]{2,1,0:T(8,128)(2,1)S(1)}, u32[]{:S(2)}, u32[]{:S(2)}) async-start(bf16[16,32,512]{2,1,0:T(8,128)(2,1)} %bitcast.23), calls=%async_computation.2 | async-start | bytes 1048576 | tf_op jit(solution)/shard_map/all_to_all | solution.py:298
  78.5 2.5 %collective-permute-done.12.refs_1_ = bf16[2,256,512]{2,1,0:T(8,128)(2,1)} collective-permute-done((bf16[2,256,512]{2,1,0:T(8,128)(2,1)}, bf16[2,256,512]{2,1,0:T(8,128)(2,1)}, u32[]{:S(2)}, u32[]{:S(2)}) %collective-permute-start.12) | collective-permute-done | bytes 524320 | tf_op jit(solution)/shard_map/ppermute | solution.py:295
  81.0 1.2 copy-done.5
  82.2 1.9 %shard_map.100 = (f32[2,128,512]{2,1,0:T(8,128)S(1)}, bf16[2,128,512]{2,1,0:T(8,128)(2,1)}) custom-call(f32[2,256,512]{2,1,0:T(8,128)S(1)} %copy-done.5, bf16[2,256,512]{2,1,0:T(8,128)(2,1)} %collective-permute-done.12.refs_1_), custom_call_target="tpu_custom_call" | custom-call | tf_op jit(solution)/shard_map/pallas_call | solution.py:259
  84.1 1.5 %collective-permute-start.14 = (bf16[2,128,512]{2,1,0:T(8,128)(2,1)}, bf16[2,128,512]{2,1,0:T(8,128)(2,1)S(1)}, u32[]{:S(2)}, u32[]{:S(2)}) collective-permute-start(bf16[2,128,512]{2,1,0:T(8,128)(2,1)} %get-tuple-element.51), channel_id=1, source_target_pairs={{0,2},{2,0},{4,6},{6,4},{8,10},{10,8},{12,14},{14,12},{16,18},{18,... | collective-permute-start | bytes 786440 | tf_op jit(solution)/shard_map/ppermute | solution.py:295
  85.6 0.0 collective-permute-done.11.refs_1_
  85.6 1.8 %shard_map.99 = (f32[2,128,512]{2,1,0:T(8,128)S(1)}, bf16[2,128,512]{2,1,0:T(8,128)(2,1)}) custom-call(f32[2,256,512]{2,1,0:T(8,128)S(1)} %copy-done.4, bf16[2,256,512]{2,1,0:T(8,128)(2,1)} %collective-permute-done.11.refs_1_), custom_call_target="tpu_custom_call" | custom-call | tf_op jit(solution)/shard_map/pallas_call | solution.py:259
  87.4 2.1 %collective-permute-start.13 = (bf16[2,128,512]{2,1,0:T(8,128)(2,1)}, bf16[2,128,512]{2,1,0:T(8,128)(2,1)S(1)}, u32[]{:S(2)}, u32[]{:S(2)}) collective-permute-start(bf16[2,128,512]{2,1,0:T(8,128)(2,1)} %get-tuple-element.50), channel_id=1, source_target_pairs={{0,4},{2,6},{4,0},{6,2},{8,12},{10,14},{12,8},{14,10},{16,20},{18,... | collective-permute-start | bytes 786440 | tf_op jit(solution)/shard_map/ppermute | solution.py:295
  89.5 1.2 shard_map.97
  90.7 0.0 collective-permute-start.9
  90.7 1.2 shard_map.93
  91.9 1.2 shard_map.94
  93.0 1.2 shard_map.95
  94.2 1.2 shard_map.96
  95.4 0.5 collective-permute-start.8
  95.9 5.7 %collective-permute-start.7 = (bf16[256,512]{1,0:T(8,128)(2,1)}, bf16[256,512]{1,0:T(8,128)(2,1)}, u32[]{:S(2)}, u32[]{:S(2)}) collective-permute-start(bf16[256,512]{1,0:T(8,128)(2,1)} %shard_map.95), channel_id=1, source_target_pairs={{6,0},{8,2},{10,4},{12,6},{14,8},{16,10},{18,12},{20,14},{22,16},{... | collective-permute-start | bytes 786440 | tf_op jit(solution)/shard_map/ppermute | solution.py:292
  101.6 0.0 collective-permute-done.14.refs_3_
  101.6 0.8 collective-permute-start.6
  102.4 8.1 %collective-permute-done.13.refs_2_ = bf16[2,128,512]{2,1,0:T(8,128)(2,1)S(1)} collective-permute-done((bf16[2,128,512]{2,1,0:T(8,128)(2,1)}, bf16[2,128,512]{2,1,0:T(8,128)(2,1)S(1)}, u32[]{:S(2)}, u32[]{:S(2)}) %collective-permute-start.13) | collective-permute-done | bytes 262176 | tf_op jit(solution)/shard_map/ppermute | solution.py:295
  110.5 0.0 collective-permute-start.5
  110.5 0.8 shard_map.101
  111.3 4.5 %collective-permute-done.9.refs_4_ = bf16[256,512]{1,0:T(8,128)(2,1)S(1)} collective-permute-done((bf16[256,512]{1,0:T(8,128)(2,1)}, bf16[256,512]{1,0:T(8,128)(2,1)S(1)}, u32[]{:S(2)}, u32[]{:S(2)}) %collective-permute-start.9) | collective-permute-done | bytes 262176 | tf_op jit(solution)/shard_map/ppermute | solution.py:292
  115.8 0.7 copy-done.18
  116.5 1.6 %collective-permute-start.15 = (bf16[4,64,512]{2,1,0:T(8,128)(2,1)}, bf16[4,64,512]{2,1,0:T(8,128)(2,1)S(1)}, u32[]{:S(2)}, u32[]{:S(2)}) collective-permute-start(bf16[4,64,512]{2,1,0:T(8,128)(2,1)} %get-tuple-element.53), channel_id=1, source_target_pairs={{0,8},{2,10},{4,12},{6,14},{8,0},{10,2},{12,4},{14,6},{16,24},{18,... | collective-permute-start | bytes 786440 | tf_op jit(solution)/shard_map/ppermute | solution.py:295
  118.1 3.4 %shard_map.92.base_ref = f32[512,512]{1,0:T(8,128)} custom-call(s32[4,256]{1,0:T(4,128)S(1)} %bitcast.21, bf16[1024,512]{1,0:T(8,128)(2,1)S(1)} %get-tuple-element.31.q_ref, f32[4,256,1]{2,1,0:T(8,128)S(1)} %copy-done.6, bf16[1024,256]{1,0:T(8,128)(2,1)S(1)} %copy-done.7, s32[16,32]{1,0:T(8,128)S(1)} %bitcast.17, s32[1,256]{1,0:T(1,128)S(1)} %copy-done.15, ...), custom_call_target="tpu_custom_call" | custom-call | tf_op jit(solution)/shard_map/pallas_call | solution.py:259
  121.6 0.0 collective-permute-done.8.refs_3_
  121.6 0.0 collective-permute-done.7.refs_2_
  121.6 0.0 collective-permute-done.6.refs_1_
  121.6 2.2 %shard_map.98 = (f32[512,256]{1,0:T(8,128)S(1)}, bf16[512,256]{1,0:T(8,128)(2,1)S(1)}) custom-call(s32[2]{0:T(128)S(1)} %copy-done.16, s32[1,256]{1,0:T(1,128)S(1)} %copy-done.15, f32[512,512]{1,0:T(8,128)} %shard_map.92.base_ref, bf16[256,512]{1,0:T(8,128)(2,1)} %collective-permute-done.5.refs_0_, bf16[256,512]{1,0:T(8,128)(2,1)} %collective-permute-done.6.refs_1_, ...), custom_call_target="tpu_custom_call" | custom-call | tf_op jit(solution)/shard_map/pallas_call | solution.py:259
  123.8 0.1 collective-permute-start.10
  123.9 0.7 collective-permute-done.15.refs_1_
  124.6 0.7 shard_map.102
  125.2 0.6 collective-permute-start.16
  125.8 8.4 %collective-permute-done.16.refs_1_ = bf16[4,32,512]{2,1,0:T(8,128)(2,1)S(1)} collective-permute-done((bf16[4,32,512]{2,1,0:T(8,128)(2,1)}, bf16[4,32,512]{2,1,0:T(8,128)(2,1)S(1)}, u32[]{:S(2)}, u32[]{:S(2)}) %collective-permute-start.16) | collective-permute-done | bytes 131104 | tf_op jit(solution)/shard_map/ppermute | solution.py:295
  134.2 0.7 shard_map.103
  135.0 0.0 collective-permute-done.10
  135.0 0.8 convert_add_fusion
  (35 shorter events, 0.1 us)
Async XLA Ops:
  0.6 56.3 %copy-start = (bf16[4,512,512]{2,1,0:T(8,128)(2,1)S(1)}, bf16[4,512,512]{2,1,0:T(8,128)(2,1)}, u32[]{:S(2)}) copy-start(bf16[4,512,512]{2,1,0:T(8,128)(2,1)} %rel_ref.3) | copy-start | bytes 6291460
  0.6 56.3 %copy-start.13 = (s32[256,4]{0,1:T(4,128)S(1)}, s32[256,4]{0,1:T(4,128)}, u32[]{:S(2)}) copy-start(s32[256,4]{0,1:T(4,128)} %param.11) | copy-start | bytes 12292
  3.0 53.9 %copy-start.17 = (s32[1,256]{1,0:T(1,128)S(1)}, s32[1,256]{1,0:T(1,128)}, u32[]{:S(2)}) copy-start(s32[1,256]{1,0:T(1,128)} %get-tuple-element.29.pos_ref) | copy-start | bytes 3076
  21.0 38.9 %copy-start.14 = (s32[256,4]{0,1:T(4,128)S(1)}, s32[256,4]{0,1:T(4,128)}, u32[]{:S(2)}) copy-start(s32[256,4]{0,1:T(4,128)} %param.12) | copy-start | bytes 12292
  21.1 38.9 %copy-start.16 = (s32[2]{0:T(128)S(1)}, s32[2]{0:T(128)}, u32[]{:S(2)}) copy-start(s32[2]{0:T(128)} %pad_add_fusion.me_ref) | copy-start | bytes 28
  21.1 35.0 %all-to-all-start.1 = ((bf16[16,32,512]{2,1,0:T(8,128)(2,1)}), bf16[16,32,512]{2,1,0:T(8,128)(2,1)S(1)}, u32[]{:S(2)}, u32[]{:S(2)}) async-start(bf16[16,32,512]{2,1,0:T(8,128)(2,1)} %bitcast.22), calls=%async_computation.1 | async-start | bytes 1048576 | tf_op jit(solution)/shard_map/all_to_all | solution.py:298
  26.8 32.4 %collective-permute-start.4 = (bf16[256,512]{1,0:T(8,128)(2,1)}, bf16[256,512]{1,0:T(8,128)(2,1)S(1)}, u32[]{:S(2)}, u32[]{:S(2)}) collective-permute-start(bf16[256,512]{1,0:T(8,128)(2,1)} %shard_map.89.refs_0_), channel_id=1, source_target_pairs={{4,0},{6,2},{8,4},{10,6},{12,8},{14,10},{16,12},{18,14},{20,16},{2... | collective-permute-start | bytes 786440 | tf_op jit(solution)/shard_map/ppermute | solution.py:292
  31.4 27.8 %collective-permute-start.3 = (bf16[256,512]{1,0:T(8,128)(2,1)}, bf16[256,512]{1,0:T(8,128)(2,1)}, u32[]{:S(2)}, u32[]{:S(2)}) collective-permute-start(bf16[256,512]{1,0:T(8,128)(2,1)} %shard_map.89.refs_0_), channel_id=1, source_target_pairs={{2,0},{4,2},{6,4},{8,6},{10,8},{12,10},{14,12},{16,14},{18,16},{20... | collective-permute-start | bytes 786440 | tf_op jit(solution)/shard_map/ppermute | solution.py:292
  32.8 26.4 %collective-permute-start.2 = (bf16[256,512]{1,0:T(8,128)(2,1)}, bf16[256,512]{1,0:T(8,128)(2,1)}, u32[]{:S(2)}, u32[]{:S(2)}) collective-permute-start(bf16[256,512]{1,0:T(8,128)(2,1)} %shard_map.89.refs_0_), channel_id=1, source_target_pairs={{26,0},{28,2},{30,4},{0,6},{2,8},{4,10},{6,12},{8,14},{10,16},{12,... | collective-permute-start | bytes 786440 | tf_op jit(solution)/shard_map/ppermute | solution.py:292
  32.8 26.4 %collective-permute-start.1 = (bf16[256,512]{1,0:T(8,128)(2,1)}, bf16[256,512]{1,0:T(8,128)(2,1)}, u32[]{:S(2)}, u32[]{:S(2)}) collective-permute-start(bf16[256,512]{1,0:T(8,128)(2,1)} %shard_map.89.refs_0_), channel_id=1, source_target_pairs={{28,0},{30,2},{0,4},{2,6},{4,8},{6,10},{8,12},{10,14},{12,16},{14,... | collective-permute-start | bytes 786440 | tf_op jit(solution)/shard_map/ppermute | solution.py:292
  34.3 24.9 %collective-permute-start = (bf16[256,512]{1,0:T(8,128)(2,1)}, bf16[256,512]{1,0:T(8,128)(2,1)}, u32[]{:S(2)}, u32[]{:S(2)}) collective-permute-start(bf16[256,512]{1,0:T(8,128)(2,1)} %shard_map.89.refs_0_), channel_id=1, source_target_pairs={{30,0},{0,2},{2,4},{4,6},{6,8},{8,10},{10,12},{12,14},{14,16},{16,... | collective-permute-start | bytes 786440 | tf_op jit(solution)/shard_map/ppermute | solution.py:292
  56.1 0.8 copy-start.2
  56.9 1.0 copy-start.3
  59.2 0.7 copy-start.19
  59.9 1.0 copy-start.1
  69.7 11.3 %collective-permute-start.12 = (bf16[2,256,512]{2,1,0:T(8,128)(2,1)}, bf16[2,256,512]{2,1,0:T(8,128)(2,1)}, u32[]{:S(2)}, u32[]{:S(2)}) collective-permute-start(bf16[2,256,512]{2,1,0:T(8,128)(2,1)} %get-tuple-element.48), channel_id=1, source_target_pairs={{0,4},{2,6},{4,0},{6,2},{8,12},{10,14},{12,8},{14,10},{16,20},{18,... | collective-permute-start | bytes 1572872 | tf_op jit(solution)/shard_map/ppermute | solution.py:295
  70.7 14.9 %collective-permute-start.11 = (bf16[2,256,512]{2,1,0:T(8,128)(2,1)}, bf16[2,256,512]{2,1,0:T(8,128)(2,1)}, u32[]{:S(2)}, u32[]{:S(2)}) collective-permute-start(bf16[2,256,512]{2,1,0:T(8,128)(2,1)} %get-tuple-element.45), channel_id=1, source_target_pairs={{0,2},{2,0},{4,6},{6,4},{8,10},{10,8},{12,14},{14,12},{16,18},{18,... | collective-permute-start | bytes 1572872 | tf_op jit(solution)/shard_map/ppermute | solution.py:295
  73.8 11.8 %copy-start.4 = (f32[2,256,512]{2,1,0:T(8,128)S(1)}, f32[2,256,512]{2,1,0:T(8,128)}, u32[]{:S(2)}) copy-start(f32[2,256,512]{2,1,0:T(8,128)} %get-tuple-element.44.refs_0_) | copy-start | bytes 3145732
  73.8 44.4 %all-to-all-start.2 = ((bf16[16,32,512]{2,1,0:T(8,128)(2,1)}), bf16[16,32,512]{2,1,0:T(8,128)(2,1)S(1)}, u32[]{:S(2)}, u32[]{:S(2)}) async-start(bf16[16,32,512]{2,1,0:T(8,128)(2,1)} %bitcast.23), calls=%async_computation.2 | async-start | bytes 1048576 | tf_op jit(solution)/shard_map/all_to_all | solution.py:298
  81.0 1.2 copy-start.5
  82.2 7.3 %copy-start.12 = (bf16[1024,256]{1,0:T(8,128)(2,1)S(1)}, bf16[1024,256]{1,0:T(8,128)(2,1)}, u32[]{:S(2)}) copy-start(bf16[1024,256]{1,0:T(8,128)(2,1)} %get-tuple-element.41.weight_ref) | copy-start | bytes 1572868
  84.1 6.6 %copy-start.11 = (bf16[1024,256]{1,0:T(8,128)(2,1)S(1)}, bf16[1024,256]{1,0:T(8,128)(2,1)}, u32[]{:S(2)}) copy-start(bf16[1024,256]{1,0:T(8,128)(2,1)} %get-tuple-element.37.weight_ref) | copy-start | bytes 1572868
  84.1 17.5 %collective-permute-start.14 = (bf16[2,128,512]{2,1,0:T(8,128)(2,1)}, bf16[2,128,512]{2,1,0:T(8,128)(2,1)S(1)}, u32[]{:S(2)}, u32[]{:S(2)}) collective-permute-start(bf16[2,128,512]{2,1,0:T(8,128)(2,1)} %get-tuple-element.51), channel_id=1, source_target_pairs={{0,2},{2,0},{4,6},{6,4},{8,10},{10,8},{12,14},{14,12},{16,18},{18,... | collective-permute-start | bytes 786440 | tf_op jit(solution)/shard_map/ppermute | solution.py:295
  87.4 4.4 %copy-start.10 = (bf16[1024,256]{1,0:T(8,128)(2,1)S(1)}, bf16[1024,256]{1,0:T(8,128)(2,1)}, u32[]{:S(2)}) copy-start(bf16[1024,256]{1,0:T(8,128)(2,1)} %get-tuple-element.38.weight_ref) | copy-start | bytes 1572868
  87.4 23.1 %collective-permute-start.13 = (bf16[2,128,512]{2,1,0:T(8,128)(2,1)}, bf16[2,128,512]{2,1,0:T(8,128)(2,1)S(1)}, u32[]{:S(2)}, u32[]{:S(2)}) collective-permute-start(bf16[2,128,512]{2,1,0:T(8,128)(2,1)} %get-tuple-element.50), channel_id=1, source_target_pairs={{0,4},{2,6},{4,0},{6,2},{8,12},{10,14},{12,8},{14,10},{16,20},{18,... | collective-permute-start | bytes 786440 | tf_op jit(solution)/shard_map/ppermute | solution.py:295
  90.7 2.4 %copy-start.9 = (bf16[1024,256]{1,0:T(8,128)(2,1)S(1)}, bf16[1024,256]{1,0:T(8,128)(2,1)}, u32[]{:S(2)}) copy-start(bf16[1024,256]{1,0:T(8,128)(2,1)} %get-tuple-element.39.weight_ref) | copy-start | bytes 1572868
  90.7 25.1 %collective-permute-start.9 = (bf16[256,512]{1,0:T(8,128)(2,1)}, bf16[256,512]{1,0:T(8,128)(2,1)S(1)}, u32[]{:S(2)}, u32[]{:S(2)}) collective-permute-start(bf16[256,512]{1,0:T(8,128)(2,1)} %shard_map.97), channel_id=1, source_target_pairs={{28,0},{30,2},{0,4},{2,6},{4,8},{6,10},{8,12},{10,14},{12,16},{14,... | collective-permute-start | bytes 786440 | tf_op jit(solution)/shard_map/ppermute | solution.py:292
  91.8 2.4 %copy-start.8 = (bf16[1024,256]{1,0:T(8,128)(2,1)S(1)}, bf16[1024,256]{1,0:T(8,128)(2,1)}, u32[]{:S(2)}) copy-start(bf16[1024,256]{1,0:T(8,128)(2,1)} %get-tuple-element.40.weight_ref) | copy-start | bytes 1572868
  94.2 23.9 %copy-start.6 = (f32[4,256,1]{2,1,0:T(8,128)S(1)}, f32[4,256,1]{2,1,0:T(8,128)}, u32[]{:S(2)}) copy-start(f32[4,256,1]{2,1,0:T(8,128)} %get-tuple-element.33.pw_ref) | copy-start | bytes 12292
  94.2 23.9 %copy-start.7 = (bf16[1024,256]{1,0:T(8,128)(2,1)S(1)}, bf16[1024,256]{1,0:T(8,128)(2,1)}, u32[]{:S(2)}) copy-start(bf16[1024,256]{1,0:T(8,128)(2,1)} %get-tuple-element.34.weight_ref) | copy-start | bytes 1572868
  94.2 23.9 %copy-start.15 = (s32[1,256]{1,0:T(1,128)S(1)}, s32[1,256]{1,0:T(1,128)}, u32[]{:S(2)}) copy-start(s32[1,256]{1,0:T(1,128)} %neg_ref.3) | copy-start | bytes 3076
  95.4 26.2 %collective-permute-start.8 = (bf16[256,512]{1,0:T(8,128)(2,1)}, bf16[256,512]{1,0:T(8,128)(2,1)}, u32[]{:S(2)}, u32[]{:S(2)}) collective-permute-start(bf16[256,512]{1,0:T(8,128)(2,1)} %shard_map.96), channel_id=1, source_target_pairs={{30,0},{0,2},{2,4},{4,6},{6,8},{8,10},{10,12},{12,14},{14,16},{16,... | collective-permute-start | bytes 786440 | tf_op jit(solution)/shard_map/ppermute | solution.py:292
  95.9 25.7 %collective-permute-start.7 = (bf16[256,512]{1,0:T(8,128)(2,1)}, bf16[256,512]{1,0:T(8,128)(2,1)}, u32[]{:S(2)}, u32[]{:S(2)}) collective-permute-start(bf16[256,512]{1,0:T(8,128)(2,1)} %shard_map.95), channel_id=1, source_target_pairs={{6,0},{8,2},{10,4},{12,6},{14,8},{16,10},{18,12},{20,14},{22,16},{... | collective-permute-start | bytes 786440 | tf_op jit(solution)/shard_map/ppermute | solution.py:292
  101.6 20.0 %collective-permute-start.6 = (bf16[256,512]{1,0:T(8,128)(2,1)}, bf16[256,512]{1,0:T(8,128)(2,1)}, u32[]{:S(2)}, u32[]{:S(2)}) collective-permute-start(bf16[256,512]{1,0:T(8,128)(2,1)} %shard_map.94), channel_id=1, source_target_pairs={{4,0},{6,2},{8,4},{10,6},{12,8},{14,10},{16,12},{18,14},{20,16},{2... | collective-permute-start | bytes 786440 | tf_op jit(solution)/shard_map/ppermute | solution.py:292
  110.5 11.1 %collective-permute-start.5 = (bf16[256,512]{1,0:T(8,128)(2,1)}, bf16[256,512]{1,0:T(8,128)(2,1)}, u32[]{:S(2)}, u32[]{:S(2)}) collective-permute-start(bf16[256,512]{1,0:T(8,128)(2,1)} %shard_map.93), channel_id=1, source_target_pairs={{2,0},{4,2},{6,4},{8,6},{10,8},{12,10},{14,12},{16,14},{18,16},{20... | collective-permute-start | bytes 786440 | tf_op jit(solution)/shard_map/ppermute | solution.py:292
  115.8 0.7 copy-start.18
  116.5 8.0 %collective-permute-start.15 = (bf16[4,64,512]{2,1,0:T(8,128)(2,1)}, bf16[4,64,512]{2,1,0:T(8,128)(2,1)S(1)}, u32[]{:S(2)}, u32[]{:S(2)}) collective-permute-start(bf16[4,64,512]{2,1,0:T(8,128)(2,1)} %get-tuple-element.53), channel_id=1, source_target_pairs={{0,8},{2,10},{4,12},{6,14},{8,0},{10,2},{12,4},{14,6},{16,24},{18,... | collective-permute-start | bytes 786440 | tf_op jit(solution)/shard_map/ppermute | solution.py:295
  123.8 11.2 %collective-permute-start.10 = (bf16[512,256]{1,0:T(8,128)(2,1)S(1)}, bf16[512,256]{1,0:T(8,128)(2,1)S(1)}, u32[]{:S(2)}, u32[]{:S(2)}) collective-permute-start(bf16[512,256]{1,0:T(8,128)(2,1)S(1)} %get-tuple-element.43), channel_id=1, source_target_pairs={{0,1},{1,0},{2,3},{3,2},{4,5},{5,4},{6,7},{7,6},{8,9},{9,8},{10,11... | collective-permute-start | bytes 786440 | tf_op jit(solution)/shard_map/ppermute | solution.py:389
  125.2 9.0 %collective-permute-start.16 = (bf16[4,32,512]{2,1,0:T(8,128)(2,1)}, bf16[4,32,512]{2,1,0:T(8,128)(2,1)S(1)}, u32[]{:S(2)}, u32[]{:S(2)}) collective-permute-start(bf16[4,32,512]{2,1,0:T(8,128)(2,1)} %get-tuple-element.55), channel_id=1, source_target_pairs={{0,16},{2,18},{4,20},{6,22},{8,24},{10,26},{12,28},{14,30},{16,0},... | collective-permute-start | bytes 393224 | tf_op jit(solution)/shard_map/ppermute | solution.py:295
